TPU v7x, 128 devices: a whole 4x4x4 slice. The times are simulated.
128 devices in a mesh: dp: 16 (over x, z_lo, core), tensor: 8 (over z_hi, y).
Axes of the slice: x: 4, y: 4, z: 4 (z_hi: 2, z_lo: 2; z = z_hi * 2 + z_lo), core: 2. Of those that a mesh axis runs over, the one named last changes fastest.
Arguments:
- tokens: bfloat16 [8192, 2048], P('dp'), may hold values from -6 to 6
- first_gain: float32 [2048], replicated, may hold values from 0.5 to 1.5
- first_shift: float32 [2048], replicated, may hold values from -1.75 to 1.75
- query_weight: float32 [2048, 2048], P('dp', 'tensor'), may hold values from -0.125 to 0.125
- query_bias: float32 [2048], P('tensor'), may hold values from -3 to 3
- key_weight: float32 [2048, 2048], P('dp', 'tensor'), may hold values from -0.125 to 0.125
- value_weight: float32 [2048, 2048], P('dp', 'tensor'), may hold values from -0.125 to 0.125
- value_bias: float32 [2048], P('tensor'), may hold values from -3 to 3
- out_weight: float32 [2048, 2048], P('tensor', 'dp'), may hold values from -0.5 to 0.5
- out_bias: float32 [2048], replicated, may hold values from -1.75 to 1.75
- second_gain: float32 [2048], replicated, may hold values from 0.5 to 1.5
- second_shift: float32 [2048], replicated, may hold values from -1.75 to 1.75
- up_weight: float32 [2048, 8192], P('dp', 'tensor'), may hold values from -0.125 to 0.125
- up_bias: float32 [8192], P('tensor'), may hold values from -3 to 3
- down_weight: float32 [8192, 2048], P('tensor', 'dp'), may hold values from -0.0625 to 0.0625
- down_bias: float32 [2048], replicated, may hold values from -1.75 to 1.75
- cotangent: bfloat16 [8192, 2048], P('dp'), may hold values from -6 to 6
- prefix: int32 [1], replicated, may hold values from 819 to 4096
- block_order: int32 [32], replicated, may hold values from 0 to 31, as said below
Outputs:
- layer_out: bfloat16 [8192, 2048], P('dp')
- tokens_grad: float32 [8192, 2048], P('dp')
- first_gain_grad: float32 [2048], replicated
- first_shift_grad: float32 [2048], replicated
- query_weight_grad: float32 [2048, 2048], P('dp', 'tensor')
- query_bias_grad: float32 [2048], P('tensor')
- key_weight_grad: float32 [2048, 2048], P('dp', 'tensor')
- value_weight_grad: float32 [2048, 2048], P('dp', 'tensor')
- value_bias_grad: float32 [2048], P('tensor')
- out_weight_grad: float32 [2048, 2048], P('tensor', 'dp')
- out_bias_grad: float32 [2048], replicated
- second_gain_grad: float32 [2048], replicated
- second_shift_grad: float32 [2048], replicated
- up_weight_grad: float32 [2048, 8192], P('dp', 'tensor')
- up_bias_grad: float32 [8192], P('tensor')
- down_weight_grad: float32 [8192, 2048], P('tensor', 'dp')
- down_bias_grad: float32 [2048], replicated
Inputs may be any that keep to these rules, and one draw needn't show every extreme that they name: `block_order`: for each sequence s, entries s * 32 to s * 32 + 31 are a permutation of those same numbers: every stored block lies in its own sequence's rows, but its place within the sequence is shuffled.
All inputs are finite; a program needn't handle non-finite values.
Results may differ from a plain program's by a relative error of at most 0.025.
Values may be sent and summed in bfloat16 or wider, within the bound.
A program may use at most 192 MiB of HBM per device.

v0:
```python
import math

import jax
import jax.numpy as jnp
from jax import lax
from jax.sharding import PartitionSpec as P

HEAD = 128


epsilon = 1e-05
masked_score = -1e30


def sent_together(arrays, axis, dim, along):
    both = jnp.concatenate(arrays, axis=along)
    filled, at, gathered = (lax.all_gather(both, axis, axis=dim, tiled=True), 0, [])
    for a in arrays:
        gathered.append(lax.slice_in_dim(filled, at, at + a.shape[along], axis=along))
        at += a.shape[along]
    return tuple(gathered)


def in_one_piece(arrays, axis, dim, along):
    ends, at = ([], 0)
    for a in arrays[:-1]:
        at += a.shape[along]
        ends.append(at)
    both = jnp.concatenate(arrays, axis=along)
    return tuple(
        jnp.split(lax.psum_scatter(both, axis, scatter_dimension=dim, tiled=True), ends, axis=along)
    )


def from_everyone(value, axis):
    copies = jnp.broadcast_to(value, (lax.axis_size(axis), *value.shape))
    return lax.all_to_all(copies, axis, split_axis=0, concat_axis=0, tiled=True)


def over_copies(value, axis):
    return from_everyone(value, axis).astype(jnp.float32).sum(axis=0)


def to_low(values_in):
    return values_in.astype(jnp.bfloat16)


def matmul(left_side, right_side):
    return jnp.dot(left_side, right_side, preferred_element_type=jnp.float32)


def rows_inner(left_side, right_side):
    return lax.dot_general(
        left_side, right_side, (((0,), (0,)), ((), ())), preferred_element_type=jnp.float32
    )


def cols_inner(left_side, right_side):
    return lax.dot_general(
        left_side, right_side, (((1,), (1,)), ((), ())), preferred_element_type=jnp.float32
    )


def norm_forward(values_in, norm_gain, norm_shift):
    average = jnp.mean(values_in, axis=-1, keepdims=True)
    centred = values_in - average
    variance = jnp.mean(centred * centred, axis=-1, keepdims=True)
    inverse = lax.rsqrt(variance + epsilon)
    scaled = centred * inverse
    return (scaled * norm_gain + norm_shift, scaled, inverse)


def norm_backward(grad_out, scaled, inverse, norm_gain):
    grad_scaled = grad_out * norm_gain
    first_mean = jnp.mean(grad_scaled, axis=-1, keepdims=True)
    second = jnp.mean(grad_scaled * scaled, axis=-1, keepdims=True)
    return inverse * (grad_scaled - first_mean - scaled * second)


def place_of(row_ids, block_order, block_rows, blocks_per_seq):
    blocks = row_ids // block_rows
    table_size = block_order.shape[0]
    matches = blocks[:, None] == jnp.arange(table_size, dtype=jnp.int32)[None, :]
    orders = jnp.sum(jnp.where(matches, block_order[None, :], 0), axis=1)
    return (orders % blocks_per_seq * block_rows + row_ids % block_rows, blocks // blocks_per_seq)


def on_device(
    tokens,
    first_gain,
    first_shift,
    query_weight,
    query_bias,
    key_weight,
    value_weight,
    value_bias,
    out_weight,
    out_bias,
    second_gain,
    second_shift,
    up_weight,
    up_bias,
    down_weight,
    down_bias,
    cotangent,
    prefix,
    block_order,
):
    row_count = tokens.shape[0]
    head_total = query_weight.shape[1] // HEAD
    head_width = head_total * HEAD
    seq_len = row_count * lax.axis_size("dp")
    block_rows = row_count // 2
    blocks_per_seq = seq_len // block_rows
    score_scale = 1.0 / math.sqrt(HEAD)
    dp_index = lax.axis_index("dp")
    own_rows = dp_index * row_count + jnp.arange(row_count, dtype=jnp.int32)
    query_places, query_seqs = place_of(own_rows, block_order, block_rows, blocks_per_seq)
    seq_count = prefix.shape[0]
    seq_match = query_seqs[:, None] == jnp.arange(seq_count, dtype=jnp.int32)[None, :]
    query_limits = jnp.sum(jnp.where(seq_match, prefix[None, :], 0), axis=1)

    def key_mask(first_row, key_width):
        key_rows = first_row + jnp.arange(key_width, dtype=jnp.int32)
        key_places, key_seqs = place_of(key_rows, block_order, block_rows, blocks_per_seq)
        same_seq = key_seqs[None, :] == query_seqs[:, None]
        before = (key_places[None, :] <= query_places[:, None]) | (
            key_places[None, :] < query_limits[:, None]
        )
        return same_seq & before

    rows_gathered = sent_together(
        (to_low(query_weight), to_low(key_weight), to_low(value_weight), to_low(up_weight)),
        "dp",
        0,
        1,
    )
    query_all, key_all, value_all, up_all = rows_gathered
    cols_gathered = sent_together((to_low(out_weight), to_low(down_weight)), "dp", 1, 0)
    out_all, down_all = cols_gathered
    residual = tokens.astype(jnp.float32)
    normed, scaled_one, inverse_one = norm_forward(residual, first_gain, first_shift)
    normed_low = to_low(normed)
    queries = to_low(matmul(normed_low, query_all) + query_bias)
    keys_local = to_low(matmul(normed_low, key_all))
    values_local = to_low(matmul(normed_low, value_all) + value_bias)
    query_heads = queries.reshape(row_count, head_total, HEAD)

    def split_blocks(key_part, value_part):
        part_rows = key_part.shape[0]
        block_width = math.gcd(part_rows, 512)
        block_count = part_rows // block_width
        key_blocks = key_part.reshape(block_count, block_width, head_total, HEAD)
        value_blocks = value_part.reshape(block_count, block_width, head_total, HEAD)
        return (block_width, (key_blocks, value_blocks, jnp.arange(block_count, dtype=jnp.int32)))

    def block_scores(key_block):
        return (
            jnp.einsum("qhd,khd->hqk", query_heads, key_block, preferred_element_type=jnp.float32)
            * score_scale
        )

    key_source, value_source = sent_together((keys_local, values_local), "dp", 0, 1)
    source_start = 0
    block_width, block_items = split_blocks(key_source, value_source)

    def advance(state_now, block_item):
        key_block, value_block, block_index = block_item
        allowed = key_mask(source_start + block_index * block_width, block_width)

        def compute(state_old):
            row_max, row_sum = state_old
            scores = jnp.where(allowed[None], block_scores(key_block), masked_score)
            new_max = jnp.maximum(row_max, jnp.max(scores, axis=-1))
            exponent = jnp.where(allowed[None], jnp.exp(scores - new_max[..., None]), 0.0)
            return (new_max, row_sum * jnp.exp(row_max - new_max) + jnp.sum(exponent, axis=-1))

        return (lax.cond(jnp.any(allowed), compute, lambda state_old: state_old, state_now), None)

    initial = (
        jnp.full((head_total, row_count), masked_score, jnp.float32),
        jnp.zeros((head_total, row_count), jnp.float32),
    )
    running, _ = lax.scan(advance, initial, block_items)
    row_max, row_sum = running
    log_total = row_max + jnp.log(row_sum)
    attention_block_width, block_items = split_blocks(key_source, value_source)

    def advance(weighted, block_item):
        key_block, value_block, block_index = block_item
        allowed = key_mask(
            source_start + block_index * attention_block_width, attention_block_width
        )

        def compute(weighted_old):
            probs = jnp.where(
                allowed[None], jnp.exp(block_scores(key_block) - log_total[..., None]), 0.0
            )
            return weighted_old + jnp.einsum(
                "hqk,khd->hqd", to_low(probs), value_block, preferred_element_type=jnp.float32
            )

        return (
            lax.cond(jnp.any(allowed), compute, lambda weighted_old: weighted_old, weighted),
            None,
        )

    start = jnp.zeros((head_total, row_count, HEAD), jnp.float32)
    weighted, _ = lax.scan(advance, start, block_items)
    mixed_low = to_low(weighted.transpose(1, 0, 2).reshape(row_count, head_width))
    branch = (
        lax.psum(matmul(mixed_low, out_all).astype(jnp.bfloat16), "tensor").astype(jnp.float32)
        + out_bias
    )
    middle = residual + branch
    normed_two, scaled_two, inverse_two = norm_forward(middle, second_gain, second_shift)
    normed_two_low = to_low(normed_two)
    pre_act = matmul(normed_two_low, up_all) + up_bias
    hidden, gelu_back = jax.vjp(lambda inputs: jax.nn.gelu(inputs, approximate=False), pre_act)
    hidden_low = to_low(hidden)
    out_branch = (
        lax.psum(matmul(hidden_low, down_all).astype(jnp.bfloat16), "tensor").astype(jnp.float32)
        + down_bias
    )
    output = middle + out_branch
    grad_out = cotangent.astype(jnp.float32)
    grad_down_bias = jnp.sum(grad_out, axis=0)
    grad_down = rows_inner(hidden_low, cotangent)
    grad_hidden = cols_inner(cotangent, down_all)
    grad_pre_low = to_low(gelu_back(grad_hidden)[0])
    grad_up_bias = jnp.sum(grad_pre_low.astype(jnp.float32), axis=0)
    grad_up = rows_inner(normed_two_low, grad_pre_low)
    grad_normed_two = lax.psum(
        cols_inner(grad_pre_low, up_all).astype(jnp.bfloat16), "tensor"
    ).astype(jnp.float32)
    grad_gain_two = jnp.sum(grad_normed_two * scaled_two, axis=0)
    grad_shift_two = jnp.sum(grad_normed_two, axis=0)
    grad_middle = grad_out + norm_backward(grad_normed_two, scaled_two, inverse_two, second_gain)
    grad_middle_low = to_low(grad_middle)
    grad_out_bias = jnp.sum(grad_middle_low.astype(jnp.float32), axis=0)
    grad_out_weight = rows_inner(mixed_low, grad_middle_low)
    grad_mixed_low = to_low(cols_inner(grad_middle_low, out_all))
    grad_heads = grad_mixed_low.reshape(row_count, head_total, HEAD)
    row_delta = jnp.sum(grad_heads.astype(jnp.float32).transpose(1, 0, 2) * weighted, axis=-1)
    part_rows = key_source.shape[0]
    attend_block_width, block_items = split_blocks(key_source, value_source)

    def advance(grad_query, block_item):
        key_block, value_block, block_index = block_item
        allowed = key_mask(source_start + block_index * attend_block_width, attend_block_width)

        def compute(grad_now):
            probs = jnp.where(
                allowed[None], jnp.exp(block_scores(key_block) - log_total[..., None]), 0.0
            )
            grad_probs = jnp.einsum(
                "qhd,khd->hqk", grad_heads, value_block, preferred_element_type=jnp.float32
            )
            grad_scores = to_low(probs * (grad_probs - row_delta[..., None]))
            new_grad = (
                grad_now
                + jnp.einsum(
                    "hqk,khd->qhd", grad_scores, key_block, preferred_element_type=jnp.float32
                )
                * score_scale
            )
            grad_key = (
                jnp.einsum(
                    "hqk,qhd->khd", grad_scores, query_heads, preferred_element_type=jnp.float32
                )
                * score_scale
            )
            grad_value = jnp.einsum(
                "hqk,qhd->khd", to_low(probs), grad_heads, preferred_element_type=jnp.float32
            )
            return (new_grad, grad_key, grad_value)

        def skipped(grad_now):
            zero_block = jnp.zeros((attend_block_width, head_total, HEAD), jnp.float32)
            return (grad_now, zero_block, zero_block)

        new_grad, grad_key, grad_value = lax.cond(jnp.any(allowed), compute, skipped, grad_query)
        return (new_grad, (grad_key, grad_value))

    start_grad = jnp.zeros((row_count, head_total, HEAD), jnp.float32)
    grad_query, key_terms = lax.scan(advance, start_grad, block_items)
    grad_query, key_term, value_term = (
        grad_query,
        key_terms[0].reshape(part_rows, head_width),
        key_terms[1].reshape(part_rows, head_width),
    )
    grad_keys, grad_values = tuple(
        (
            part.astype(jnp.float32)
            for part in in_one_piece(
                (key_term.astype(jnp.bfloat16), value_term.astype(jnp.bfloat16)), "dp", 0, 1
            )
        )
    )
    grad_query_low = to_low(grad_query.reshape(row_count, head_width))
    grad_keys_low = to_low(grad_keys)
    grad_values_low = to_low(grad_values)
    grad_query_bias = jnp.sum(grad_query_low.astype(jnp.float32), axis=0)
    grad_value_bias = jnp.sum(grad_values_low.astype(jnp.float32), axis=0)
    grad_query_weight = rows_inner(normed_low, grad_query_low)
    grad_key_weight = rows_inner(normed_low, grad_keys_low)
    grad_value_weight = rows_inner(normed_low, grad_values_low)
    local_normed = (
        cols_inner(grad_query_low, query_all)
        + cols_inner(grad_keys_low, key_all)
        + cols_inner(grad_values_low, value_all)
    )
    grad_normed_one = lax.psum(local_normed.astype(jnp.bfloat16), "tensor").astype(jnp.float32)
    grad_gain_one = jnp.sum(grad_normed_one * scaled_one, axis=0)
    grad_shift_one = jnp.sum(grad_normed_one, axis=0)
    grad_tokens = grad_middle + norm_backward(grad_normed_one, scaled_one, inverse_one, first_gain)
    row_sums = tuple(
        (
            part.astype(jnp.float32)
            for part in in_one_piece(
                (
                    grad_query_weight.astype(jnp.bfloat16),
                    grad_key_weight.astype(jnp.bfloat16),
                    grad_value_weight.astype(jnp.bfloat16),
                    grad_up.astype(jnp.bfloat16),
                ),
                "dp",
                0,
                1,
            )
        )
    )
    column_sums = tuple(
        (
            part.astype(jnp.float32)
            for part in in_one_piece(
                (grad_out_weight.astype(jnp.bfloat16), grad_down.astype(jnp.bfloat16)), "dp", 1, 0
            )
        )
    )
    small_sums = (
        over_copies(grad_gain_one.astype(jnp.bfloat16), "dp").astype(jnp.float32),
        over_copies(grad_shift_one.astype(jnp.bfloat16), "dp").astype(jnp.float32),
        over_copies(grad_query_bias.astype(jnp.bfloat16), "dp").astype(jnp.float32),
        over_copies(grad_value_bias.astype(jnp.bfloat16), "dp").astype(jnp.float32),
        over_copies(grad_out_bias.astype(jnp.bfloat16), "dp").astype(jnp.float32),
        over_copies(grad_gain_two.astype(jnp.bfloat16), "dp").astype(jnp.float32),
        over_copies(grad_shift_two.astype(jnp.bfloat16), "dp").astype(jnp.float32),
        over_copies(grad_up_bias.astype(jnp.bfloat16), "dp").astype(jnp.float32),
        over_copies(grad_down_bias.astype(jnp.bfloat16), "dp").astype(jnp.float32),
    )
    return (
        output.astype(jnp.bfloat16),
        grad_tokens,
        small_sums[0],
        small_sums[1],
        row_sums[0],
        small_sums[2],
        row_sums[1],
        row_sums[2],
        small_sums[3],
        column_sums[0],
        small_sums[4],
        small_sums[5],
        small_sums[6],
        row_sums[3],
        small_sums[7],
        column_sums[1],
        small_sums[8],
    )


def solution(mesh):
    return jax.shard_map(
        on_device,
        mesh=mesh,
        in_specs=(
            P("dp", None),
            P(),
            P(),
            P("dp", "tensor"),
            P("tensor"),
            P("dp", "tensor"),
            P("dp", "tensor"),
            P("tensor"),
            P("tensor", "dp"),
            P(),
            P(),
            P(),
            P("dp", "tensor"),
            P("tensor"),
            P("tensor", "dp"),
            P(),
            P("dp", None),
            P(),
            P(),
        ),
        out_specs=(
            P("dp", None),
            P("dp", None),
            P(),
            P(),
            P("dp", "tensor"),
            P("tensor"),
            P("dp", "tensor"),
            P("dp", "tensor"),
            P("tensor"),
            P("tensor", "dp"),
            P(),
            P(),
            P(),
            P("dp", "tensor"),
            P("tensor"),
            P("tensor", "dp"),
            P(),
        ),
        check_vma=False,
    )
```

profile of v0, /device:TPU:1, one launch (start us, length us, event | category | flops | bytes accessed | tf_op | source)
XLA Modules:
  0.0 1173.6 jit_solution(17197489712279023680)
XLA Ops:
  15.4 47.7 %all-gather.4.cloned.1.call-done = bf16[2048,1792]{1,0:T(8,128)(2,1)} async-done(((bf16[128,1792]{1,0:T(8,128)(2,1)}), bf16[2048,1792]{1,0:T(8,128)(2,1)}) %all-gather.4.cloned.1.call-update) | async-done | bytes 7340048 | tf_op jit(solution)/shard_map/all_gather | solution.py:17
  73.4 49.0 %all-gather.6.cloned.1.call-done = bf16[8192,512]{0,1:T(8,128)(2,1)} async-done(((bf16[512,512]{0,1:T(8,128)(2,1)}), bf16[8192,512]{0,1:T(8,128)(2,1)}) %all-gather.6.cloned.1.call-update) | async-done | bytes 8388624 | tf_op jit(solution)/shard_map/all_gather | solution.py:17
  122.3 5.1 fusion.170
  127.4 3.8 copy.180
  131.3 8.0 copy.143
  139.2 93.2 %while.57 = (s32[]{:T(128)}, f32[2,512]{1,0:T(2,128)S(1)}, f32[2,512]{1,0:T(2,128)S(1)}, s32[16]{0:T(128)S(1)}, s32[32]{0:T(128)S(1)}, /*index=5*/s32[512]{0:T(5...) while((s32[]{:T(128)}, f32[2,512]{1,0:T(2,128)S(1)}, ...), condition=%wide.region_10.11_spmd.clone.clone, body=%wide.region_3.0_spmd.clone.clone.sunk | while | flops 140081152 | bytes 5585795 | solution.py:184
  232.5 6.0 copy.181
  238.5 7.9 copy.145
  246.4 93.6 %while.58 = (s32[]{:T(128)}, f32[2,512,128]{2,1,0:T(8,128)S(1)}, s32[16]{0:T(128)S(1)}, s32[32]{0:T(128)S(1)}, s32[512]{0:T(512)S(1)}, /*index=5*/bf16[16,512,2,...) while((s32[]{:T(128)}, f32[2,512,128]{2,1,0:T(8,128)S(1)}, ...), condition=%wide.region_16.17_spmd.clone.clone, body=%wide.region_11.16_spmd.clone.clone.sunk | while | flops 272330752 | bytes 2391411 | solution.py:209
  344.2 88.0 %all-reduce.5.cloned.1.call-done = bf16[512,2048]{1,0:T(8,128)(2,1)} async-done(((bf16[512,2048]{1,0:T(8,128)(2,1)}), bf16[512,2048]{1,0:T(8,128)(2,1)}) %all-reduce.5.cloned.1.call-update) | async-done | bytes 2097168 | tf_op jit(solution)/shard_map/psum | solution.py:212
  435.9 10.5 multiply_convert_fusion
  450.5 3.8 fusion.118
  454.4 91.3 %all-reduce.7.cloned.1.call-done = bf16[512,2048]{1,0:T(8,128)(2,1)} async-done(((bf16[512,2048]{1,0:T(8,128)(2,1)}), bf16[512,2048]{1,0:T(8,128)(2,1)}) %all-reduce.7.cloned.1.call-update) | async-done | bytes 2097168 | tf_op jit(solution)/shard_map/psum | solution.py:233
  545.7 4.5 fusion.107
  550.3 3.4 convert_reduce_fusion.10
  558.2 185.5 %while.59 = (s32[]{:T(128)}, f32[512,2,128]{2,0,1:T(8,128)S(1)}, bf16[16,512,2,128]{3,1,2,0:T(8,128)(2,1)}, bf16[16,512,2,128]{3,1,2,0:T(8,128)(2,1)}, s32[16]{0...) while((s32[]{:T(128)}, f32[512,2,128]{2,0,1:T(8,128)S(1)}, ...), condition=%wide.region_30.31_spmd.clone.clone, body=%wide.region_25.30_spmd.clone.clone.sunk | while | flops 676950016 | bytes 15504335 | solution.py:286
  562.6 5.8 conditional.14
  574.1 5.8 conditional.14
  585.7 5.8 conditional.14
  597.3 5.8 conditional.14
  608.9 5.8 conditional.14
  620.5 5.8 conditional.14
  632.1 5.8 conditional.14
  643.7 5.8 conditional.14
  655.3 5.8 conditional.14
  666.9 5.8 conditional.14
  678.5 5.8 conditional.14
  690.1 5.8 conditional.14
  701.7 5.8 conditional.14
  713.3 5.8 conditional.14
  724.9 5.8 conditional.14
  736.4 5.8 conditional.14
  743.7 7.8 copy.154
  751.5 8.5 copy.183
  760.0 8.0 copy.153
  768.0 8.5 copy.182
  776.4 7.7 pad_maximum_fusion
  784.2 4.4 convolution_convert_fusion
  792.3 8.1 copy.172
  800.8 6.2 fusion.121
  807.1 4.0 fusion.144
  811.2 72.3 %reduce-scatter.8.cloned.1.call-done = bf16[512,512]{0,1:T(8,128)(2,1)} async-done(((bf16[8192,512]{0,1:T(8,128)(2,1)}), bf16[512,512]{0,1:T(8,128)(2,1)}) %reduce-scatter.8.cloned.1.call-update) | async-done | bytes 524304 | tf_op jit(solution)/shard_map/reduce_scatter | solution.py:31
  889.6 4.8 convolution_convert_fusion.1
  896.6 3.7 pad_maximum_fusion.1
  900.3 10.1 copy.170
  912.5 5.9 all-to-all-start.7
  919.8 4.4 all-to-all-done.7
  924.2 3.7 all-to-all-start.2
  929.7 3.8 all-to-all-done.2
  933.5 3.9 all-to-all-start.4
  939.1 4.2 all-to-all-done.4
  943.3 3.9 all-to-all-start.5
  949.0 4.1 all-to-all-done.5
  953.1 3.7 all-to-all-start.6
  959.2 3.6 all-to-all-done.6
  962.7 3.7 all-to-all-start.8
  967.2 5.2 all-to-all-done.8
  975.8 3.7 all-to-all-start.3
  985.9 87.0 %all-reduce.9.cloned.1.call-done = (bf16[512,2048]{1,0:T(8,128)(2,1)}, bf16[512,2048]{1,0:T(8,128)(2,1)}) async-done(((bf16[512,2048]{1,0:T(8,128)(2,1)}, bf16[512,2048]{1,0:T(8,128)(2,1)}), (bf16[512,2048]{1,0:T(8,128)(2,1)}, bf16[512,2048]{1,0:T(8,128)(2,1)})) %all-reduce.9.cloned.1.call-update) | async-done | bytes 4194320 | tf_op jit(solution)/shard_map/psum | solution.py:222
  1072.9 3.5 fusion.109
  1078.2 5.0 all-to-all-start
  1089.3 4.3 all-to-all-start.1
  1093.6 7.2 fusion.101
  1102.2 59.0 %reduce-scatter.10.cloned.1.call-done = bf16[128,1792]{1,0:T(8,128)(2,1)} async-done(((bf16[2048,1792]{1,0:T(8,128)(2,1)}), bf16[128,1792]{1,0:T(8,128)(2,1)}) %reduce-scatter.10.cloned.1.call-update) | async-done | bytes 458768
  (775 shorter events, 458.6 us)
Async XLA Ops:
  7.2 4.9 copy-start
  7.2 6.0 copy-start.26
  7.2 6.0 copy-start.19
  7.2 55.8 %all-gather.4.cloned.1.call-start = ((), (), s32[]{:S(2)}) async-start(), calls=%async_computation.12 | async-start | bytes 7798784 | tf_op jit(solution)/shard_map/all_gather | solution.py:17
  12.0 110.3 %all-gather.6.cloned.1.call-start = ((), (), s32[]{:S(2)}) async-start(), calls=%async_computation.13 | async-start | bytes 8912896 | tf_op jit(solution)/shard_map/all_gather | solution.py:17
  12.5 50.6 %copy-start.21 = (f32[512]{0:T(512)}, f32[512]{0:T(512)S(1)}, u32[]{:S(2)}) copy-start(f32[512]{0:T(512)S(1)} %broadcast_multiply_fusion.5) | copy-start | bytes 6148
  13.2 52.5 %copy-start.30 = (f32[256]{0:T(256)S(1)}, f32[256]{0:T(256)}, u32[]{:S(2)}) copy-start(f32[256]{0:T(256)} %param.38) | copy-start | bytes 3076
  13.2 49.9 %copy-start.23 = (f32[512]{0:T(512)}, f32[512]{0:T(512)S(1)}, u32[]{:S(2)}) copy-start(f32[512]{0:T(512)S(1)} %add_rsqrt_fusion.1) | copy-start | bytes 6148
  15.4 53.9 %copy-start.15 = (f32[1024,128]{1,0:T(8,128)S(1)}, f32[1024,128]{1,0:T(8,128)}, u32[]{:S(2)}) copy-start(f32[1024,128]{1,0:T(8,128)} %param.45) | copy-start | bytes 1572868
  15.4 53.9 %copy-start.18 = (f32[256,128]{1,0:T(8,128)S(1)}, f32[256,128]{1,0:T(8,128)}, u32[]{:S(2)}) copy-start(f32[256,128]{1,0:T(8,128)} %param.39) | copy-start | bytes 393220
  65.7 4.8 copy-start.17
  65.7 4.9 copy-start.31
  69.2 271.0 %all-gather.8.cloned.1.call-start = ((), (), s32[]{:S(2)}) async-start(), calls=%async_computation.14 | async-start | bytes 5570560 | tf_op jit(solution)/shard_map/all_gather | solution.py:17
  70.1 362.1 %all-reduce.5.cloned.1.call-start = ((), (), s32[]{:S(2)}) async-start(), calls=%async_computation.15 | async-start | bytes 4194304 | tf_op jit(solution)/shard_map/psum | solution.py:212
  340.0 94.7 %copy-start.7 = (bf16[512,2,128]{2,0,1:T(8,128)(2,1)}, bf16[512,2,128]{2,0,1:T(8,128)(2,1)S(1)}, u32[]{:S(2)}) copy-start(bf16[512,2,128]{2,0,1:T(8,128)(2,1)S(1)} %get-tuple-element.1875) | copy-start | bytes 786436
  340.0 92.2 %copy-start.16 = (f32[2048]{0:T(1024)S(1)}, f32[2048]{0:T(1024)}, u32[]{:S(2)}) copy-start(f32[2048]{0:T(1024)} %param.40) | copy-start | bytes 24580
  340.2 94.6 %copy-start.11 = (bf16[2,512,128]{1,2,0:T(8,128)(2,1)}, bf16[2,512,128]{1,2,0:T(8,128)(2,1)S(1)}, u32[]{:S(2)}) copy-start(bf16[2,512,128]{1,2,0:T(8,128)(2,1)S(1)} %copy.146) | copy-start | bytes 786436
  343.6 92.3 %copy-start.25 = (f32[2048]{0:T(1024)S(1)}, f32[2048]{0:T(1024)}, u32[]{:S(2)}) copy-start(f32[2048]{0:T(1024)} %param.41) | copy-start | bytes 24580
  343.6 92.3 %copy-start.28 = (f32[2048]{0:T(1024)S(1)}, f32[2048]{0:T(1024)}, u32[]{:S(2)}) copy-start(f32[2048]{0:T(1024)} %param.42) | copy-start | bytes 24580
  343.6 92.3 %copy-start.29 = (f32[1024]{0:T(1024)S(1)}, f32[1024]{0:T(1024)}, u32[]{:S(2)}) copy-start(f32[1024]{0:T(1024)} %param.44) | copy-start | bytes 12292
  343.6 202.1 %all-reduce.7.cloned.1.call-start = ((), (), s32[]{:S(2)}) async-start(), calls=%async_computation.16 | async-start | bytes 4194304 | tf_op jit(solution)/shard_map/psum | solution.py:233
  434.8 11.7 slice-start.2
  434.8 15.7 %slice-start = ((s8[7340032]{0:T(1024)(128)(4,1)}), s8[4194304]{0:T(1024)(128)(4,1)S(1)}, s32[]{:S(2)}) async-start(s8[7340032]{0:T(1024)(128)(4,1)} %bitcast.152), calls=%async_computation.21 | async-start | bytes 8388608
  435.9 10.6 copy-start.13
  435.9 10.5 slice-start.3
  435.9 14.6 %slice-start.1 = ((s8[7340032]{0:T(1024)(128)(4,1)}), s8[3145728]{0:T(1024)(128)(4,1)S(1)}, s32[]{:S(2)}) async-start(s8[7340032]{0:T(1024)(128)(4,1)} %bitcast.152), calls=%async_computation.22 | async-start | bytes 6291456
  454.4 429.1 %reduce-scatter.8.cloned.1.call-start = ((), (), s32[]{:S(2)}) async-start(), calls=%async_computation.17 | async-start | bytes 8912896 | tf_op jit(solution)/shard_map/reduce_scatter | solution.py:31
  545.7 4.5 copy-start.4
  545.7 4.5 copy-start.9
  545.7 4.5 copy-start.14
  562.6 4.8 copy-start.8
  574.1 4.8 copy-start.8
  585.7 4.8 copy-start.8
  597.3 4.8 copy-start.8
  608.9 4.8 copy-start.8
  620.5 4.8 copy-start.8
  632.1 4.8 copy-start.8
  643.7 4.9 copy-start.8
  655.3 4.8 copy-start.8
  666.9 4.8 copy-start.8
  678.5 4.9 copy-start.8
  690.1 4.9 copy-start.8
  701.7 4.8 copy-start.8
  713.3 4.9 copy-start.8
  724.9 4.8 copy-start.8
  736.4 4.8 copy-start.8
  784.2 195.9 %reduce-scatter.12.cloned.1.call-start = ((), (), s32[]{:S(2)}) async-start(), calls=%async_computation.19 | async-start | bytes 5570560
  784.2 4.5 copy-start.2
  800.4 272.6 %all-reduce.9.cloned.1.call-start = ((), (), s32[]{:S(2)}) async-start(), calls=%async_computation.20 | async-start | bytes 8388608 | tf_op jit(solution)/shard_map/psum | solution.py:222
  889.5 271.7 %reduce-scatter.10.cloned.1.call-start = ((), (), s32[]{:S(2)}) async-start(), calls=%async_computation.18 | async-start | bytes 7798784
  889.6 4.8 copy-start.5
  910.4 162.5 %copy-start.20 = (f32[2048]{0:T(1024)S(1)}, f32[2048]{0:T(1024)}, u32[]{:S(2)}) copy-start(f32[2048]{0:T(1024)} %param.32) | copy-start | bytes 24580
  910.4 162.5 %copy-start.22 = (f32[512]{0:T(512)S(1)}, f32[512]{0:T(512)}, u32[]{:S(2)}) copy-start(f32[512]{0:T(512)} %copy-done.21) | copy-start | bytes 6148
  910.5 162.5 %copy-start.24 = (f32[512]{0:T(512)S(1)}, f32[512]{0:T(512)}, u32[]{:S(2)}) copy-start(f32[512]{0:T(512)} %copy-done.23) | copy-start | bytes 6148
  912.5 11.8 %all-to-all-start.7 = ((bf16[16,2,512]{2,1,0:T(2,128)(2,1)}), bf16[16,2,512]{2,1,0:T(2,128)(2,1)S(1)}, u32[]{:S(2)}, u32[]{:S(2)}) async-start(bf16[16,2,512]{2,1,0:T(2,128)(2,1)} %reshape.445), calls=%async_computation.8 | async-start | bytes 65536 | tf_op jit(solution)/shard_map/all_to_all | solution.py:37
  924.2 9.3 all-to-all-start.2
  933.5 9.8 all-to-all-start.4
  943.3 9.8 all-to-all-start.5
  953.1 9.6 all-to-all-start.6
  962.7 9.6 all-to-all-start.8
  975.8 9.5 all-to-all-start.3
  982.9 110.7 %copy-start.27 = (f32[2048]{0:T(1024)S(1)}, f32[2048]{0:T(1024)}, u32[]{:S(2)}) copy-start(f32[2048]{0:T(1024)} %param.46) | copy-start | bytes 24580
  1078.2 11.1 all-to-all-start
  1089.3 11.6 all-to-all-start.1
  (6 other events, 15.3 us)
Sparse Core Ops, SparseCore 0:
  12.2 50.8 all-gather.3
  69.3 52.9 all-gather.5
  124.5 50.7 all-gather.7
  343.7 88.4 all-reduce.4
  454.5 91.1 all-reduce.6
  784.3 99.1 reduce-scatter.7
  885.9 71.5 reduce-scatter.11
  960.6 112.2 all-reduce.8
  1075.4 85.8 reduce-scatter.9
where the time goes:
time: 1180 us; the launch traced here: 1170 us
  waiting for transfers between devices  524 us (44%)
  matrix products  208 us (18%)
  other arithmetic  169 us (14%)
  local copies, waits for them, and re-layouts  153 us (13%)
  loops' own time  66 us (6%)
  starting transfers between devices  39.3 us (3%)
  between operations  15 us (1%)
    all_gather x3, waiting for transfers between devices, sent_together(): lax.all_gather(both, axis, axis=dim, tiled=True)  96.7 us
    psum x1, waiting for transfers between devices, on_device(): lax.psum(cols_inner(grad_pre_low, up_all).astype(jnp.bfloat16), 'tensor')  91.3 us
    psum x1, waiting for transfers between devices, on_device(): lax.psum(matmul(mixed_low, out_all).astype(jnp.bfloat16), 'tensor')  88 us
    psum x1, waiting for transfers between devices, on_device(): lax.psum(matmul(hidden_low, down_all).astype(jnp.bfloat16), 'tensor')  87 us
    unnamed x111, local copies, waits for them, and re-layouts  74.9 us
    reduce_scatter x1, waiting for transfers between devices, in_one_piece(): lax.psum_scatter(both, axis, scatter_dimension=dim, tiled=True)  72.3 us
    unnamed x11, waiting for transfers between devices  59.2 us
    reduce_or x48, other arithmetic, advance(): jnp.any(allowed)  58 us
  transfers between devices with their start and end apart: 18, of which 15 were waited for; matrix products, arithmetic and copies ran while one was open for 23% of the time, Pallas kernels for 0%

commit v1 on v0

v1 whole, which is shorter than its diff:
```python
import functools
import math

import jax
import jax.numpy as jnp
from jax import lax
from jax.experimental import pallas as pl
from jax.experimental.pallas import tpu as pltpu
from jax.sharding import PartitionSpec as P

HEAD = 128
BLK = 256
GRP = 4
RING = 4
EPS = 1e-05
LOG2E = math.log2(math.e)
SCALE = 1.0 / math.sqrt(HEAD)
C1 = LOG2E * SCALE
NN = (((1,), (0,)), ((), ()))
NT = (((1,), (1,)), ((), ()))
TN = (((0,), (0,)), ((), ()))
MESH = pl.DeviceIdType.MESH
VM = pl.BlockSpec(memory_space=pltpu.VMEM)
SM = pl.BlockSpec(memory_space=pltpu.SMEM)
BF = jnp.bfloat16
F32 = jnp.float32
DMA = pltpu.SemaphoreType.DMA


def dg(a, b, dims):
    return lax.dot_general(a, b, dims, preferred_element_type=F32)


def struct(shape, dtype):
    return jax.ShapeDtypeStruct(shape, dtype)


class Eight:
    def __init__(self, axis):
        d, t = lax.axis_index("dp"), lax.axis_index("tensor")
        self.axis, self.d, self.t = axis, d, t
        if axis == "dp":
            self.r, self.p = d // 4, lax.rem(d // 2, 2)
        else:
            self.r, self.p = lax.rem(t, 4), t // 4

    def ring(self, i):
        return lax.rem(self.r + i, RING)

    def index(self, r, p):
        return r * 2 + p if self.axis == "dp" else p * 4 + r

    def device(self, r, p):
        if self.axis == "dp":
            return ((r * 2 + p) * 2 + lax.rem(self.d, 2), self.t)
        return (self.d, p * 4 + r)

    def others(self):
        return [self.device(self.ring(i), self.p) for i in (1, 2, 3)] + [self.device(self.r, 1 - self.p)]


def other_core():
    d = lax.axis_index("dp")
    return (d + 1 - 2 * lax.rem(d, 2), lax.axis_index("tensor"))


def greet(devices):
    barrier = pltpu.get_barrier_semaphore()
    for device in devices:
        pl.semaphore_signal(barrier, inc=1, device_id=device, device_id_type=MESH)
    pl.semaphore_wait(barrier, len(devices))


def send(src, dst, sems, k, device):
    copy = pltpu.make_async_remote_copy(
        src_ref=src, dst_ref=dst, send_sem=sems[0].at[k], recv_sem=sems[1].at[k],
        device_id=device, device_id_type=MESH)
    copy.start()
    return copy


def split_at(rows):
    return max(16, int(rows * 0.4) // 16 * 16)


class Gather:
    SEMS = 10

    def __init__(self, group, out, sems):
        self.g, self.out, self.sems = group, out, sems
        self.cut = split_at(out.shape[1])

    def start(self):
        g, out = self.g, self.out
        own = out.at[g.index(g.r, g.p)]
        self.first = [send(own, own, self.sems, 0, g.device(g.r, 1 - g.p))]
        for i in (1, 2, 3):
            self.first.append(send(own, own, self.sems, i, g.device(g.ring(i), g.p)))

    def forward(self):
        g, out, cut = self.g, self.out, self.cut
        self.second = []
        self.first[0].wait_recv()
        part = out.at[g.index(g.r, 1 - g.p), pl.ds(0, cut)]
        for i in (1, 2, 3):
            self.second.append(send(part, part, self.sems, 3 + i, g.device(g.ring(i), g.p)))
        rest = out.shape[1] - cut
        for i in (1, 2, 3):
            self.first[i].wait_recv()
            part = out.at[g.index(g.ring(4 - i), g.p), pl.ds(cut, rest)]
            self.second.append(send(part, part, self.sems, 6 + i, g.device(g.r, 1 - g.p)))

    def finish(self):
        for copy in self.second:
            copy.wait_recv()
        for copy in self.first + self.second:
            copy.wait_send()


class Scatter:
    SEMS = 14

    @staticmethod
    def scratch(rows, width):
        cut = split_at(rows)
        return [
            pltpu.VMEM((3, cut, width), BF), pltpu.VMEM((3, rows - cut, width), BF),
            pltpu.VMEM((4, rows, width), BF), pltpu.VMEM((cut, width), BF),
            pltpu.VMEM((3, rows - cut, width), BF), DMA((14,)), DMA((14,))]

    def __init__(self, group, part, scratch, step):
        self.g, self.part, self.step = group, part, step
        self.at_a, self.at_b, self.last, self.sum_a, self.sum_b = scratch[:5]
        self.sems = scratch[5:]
        self.rows = part.shape[1]
        self.cut = split_at(self.rows)
        self.low, self.high = pl.ds(0, self.cut), pl.ds(self.cut, self.rows - self.cut)

    def start(self):
        g, part, low, high = self.g, self.part, self.low, self.high
        pair = g.device(g.r, 1 - g.p)
        a, b, c = [], [], []
        for i in (1, 2, 3):
            ring = g.device(g.ring(i), g.p)
            b.append(send(part.at[g.index(g.ring(i), 1 - g.p), high], self.at_b.at[i - 1], self.sems, 2 + i, pair))
            a.append(send(part.at[g.index(g.ring(i), 1 - g.p), low], self.at_a.at[i - 1], self.sems, i - 1, ring))
        for i in (1, 2, 3):
            ring = g.device(g.ring(i), g.p)
            c.append(send(part.at[g.index(g.ring(i), g.p), low], self.last.at[i, low], self.sems, 6 + i, ring))
        c.append(send(part.at[g.index(g.r, 1 - g.p), high], self.last.at[0, high], self.sems, 6, pair))
        self.a, self.b, self.c = a, b, c

    def by_rows(self, rows, body):
        step = self.step
        count = rows // step

        @pl.loop(0, count)
        def _(n):
            body(pl.multiple_of(n * step, step), step)

        if rows % step:
            body(count * step, rows % step)

    def forward(self):
        g, part = self.g, self.part
        pair = g.device(g.r, 1 - g.p)
        for i in (1, 2, 3):
            self.b[i - 1].wait_recv()
            mine = g.index(g.ring(i), g.p)

            def add_b(at, n, i=i, mine=mine):
                rows = pl.ds(at, n)
                total = part[mine, pl.ds(self.cut + at, n), :].astype(F32) + self.at_b[i - 1, rows, :].astype(F32)
                self.sum_b[i - 1, rows, :] = total.astype(BF)

            self.by_rows(self.rows - self.cut, add_b)
            self.c.append(send(self.sum_b.at[i - 1], self.last.at[i, self.high], self.sems, 9 + i, g.device(g.ring(i), g.p)))
        for copy in self.a:
            copy.wait_recv()
        mine = g.index(g.r, 1 - g.p)

        def add_a(at, n):
            rows = pl.ds(at, n)
            total = part[mine, rows, :].astype(F32)
            for i in range(3):
                total += self.at_a[i, rows, :].astype(F32)
            self.sum_a[rows, :] = total.astype(BF)

        self.by_rows(self.cut, add_a)
        self.c.append(send(self.sum_a, self.last.at[0, self.low], self.sems, 13, pair))

    def finish(self, store):
        g = self.g
        for copy in self.c:
            copy.wait_recv()
        mine = g.index(g.r, g.p)

        def add(at, n):
            rows = pl.ds(at, n)
            total = self.part[mine, rows, :].astype(F32)
            for i in range(4):
                total += self.last[i, rows, :].astype(F32)
            store(rows, total)

        self.by_rows(self.rows, add)
        for copy in self.a + self.b + self.c:
            copy.wait_send()


def remote_call(kernel, name, cid, outs, ins, scratch, *args):
    return pl.pallas_call(
        kernel, out_shape=outs, in_specs=ins, out_specs=jax.tree.map(lambda _: VM, outs),
        scratch_shapes=scratch, name=name,
        compiler_params=pltpu.CompilerParams(collective_id=cid, has_side_effects=True, vmem_limit_bytes=56 << 20),
    )(*args)


def weights_kernel(w_ref, n_ref, w_out, n_out, ss, rs, css, crs):
    g = Eight("dp")
    c = lax.rem(g.d, 2)
    core = other_core()
    greet(g.others() + [core])
    me = g.index(g.r, g.p)
    rows = w_ref.shape[1]
    csems = (css, crs)
    swap = send(w_ref.at[1 - c], w_out.at[me, pl.ds(pl.multiple_of(c * rows, rows), rows)], csems, 0, core)
    norm = send(n_ref, n_out.at[c], csems, 1, core)
    w_out[me, pl.ds(pl.multiple_of(c * rows, rows), rows), :] = w_ref[c]
    swap.wait_recv()
    gather = Gather(g, w_out, (ss, rs))
    gather.start()
    n_out[c] = n_ref[...]
    gather.forward()
    gather.finish()
    norm.wait()
    swap.wait_send()


def gather_weights(w, n):
    rows, width = w.shape[1:]
    return remote_call(
        weights_kernel, "weights", 1,
        (struct((8, 2 * rows, width), BF), struct((2, *n.shape), BF)), [VM, VM],
        [DMA((10,)), DMA((10,)), DMA((2,)), DMA((2,))], w, n)


def keys_kernel(k_ref, out, ss, rs):
    g = Eight("dp")
    greet(g.others())
    out[g.index(g.r, g.p)] = k_ref[...]
    gather = Gather(g, out, (ss, rs))
    gather.start()
    gather.forward()
    gather.finish()


def gather_keys(kv):
    return remote_call(
        keys_kernel, "keys", 2, struct((8, *kv.shape), BF), [VM], [DMA((10,)), DMA((10,))], kv)


def invert(meta, inv, nblk):
    @pl.loop(0, nblk)
    def _(b):
        inv[meta[b]] = b


def extents(meta, a, nblk):
    place = meta[meta[nblk + 1] + a]
    prefix = meta[nblk]
    full = jnp.maximum(place, prefix // BLK)
    seen = jnp.maximum(place + 1, (prefix + BLK - 1) // BLK)
    return place, prefix, full // GRP, (seen + GRP - 1) // GRP


def attn_fwd_kernel(meta, q_ref, kv_ref, o_ref, lse_ref, inv, m_ref, acc_ref):
    rows = q_ref.shape[0]
    nblk = kv_ref.shape[0] // BLK
    invert(meta, inv, nblk)
    ones = jnp.ones((BLK, HEAD), BF)

    @pl.loop(0, rows // BLK)
    def _(a):
        place, prefix, full, seen = extents(meta, a, nblk)
        q = q_ref[pl.ds(a * BLK, BLK), :]
        m_ref[...] = jnp.full((BLK, HEAD), -1e30, F32)
        acc_ref[...] = jnp.zeros((BLK, 2 * HEAD), F32)

        def step(j, masked):
            ks, vs = [], []
            for i in range(GRP):
                kb = pl.multiple_of(inv[j * GRP + i] * BLK, BLK)
                ks.append(kv_ref[pl.ds(kb, BLK), :HEAD])
                vs.append(kv_ref[pl.ds(kb, BLK), HEAD:])
            ss = [dg(q, k, NT) for k in ks]
            if masked:
                lim = jnp.maximum(place * BLK + lax.broadcasted_iota(jnp.int32, (BLK, BLK), 0), prefix - 1)
                for i in range(GRP):
                    at = (j * GRP + i) * BLK + lax.broadcasted_iota(jnp.int32, (BLK, BLK), 1)
                    ss[i] = jnp.where(at <= lim, ss[i], -1e30)
            top = ss[0]
            for s in ss[1:]:
                top = jnp.maximum(top, s)
            old = m_ref[:, :1]
            new = jnp.maximum(old, jnp.max(top, axis=1, keepdims=True) * C1)
            alpha = jnp.exp2(old - new)
            add = None
            for s, v in zip(ss, vs):
                p = jnp.exp2(s * C1 - new).astype(BF)
                t = jnp.dot(p, jnp.concatenate([v, ones], axis=1), preferred_element_type=F32)
                add = t if add is None else add + t
            acc_ref[...] = acc_ref[...] * alpha + add
            m_ref[...] = jnp.broadcast_to(new, (BLK, HEAD))

        @pl.loop(0, full)
        def _(j):
            step(j, False)

        @pl.loop(full, seen)
        def _(j):
            step(j, True)

        total = acc_ref[:, HEAD:]
        o_ref[pl.ds(a * BLK, BLK), :] = (acc_ref[:, :HEAD] / total).astype(BF)
        lse = m_ref[...] + jnp.log2(total)
        lse_ref[pl.ds(a, 1), :] = jnp.transpose(lse)[:1, :]


def attn_fwd(meta, q, kv):
    rows = q.shape[0]
    nblk = kv.shape[0] // BLK
    return pl.pallas_call(
        attn_fwd_kernel,
        out_shape=(struct((rows, HEAD), BF), struct((rows // BLK, BLK), F32)),
        in_specs=[SM, VM, VM],
        out_specs=(VM, VM),
        scratch_shapes=[pltpu.SMEM((nblk,), jnp.int32), pltpu.VMEM((BLK, HEAD), F32), pltpu.VMEM((BLK, 2 * HEAD), F32)],
        compiler_params=pltpu.CompilerParams(vmem_limit_bytes=24 << 20),
        cost_estimate=pl.CostEstimate(flops=8 * rows * kv.shape[0] * HEAD, bytes_accessed=6 << 20, transcendentals=rows * kv.shape[0]),
        name="attn_fwd",
    )(meta, q, kv)


def attn_bwd_kernel(meta, q_ref, kv_ref, o_ref, do_ref, lse_ref, dq_ref, dkv_ref, inv, dq_acc, dk_acc, dv_acc):
    rows = q_ref.shape[0]
    nblk = kv_ref.shape[0] // BLK
    invert(meta, inv, nblk)
    dk_acc[...] = jnp.zeros_like(dk_acc)
    dv_acc[...] = jnp.zeros_like(dv_acc)

    @pl.loop(0, rows // BLK)
    def _(a):
        place, prefix, full, seen = extents(meta, a, nblk)
        mine = pl.ds(a * BLK, BLK)
        q = q_ref[mine, :]
        do = do_ref[mine, :]
        prod = do.astype(F32) * o_ref[mine, :].astype(F32)
        delta = jnp.sum(jnp.transpose(prod), axis=0, keepdims=True)
        lse = lse_ref[pl.ds(a, 1), :]
        dq_acc[...] = jnp.zeros_like(dq_acc)

        def step(j, masked):
            add = None
            for i in range(GRP):
                kb = pl.multiple_of(inv[j * GRP + i] * BLK, BLK)
                at_k = pl.ds(kb, BLK)
                k = kv_ref[at_k, :HEAD]
                v = kv_ref[at_k, HEAD:]
                p = jnp.exp2(dg(k, q, NT) * C1 - lse)
                if masked:
                    lim = jnp.maximum(place * BLK + lax.broadcasted_iota(jnp.int32, (BLK, BLK), 1), prefix - 1)
                    at = (j * GRP + i) * BLK + lax.broadcasted_iota(jnp.int32, (BLK, BLK), 0)
                    p = jnp.where(at <= lim, p, 0.0)
                ds = (p * (dg(v, do, NT) - delta)).astype(BF)
                dv_acc[at_k, :] += jnp.dot(p.astype(BF), do, preferred_element_type=F32)
                dk_acc[at_k, :] += jnp.dot(ds, q, preferred_element_type=F32)
                t = dg(ds, k, TN)
                add = t if add is None else add + t
            dq_acc[...] += add

        @pl.loop(0, full)
        def _(j):
            step(j, False)

        @pl.loop(full, seen)
        def _(j):
            step(j, True)

        dq_ref[mine, :] = (dq_acc[...] * SCALE).astype(BF)

    @pl.loop(0, nblk)
    def _(b):
        at = pl.ds(pl.multiple_of(b * BLK, BLK), BLK)
        dkv_ref[at, :HEAD] = (dk_acc[at, :] * SCALE).astype(BF)
        dkv_ref[at, HEAD:] = dv_acc[at, :].astype(BF)


def attn_bwd(meta, q, kv, o, do, lse):
    rows, keys = q.shape[0], kv.shape[0]
    nblk = keys // BLK
    return pl.pallas_call(
        attn_bwd_kernel,
        out_shape=(struct(q.shape, BF), struct(kv.shape, BF)),
        in_specs=[SM] + [VM] * 5,
        out_specs=(VM,) * 2,
        scratch_shapes=[pltpu.SMEM((nblk,), jnp.int32), pltpu.VMEM((BLK, HEAD), F32), pltpu.VMEM((keys, HEAD), F32), pltpu.VMEM((keys, HEAD), F32)],
        compiler_params=pltpu.CompilerParams(vmem_limit_bytes=32 << 20),
        cost_estimate=pl.CostEstimate(flops=20 * rows * keys * HEAD, bytes_accessed=12 << 20, transcendentals=rows * keys),
        name="attn_bwd",
    )(meta, q, kv, o, do, lse)


def chip_members():
    d, t = lax.axis_index("dp"), lax.axis_index("tensor")
    c = lax.rem(d, 2)
    out = []
    for dt in range(8):
        for dc in range(2):
            if dt or dc:
                tt = lax.rem(t + dt, 8)
                cc = lax.rem(c + dc, 2)
                out.append((tt, cc, (d - c + cc, tt)))
    return out


def norm_rows(values):
    average = jnp.mean(values, axis=-1, keepdims=True)
    centred = values - average
    variance = jnp.mean(centred * centred, axis=-1, keepdims=True)
    inverse = lax.rsqrt(variance + EPS)
    return centred * inverse, inverse


def norm_back(grad, scaled, inverse, gain):
    e = grad * gain
    first = jnp.mean(e, axis=-1, keepdims=True)
    second = jnp.mean(e * scaled, axis=-1, keepdims=True)
    return inverse * (e - first - scaled * second)


def middle_kernel(o_ref, w_ref, x_ref, bias_ref, gain_ref, shift_ref, n_out, mid_out, own_out, mixed, asems, arecv, ss, rs):
    g = Eight("tensor")
    c = lax.rem(g.d, 2)
    members = chip_members()
    greet([m[2] for m in members])
    rows = x_ref.shape[0]
    half = o_ref.shape[0] // 2
    sems = (asems, arecv)
    head = pl.ds(pl.multiple_of((2 * g.t + c) * HEAD, HEAD), HEAD)
    local = pl.ds(pl.multiple_of(c * HEAD, HEAD), HEAD)
    copies = []
    for k, (tt, cc, device) in enumerate(members):
        take = pl.ds(pl.multiple_of(cc * half + tt * rows, rows), rows)
        copies.append(send(o_ref.at[take], mixed.at[:, head], sems, k, device))
    copies.append(send(o_ref.at[pl.ds(pl.multiple_of((1 - c) * half, half), half)], own_out.at[:, local], sems, 15, other_core()))
    mixed[:, head] = o_ref[pl.ds(pl.multiple_of(c * half + g.t * rows, rows), rows), :]
    own_out[:, local] = o_ref[pl.ds(pl.multiple_of(c * half, half), half), :]
    for copy in copies:
        copy.wait_recv()
    wide = 512
    for n in range(mid_out.shape[1] // wide):
        cols = pl.ds(n * wide, wide)
        total = None
        for t in range(8):
            term = dg(mixed[:, t * 256:(t + 1) * 256], w_ref[t, cols, :], NT)
            total = term if total is None else total + term
        mid_out[:, cols] = total + (x_ref[:, cols].astype(F32) + bias_ref[:, cols])
    scaled, _ = norm_rows(mid_out[...])
    n_out[g.index(g.r, g.p)] = (scaled * gain_ref[...] + shift_ref[...]).astype(BF)
    gather = Gather(g, n_out, (ss, rs))
    gather.start()
    gather.forward()
    gather.finish()
    for copy in copies:
        copy.wait_send()


def middle_call(o, w, x, bias, gain, shift):
    rows, width = x.shape
    return remote_call(
        middle_kernel, "middle", 3,
        (struct((8, rows, width), BF), struct((rows, width), F32), struct((o.shape[0] // 2, 2 * HEAD), BF)),
        [VM] * 6,
        [pltpu.VMEM((rows, width), BF), DMA((16,)), DMA((16,)), DMA((10,)), DMA((10,))],
        o, w, x, bias, gain, shift)


def back_kernel(part_ref, opart_ref, mid_ref, g_ref, w_ref, gain_ref, bias_ref, do_out, gm_out, sums_out, gb_out, lay_out,
                total, heads, asems, arecv, gs, gr, ls, lr, *scratch):
    g = Eight("tensor")
    c = lax.rem(g.d, 2)
    members = chip_members()
    greet([m[2] for m in members])
    rows = g_ref.shape[0]
    half = do_out.shape[0] // 2
    step = 32
    first = Scatter(g, part_ref, scratch[:7], step)
    second = Scatter(g, opart_ref, scratch[7:], step)
    first.start()
    second.start()
    first.forward()

    def keep(at, value):
        total[at, :] = value

    first.finish(keep)
    scaled, inverse = norm_rows(mid_ref[...])
    grad = total[...]
    sums_out[...] = jnp.zeros_like(sums_out)
    sums_out[0:1, :] = jnp.sum(grad * scaled, axis=0, keepdims=True)
    sums_out[1:2, :] = jnp.sum(grad, axis=0, keepdims=True)
    gm = g_ref[...].astype(F32) + norm_back(grad, scaled, inverse, gain_ref[...])
    gm_out[...] = gm
    low = gm.astype(BF)
    gb_out[g.index(g.r, g.p)] = low
    sums_out[2:3, :] = jnp.sum(low.astype(F32), axis=0, keepdims=True)
    sums_out[3:4, :] = jnp.sum(g_ref[...].astype(F32), axis=0, keepdims=True)
    for t in range(8):
        heads[:, t * 256:(t + 1) * 256] = jnp.dot(low, w_ref[t], preferred_element_type=F32).astype(BF)
    sems = (asems, arecv)
    take = pl.ds(pl.multiple_of(c * half + g.t * rows, rows), rows)
    copies = []
    for k, (tt, cc, device) in enumerate(members):
        cols = pl.ds(pl.multiple_of((2 * tt + cc) * HEAD, HEAD), HEAD)
        copies.append(send(heads.at[:, cols], do_out.at[take], sems, k, device))
    do_out[take, :] = heads[:, pl.ds(pl.multiple_of((2 * g.t + c) * HEAD, HEAD), HEAD)]
    wide = Gather(g, gb_out, (gs, gr))
    wide.start()
    second.forward()
    me = g.index(g.r, g.p)

    def layer(at, value):
        lay_out[me, at, :] = (mid_ref[at, :] + (value + bias_ref[...])).astype(BF)

    second.finish(layer)
    out = Gather(g, lay_out, (ls, lr))
    out.start()
    wide.forward()
    out.forward()
    wide.finish()
    out.finish()
    for copy in copies:
        copy.wait()


def back_call(part, opart, mid, g, w, gain, bias):
    rows, width = g.shape
    chunks = struct((8, rows, width), BF)
    return remote_call(
        back_kernel, "back", 4,
        (struct((16 * rows, HEAD), BF), struct((rows, width), F32), struct((8, width), F32), chunks, chunks),
        [VM] * 7,
        [pltpu.VMEM((rows, width), F32), pltpu.VMEM((rows, width), BF), DMA((15,)), DMA((15,)),
         DMA((10,)), DMA((10,)), DMA((10,)), DMA((10,))] + Scatter.scratch(rows, width) * 2,
        part, opart, mid, g, w, gain, bias)


def key_grads_kernel(part_ref, out_ref, *scratch):
    g = Eight("dp")
    greet(g.others())
    scatter = Scatter(g, part_ref, scratch, 128)
    scatter.start()
    scatter.forward()

    def keep(at, value):
        out_ref[at, :] = value.astype(BF)

    scatter.finish(keep)


def scatter_keys(part):
    return remote_call(
        key_grads_kernel, "key_grads", 5, struct(part.shape[1:], BF), [VM], Scatter.scratch(*part.shape[1:]), part)


def tail_kernel(dw_ref, part_ref, gm_ref, x_ref, gain_ref, dw_out, tg_out, sums_out, summed, arrived, total, mine_w,
                css, crs, ss, rs, *scratch):
    dp, g = Eight("dp"), Eight("tensor")
    c = lax.rem(g.d, 2)
    core = other_core()
    greet(dp.others() + g.others() + [core])
    csems = (css, crs)
    swap = send(part_ref.at[1 - c], arrived, csems, 0, core)
    weights = Scatter(dp, dw_ref, scratch[:7], 128)
    weights.start()
    swap.wait_recv()
    rows, width = x_ref.shape
    for t in range(8):
        @pl.loop(0, rows // 32)
        def _(n):
            at = pl.ds(pl.multiple_of(n * 32, 32), 32)
            summed[t, at, :] = (part_ref[c, t, at, :].astype(F32) + arrived[t, at, :].astype(F32)).astype(BF)
    tokens = Scatter(g, summed, scratch[7:], 32)
    tokens.start()
    weights.forward()
    tokens.forward()

    def keep(at, value):
        total[at, :] = value

    tokens.finish(keep)
    scaled, inverse = norm_rows(x_ref[...].astype(F32))
    grad = total[...]
    sums_out[...] = jnp.zeros_like(sums_out)
    sums_out[0:1, :] = jnp.sum(grad * scaled, axis=0, keepdims=True)
    sums_out[1:2, :] = jnp.sum(grad, axis=0, keepdims=True)
    tg = gm_ref[...] + norm_back(grad, scaled, inverse, gain_ref[...])
    tg_out[g.index(g.r, g.p)] = tg.astype(BF)
    gather = Gather(g, tg_out, (ss, rs))
    gather.start()

    def keep_w(at, value):
        mine_w[at, :] = value.astype(BF)

    weights.finish(keep_w)
    share = dw_out.shape[1]
    there = send(mine_w.at[pl.ds(pl.multiple_of((1 - c) * share, share), share)], dw_out.at[c], csems, 1, core)
    dw_out[c] = mine_w[pl.ds(pl.multiple_of(c * share, share), share), :]
    gather.forward()
    gather.finish()
    there.wait()
    swap.wait_send()


def tail_call(dw, part, gm, x, gain):
    rows, width = x.shape
    wr, wc = dw.shape[1:]
    return remote_call(
        tail_kernel, "tail", 6,
        (struct((2, wr // 2, wc), BF), struct((8, rows, width), BF), struct((8, width), F32)),
        [VM] * 5,
        [pltpu.VMEM((8, rows, width), BF), pltpu.VMEM((8, rows, width), BF), pltpu.VMEM((rows, width), F32), pltpu.VMEM((wr, wc), BF),
         DMA((2,)), DMA((2,)), DMA((10,)), DMA((10,))] + Scatter.scratch(wr, wc) + Scatter.scratch(rows, width),
        dw, part, gm, x, gain)


def on_device(tokens, first_gain, first_shift, query_weight, query_bias, key_weight, value_weight, value_bias,
              out_weight, out_bias, second_gain, second_shift, up_weight, up_bias, down_weight, down_bias,
              cotangent, prefix, block_order):
    own, width = tokens.shape
    d, t = lax.axis_index("dp"), lax.axis_index("tensor")
    c = lax.rem(d, 2)
    nblk = block_order.shape[0]
    rows = own // 8
    meta = jnp.concatenate([block_order % nblk, prefix, (d // 2 * 4).astype(jnp.int32).reshape(1)])
    row = lambda v: v.reshape(1, -1)

    up_all = lax.all_gather(up_weight.astype(BF), "dp", axis=0, tiled=True)
    down_all = lax.all_gather(down_weight.astype(BF).T, "dp", axis=0, tiled=True)
    out_all = lax.all_gather(lax.all_gather(out_weight.astype(BF).T, "dp", axis=0, tiled=True), "tensor", axis=0)

    scaled, _ = norm_rows(tokens.astype(F32))
    normed = (scaled * first_gain + first_shift).astype(BF)
    shards = jnp.stack([
        jnp.concatenate([w[:, h * HEAD:(h + 1) * HEAD] for w in (query_weight, key_weight, value_weight)], axis=1).astype(BF)
        for h in range(2)])
    w_all, n_all = gather_weights(shards, normed)
    w_all = w_all.reshape(width, 3 * HEAD)
    n_all = n_all.reshape(2 * own, width)
    pick = lambda v: lax.dynamic_slice_in_dim(v, c * HEAD, HEAD)
    bias = jnp.concatenate([pick(query_bias), jnp.zeros((HEAD,), F32), pick(value_bias)])
    qkv = (dg(n_all, w_all, NN) + bias).astype(BF)
    q = qkv[:, :HEAD]
    kv = gather_keys(qkv[:, HEAD:]).reshape(8 * 2 * own, 2 * HEAD)
    o, lse = attn_fwd(meta, q, kv)

    here = lambda v: lax.dynamic_slice_in_dim(v, t * rows, rows)
    x_rows, g_rows = here(tokens), here(cotangent)
    n2, mid, mixed = middle_call(o, out_all, x_rows, row(out_bias), row(second_gain), row(second_shift))
    n2 = n2.reshape(own, width)
    pre = dg(n2, up_all, NN) + up_bias
    half_erf = 0.5 + 0.5 * lax.erf(pre * math.sqrt(0.5))
    hidden = (pre * half_erf).astype(BF)
    slope = half_erf + pre * jnp.exp(-0.5 * pre * pre) * (1.0 / math.sqrt(2.0 * math.pi))
    grad_pre = (dg(cotangent, down_all, NN) * slope).astype(BF)
    gn2 = dg(grad_pre, up_all, NT).astype(BF).reshape(8, rows, width)
    out_part = dg(hidden, down_all, NT).astype(BF).reshape(8, rows, width)
    do, gm, sums, gb, layer = back_call(gn2, out_part, mid, g_rows, out_all, row(second_gain), row(down_bias))
    gb = gb.reshape(own, width)
    dw_up = dg(n2, grad_pre, TN)
    dw_down = dg(cotangent, hidden, TN)
    dw_out = dg(gb, mixed, TN)
    late = lax.psum_scatter(
        jnp.concatenate([dw_up.astype(BF), dw_down.astype(BF), dw_out.astype(BF)], axis=1), "dp", scatter_dimension=0, tiled=True)

    dq, dkv = attn_bwd(meta, q, kv, o, do, lse)
    dkv = scatter_keys(dkv.reshape(8, 2 * own, 2 * HEAD))
    dqkv = jnp.concatenate([dq, dkv], axis=1)
    dw = dg(n_all, dqkv, TN).astype(BF).reshape(8, width // 8, 3 * HEAD)
    gn1 = dg(dqkv, w_all, NT).astype(BF).reshape(2, 8, rows, width)
    dw_mine, tg, sums1 = tail_call(dw, gn1, gm, x_rows, row(first_gain))

    def slot(value, count, at):
        return lax.dynamic_update_slice_in_dim(jnp.zeros((count * value.shape[0],), F32), value, at * value.shape[0], 0)

    col = jnp.sum(dqkv.astype(F32), axis=0)
    head = 2 * t + c
    up_sum = slot(jnp.sum(grad_pre.astype(F32), axis=0), 8, t)
    vec = jnp.concatenate([
        sums[0], sums[1], sums[2], sums[3], up_sum, slot(col[:HEAD], 16, head), slot(col[2 * HEAD:], 16, head), sums1[0], sums1[1]])
    vec = lax.psum(vec, ("dp", "tensor"))
    ups = up_sum.shape[0]
    at = 4 * width
    gain2, shift2, outb, downb = (vec[i * width:(i + 1) * width] for i in range(4))
    mine = lambda start, size, index: lax.dynamic_slice_in_dim(vec, start + index * size, size)
    upb = mine(at, ups // 8, t)
    qb = mine(at + ups, 2 * HEAD, t)
    vb = mine(at + ups + width, 2 * HEAD, t)
    gain1 = vec[at + ups + 2 * width:at + ups + 3 * width]
    shift1 = vec[at + ups + 3 * width:]
    hid = up_weight.shape[1]
    pieces = [
        jnp.concatenate([dw_mine[0, :, i * HEAD:(i + 1) * HEAD], dw_mine[1, :, i * HEAD:(i + 1) * HEAD]], axis=1).astype(F32)
        for i in range(3)]
    return (
        layer.reshape(own, width),
        tg.reshape(own, width).astype(F32),
        gain1, shift1,
        pieces[0], qb, pieces[1], pieces[2], vb,
        late[:, 2 * hid:].astype(F32).T, outb,
        gain2, shift2,
        late[:, :hid].astype(F32), upb,
        late[:, hid:2 * hid].astype(F32).T, downb,
    )


def solution(mesh):
    rows, cols = P("dp", "tensor"), P("tensor", "dp")
    return jax.shard_map(
        on_device,
        mesh=mesh,
        in_specs=(
            P("dp", None), P(), P(), rows, P("tensor"), rows, rows, P("tensor"), cols, P(), P(), P(), rows, P("tensor"),
            cols, P(), P("dp", None), P(), P()),
        out_specs=(
            P("dp", None), P("dp", None), P(), P(), rows, P("tensor"), rows, rows, P("tensor"), cols, P(), P(), P(), rows,
            P("tensor"), cols, P()),
        check_vma=False,
    )
```

time: 1180 us -> 832 us (0.71)
  Pallas kernels: 0 us -> 408 us
  waiting for transfers between devices: 524 us -> 288 us
  matrix products: 208 us -> 44.5 us
  other arithmetic: 169 us -> 22.8 us
  local copies, waits for them, and re-layouts: 153 us -> 48.3 us
  loops' own time: 66 us -> 0 us
  starting transfers between devices: 39.3 us -> 0.24 us
    pallas_call x0 -> x8, Pallas kernels: none -> 408 us  [the longest x6 352 us: remote_call(): pl.pallas_call(kernel, out_shape=outs, in_specs=ins, out_specs=jax.tree.m...]
    dot_general x130 -> x10, matrix products: 208 us -> 44.5 us  [dg(): return lax.dot_general(a, b, dims, preferred_element_type=F32)]
    psum x3 -> x1, waiting for transfers between devices: 266 us -> 117 us  [on_device(): vec = lax.psum(vec, ('dp', 'tensor'))]
    reduce_scatter x1 -> x0, waiting for transfers between devices: 72.3 us -> none  [in_one_piece(): lax.psum_scatter(both, axis, scatter_dimension=dim, tiled=True)]
    another operation x51 -> x0, loops' own time: 66 us -> none  [the longest x1 21.4 us: on_device(): running, _ = lax.scan(advance, initial, block_items)]
    reduce_or x48 -> x0, other arithmetic: 58 us -> none  [advance(): jnp.any(allowed)]
    unnamed x111 -> x80, local copies, waits for them, and re-layouts: 74.9 us -> 26.3 us
    unnamed x11 -> x7, waiting for transfers between devices: 59.2 us -> 103 us
  transfers between devices with their start and end apart: 18 -> 6, of which waited for: 15 -> 5; matrix products, arithmetic and copies ran while one was open for 23% -> 8% of each run, Pallas kernels for 0% -> 20%
where the time goes in v1:
time: 832 us; the launch traced here: 828 us
  Pallas kernels  408 us (49%)
  waiting for transfers between devices  288 us (35%)
  local copies, waits for them, and re-layouts  48.3 us (6%)
  matrix products  44.5 us (5%)
  other arithmetic  22.8 us (3%)
  between operations  15.8 us (2%)
    pallas_call x6, Pallas kernels, remote_call(): pl.pallas_call(kernel, out_shape=outs, in_specs=ins, out_specs=jax.tree.m...  352 us
    psum x1, waiting for transfers between devices, on_device(): vec = lax.psum(vec, ('dp', 'tensor'))  117 us
    unnamed x7, waiting for transfers between devices  103 us
    dot_general x10, matrix products, dg(): return lax.dot_general(a, b, dims, preferred_element_type=F32)  44.5 us
    all_gather x1, waiting for transfers between devices, on_device(): lax.all_gather(out_weight.astype(BF).T, 'dp', axis=0, tiled=True)  38.9 us
    pallas_call x1, Pallas kernels, attn_bwd(): pl.pallas_call(attn_bwd_kernel, out_shape=(struct(q.shape, BF), struct(kv...  32.5 us
    unnamed x80, local copies, waits for them, and re-layouts  26.3 us
    all_gather x1, waiting for transfers between devices, on_device(): lax.all_gather(down_weight.astype(BF).T, 'dp', axis=0, tiled=True)  23.7 us
  transfers between devices with their start and end apart: 6, of which 5 were waited for; matrix products, arithmetic and copies ran while one was open for 8% of the time, Pallas kernels for 20%

profile of v1, /device:TPU:1, one launch (start us, length us, event | category | flops | bytes accessed | tf_op | source)
XLA Modules:
  0.0 827.7 jit_solution(1910594733836674181)
XLA Ops:
  7.3 1.7 convert_bitcast_fusion.4
  9.1 38.9 %all-gather.8.cloned.1.call-done = bf16[2048,256]{0,1:T(8,128)(2,1)} async-done(((bf16[128,256]{0,1:T(8,128)(2,1)}), bf16[2048,256]{0,1:T(8,128)(2,1)}) %all-gather.8.cloned.1.call-update) | async-done | bytes 1048592 | tf_op jit(solution)/shard_map/all_gather | solution.py:650
  48.0 1.8 convert_element_type.95
  49.9 0.7 convert_bitcast_fusion.2
  51.0 0.7 maximum_maximum_fusion.w_ref
  51.7 2.0 convert_reduce_fusion
  53.7 0.7 fusion.2
  54.4 2.2 fusion.5.n_ref
  56.6 32.9 %weights.1 = (bf16[8,256,384]{2,1,0:T(8,128)(2,1)}, bf16[2,512,2048]{2,1,0:T(8,128)(2,1)}) custom-call(bf16[2,128,384]{2,1,0:T(8,128)(2,1)} %maximum_maximum_fusion.w_ref, bf16[512,2048]{1,0:T(8,128)(2,1)} %fusion.5.n_ref), custom_call_target="tpu_custom_call" | custom-call | tf_op jit(solution)/shard_map/weights/pallas_call | solution.py:211
  89.5 5.0 add_convert_fusion
  94.5 0.8 slice.137.k_ref
  95.4 65.4 %keys.1 = bf16[8,1024,256]{2,1,0:T(8,128)(2,1)} custom-call(bf16[1024,256]{1,0:T(8,128)(2,1)} %slice.137.k_ref), custom_call_target="tpu_custom_call" | custom-call | tf_op jit(solution)/shard_map/keys/pallas_call | solution.py:211
  161.6 1.7 constant_dynamic-slice_fusion.1.x_ref
  163.3 0.8 constant_dynamic-slice_fusion.g_ref
  164.0 2.2 copy-done.2
  166.2 23.6 %attn_fwd.1 = (bf16[1024,128]{1,0:T(8,128)(2,1)S(1)}, f32[4,256]{1,0:T(4,128)S(1)}) custom-call(s32[34]{0:T(128)S(1)} %pad_add_fusion.meta, bf16[1024,128]{1,0:T(8,128)(2,1)S(1)} %slice.136.q_ref, bf16[8192,256]{1,0:T(8,128)(2,1)S(1)} %bitcast.78), custom_call_target="tpu_custom_call" | custom-call | flops 8589934592 | bytes 6291456 | tf_op jit(solution)/shard_map/attn_fwd/pallas_call | solution.py:332
  189.8 0.7 copy-done.5
  190.5 5.9 all-gather.12.cloned.1.call-done
  196.5 12.0 %copy.38 = bf16[16384,256]{1,0:T(8,128)(2,1)} copy(bf16[16384,256]{0,1:T(8,128)(2,1)} %all-gather.12.cloned.1.call-done) | data formatting | bytes 16777216 | tf_op jit(solution)/shard_map/all_gather | solution.py:650
  208.4 45.7 %middle.1 = (bf16[8,64,2048]{2,1,0:T(8,128)(2,1)}, f32[64,2048]{1,0:T(8,128)}, bf16[512,256]{1,0:T(8,128)(2,1)}) custom-call(bf16[1024,128]{1,0:T(8,128)(2,1)} %copy-done.5, bf16[8,2048,256]{2,1,0:T(8,128)(2,1)} %bitcast.81, bf16[64,2048]{1,0:T(8,128)(2,1)} %constant_dynamic-slice_fusion.1.x_ref, f32[1,2048]{1,0:T(1,128)} %bitcast.97, f32[1,2048]{1,0:T(1,128)} %bitcast.88, ...), custom_call_target="tpu_custom_call" | custom-call | tf_op jit(solution)/shard_map/middle/pallas_call | solution.py:211
  254.2 5.3 fusion.20
  259.6 1.3 copy-done.31
  260.9 4.5 convert_bitcast_fusion
  265.4 23.7 %all-gather.6.cloned.1.call-done = bf16[2048,1024]{0,1:T(8,128)(2,1)} async-done(((bf16[128,1024]{0,1:T(8,128)(2,1)}), bf16[2048,1024]{0,1:T(8,128)(2,1)}) %all-gather.6.cloned.1.call-update) | async-done | bytes 4194320 | tf_op jit(solution)/shard_map/all_gather | solution.py:649
  289.1 6.1 convert_reduce_fusion.1
  295.2 4.5 convolution_convert_fusion.1
  299.7 3.7 convolution_convert_fusion.3
  303.4 3.7 convolution_convert_fusion.2
  307.1 106.9 %back.1 = (bf16[1024,128]{1,0:T(8,128)(2,1)}, f32[64,2048]{1,0:T(8,128)}, f32[8,2048]{1,0:T(8,128)}, bf16[8,64,2048]{2,1,0:T(8,128)(2,1)}, bf16[8,64,2048]{2,1,0:T(8,128)(2,1)}) custom-call(bf16[8,64,2048]{2,1,0:T(8,128)(2,1)} %bitcast.84, bf16[8,64,2048]{2,1,0:T(8,128)(2,1)} %bitcast.85, f32[64,2048]{1,0:T(8,128)} %get-tuple-element.38.mid_ref, ...), custom_call_target="tpu_custom_call" | custom-call | tf_op jit(solution)/shard_map/back/pallas_call | solution.py:211
  414.1 0.9 copy-done.7
  415.0 32.5 %attn_bwd.1 = (bf16[1024,128]{1,0:T(8,128)(2,1)S(1)}, bf16[8192,256]{1,0:T(8,128)(2,1)S(1)}) custom-call(s32[34]{0:T(128)S(1)} %pad_add_fusion.meta, bf16[1024,128]{1,0:T(8,128)(2,1)S(1)} %slice.136.q_ref, bf16[8192,256]{1,0:T(8,128)(2,1)S(1)} %bitcast.79, bf16[1024,128]{1,0:T(8,128)(2,1)S(1)} %copy-done.6, bf16[1024,128]{1,0:T(8,128)(2,1)S(1)} %copy-done.7, ...), custom_call_target="tpu_custom_call" | custom-call | flops 21474836480 | bytes 12582912 | tf_op jit(solution)/shard_map/attn_bwd/pallas_call | solution.py:401
  447.6 2.0 copy-done.4
  449.6 42.0 %key_grads.1 = bf16[1024,256]{1,0:T(8,128)(2,1)} custom-call(bf16[8,1024,256]{2,1,0:T(8,128)(2,1)} %bitcast.80), custom_call_target="tpu_custom_call" | custom-call | tf_op jit(solution)/shard_map/key_grads/pallas_call | solution.py:211
  491.6 5.6 convolution_convert_fusion
  497.2 3.6 convolution_convert_fusion.4
  500.8 0.2 convert_reduce_fusion.2
  501.0 0.1 slice_dynamic-update-slice_fusion.1
  501.1 0.1 slice_dynamic-update-slice_fusion
  501.2 59.1 %tail.1 = (bf16[2,128,384]{2,1,0:T(8,128)(2,1)}, bf16[8,64,2048]{2,1,0:T(8,128)(2,1)}, f32[8,2048]{1,0:T(8,128)}) custom-call(bf16[8,256,384]{2,1,0:T(8,128)(2,1)} %bitcast.87, bf16[2,8,64,2048]{3,2,1,0:T(8,128)(2,1)} %bitcast.83, f32[64,2048]{1,0:T(8,128)} %get-tuple-element.44.gm_ref, bf16[64,2048]{1,0:T(8,128)(2,1)} %constant_dynamic-slice_fusion.1.x_ref, ...), custom_call_target="tpu_custom_call" | custom-call | tf_op jit(solution)/shard_map/tail/pallas_call | solution.py:211
  560.3 0.9 fusion.18
  561.3 0.3 dynamic_update_slice.9
  561.7 0.6 copy-done.17
  562.4 2.5 convolution_convert_fusion.5
  564.9 0.3 copy-done.9
  565.2 6.6 pad_maximum_fusion
  571.8 12.4 %copy.40 = bf16[2048,2304]{1,0:T(8,128)(2,1)} copy(bf16[2048,2304]{0,1:T(8,128)(2,1)} %pad_maximum_fusion) | data formatting | bytes 18874368
  584.2 0.9 copy-done.13
  585.2 0.7 maximum_convert_fusion.2
  585.8 0.7 maximum_convert_fusion.1
  586.5 0.7 maximum_convert_fusion
  587.2 2.7 bitcast_convert_fusion
  589.8 116.8 %all-reduce.2.cloned.1.call-done = f32[24576]{0:T(1024)} async-done(((f32[24576]{0:T(1024)}), f32[24576]{0:T(1024)}) %all-reduce.2.cloned.1.call-update) | async-done | bytes 98320 | tf_op jit(solution)/shard_map/psum | solution.py:701
  706.6 1.3 dynamic_slice.27
  707.9 1.3 fusion.17
  709.2 1.4 fusion.16
  710.6 102.5 %reduce-scatter.4.cloned.1.call-done = bf16[128,2304]{1,0:T(8,128)(2,1)} async-done(((bf16[2048,2304]{1,0:T(8,128)(2,1)}), bf16[128,2304]{1,0:T(8,128)(2,1)}) %reduce-scatter.4.cloned.1.call-update) | async-done | bytes 589840
  813.1 1.1 fusion.15
  814.2 0.2 copy.44
  814.4 0.8 convert_bitcast_fusion.1
  815.2 0.2 copy.43
  815.4 0.9 copy.39
  816.3 0.1 copy.42
  816.4 0.7 convert_bitcast_fusion.3
  817.1 3.3 copy.59
  (101 shorter events, 0.9 us)
Async XLA Ops:
  7.2 156.1 %copy-start = (bf16[512,2048]{1,0:T(8,128)(2,1)S(1)}, bf16[512,2048]{1,0:T(8,128)(2,1)}, u32[]{:S(2)}) copy-start(bf16[512,2048]{1,0:T(8,128)(2,1)} %param.35) | copy-start | bytes 6291460
  7.2 42.7 %copy-start.12 = (f32[1024,128]{1,0:T(8,128)S(1)}, f32[1024,128]{1,0:T(8,128)}, u32[]{:S(2)}) copy-start(f32[1024,128]{1,0:T(8,128)} %param.33) | copy-start | bytes 1572868
  7.2 43.5 %copy-start.28 = (f32[256]{0:T(256)S(1)}, f32[256]{0:T(256)}, u32[]{:S(2)}) copy-start(f32[256]{0:T(256)} %param.23) | copy-start | bytes 3076
  7.2 43.6 %copy-start.29 = (f32[256]{0:T(256)S(1)}, f32[256]{0:T(256)}, u32[]{:S(2)}) copy-start(f32[256]{0:T(256)} %param.26) | copy-start | bytes 3076
  7.2 43.7 %copy-start.14 = (f32[128,256]{1,0:T(8,128)S(1)}, f32[128,256]{1,0:T(8,128)}, u32[]{:S(2)}) copy-start(f32[128,256]{1,0:T(8,128)} %param.24) | copy-start | bytes 393220
  7.2 43.7 %copy-start.15 = (f32[128,256]{1,0:T(8,128)S(1)}, f32[128,256]{1,0:T(8,128)}, u32[]{:S(2)}) copy-start(f32[128,256]{1,0:T(8,128)} %param.25) | copy-start | bytes 393220
  7.3 43.7 %copy-start.16 = (f32[128,256]{1,0:T(8,128)S(1)}, f32[128,256]{1,0:T(8,128)}, u32[]{:S(2)}) copy-start(f32[128,256]{1,0:T(8,128)} %param.22) | copy-start | bytes 393220
  7.3 40.7 %all-gather.8.cloned.1.call-start = ((), (), s32[]{:S(2)}) async-start(), calls=%async_computation.2 | async-start | bytes 1114112 | tf_op jit(solution)/shard_map/all_gather | solution.py:650
  9.0 187.4 %all-gather.12.cloned.1.call-start = ((), (), s32[]{:S(2)}) async-start(), calls=%async_computation.5 | async-start | bytes 9437184 | tf_op jit(solution)/shard_map/all_gather | solution.py:650
  48.0 206.2 %all-gather.10.cloned.1.call-start = ((), (), s32[]{:S(2)}) async-start(), calls=%async_computation.3 | async-start | bytes 4456448 | tf_op jit(solution)/shard_map/all_gather | solution.py:648
  49.8 239.3 %all-gather.6.cloned.1.call-start = ((), (), s32[]{:S(2)}) async-start(), calls=%async_computation.1 | async-start | bytes 4456448 | tf_op jit(solution)/shard_map/all_gather | solution.py:649
  50.7 656.0 %all-reduce.2.cloned.1.call-start = ((), (), s32[]{:S(2)}) async-start(), calls=%async_computation.4 | async-start | bytes 196608 | tf_op jit(solution)/shard_map/psum | solution.py:701
  50.7 3.0 copy-start.8
  51.7 2.7 copy-start.18
  51.7 2.7 copy-start.20
  95.4 66.1 %copy-start.30 = (s32[32]{0:T(128)S(1)}, s32[32]{0:T(128)}, u32[]{:S(2)}) copy-start(s32[32]{0:T(128)} %param.37) | copy-start | bytes 388
  164.0 2.2 copy-start.2
  189.8 0.7 copy-start.5
  254.2 6.7 copy-start.27
  259.6 1.3 copy-start.31
  289.1 6.1 copy-start.24
  295.2 4.5 copy-start.21
  299.7 3.7 copy-start.22
  299.7 3.7 copy-start.32
  307.1 107.0 %copy-start.3 = (bf16[8,1024,256]{2,1,0:T(8,128)(2,1)S(1)}, bf16[8,1024,256]{2,1,0:T(8,128)(2,1)}, u32[]{:S(2)}) copy-start(bf16[8,1024,256]{2,1,0:T(8,128)(2,1)} %keys.1) | copy-start | bytes 12582916
  307.1 107.0 %copy-start.6 = (bf16[1024,128]{1,0:T(8,128)(2,1)S(1)}, bf16[1024,128]{1,0:T(8,128)(2,1)}, u32[]{:S(2)}) copy-start(bf16[1024,128]{1,0:T(8,128)(2,1)} %copy-done.5) | copy-start | bytes 786436
  414.1 1.0 copy-start.7
  447.6 2.0 copy-start.4
  449.6 42.0 %copy-start.25 = (bf16[8,256,384]{2,1,0:T(8,128)(2,1)S(1)}, bf16[8,256,384]{2,1,0:T(8,128)(2,1)}, u32[]{:S(2)}) copy-start(bf16[8,256,384]{2,1,0:T(8,128)(2,1)} %get-tuple-element.35) | copy-start | bytes 4718596
  491.6 5.6 copy-start.11
  491.6 5.6 copy-start.23
  497.2 3.8 copy-start.19
  501.2 61.1 %copy-start.26 = (bf16[512,256]{1,0:T(8,128)(2,1)S(1)}, bf16[512,256]{1,0:T(8,128)(2,1)}, u32[]{:S(2)}) copy-start(bf16[512,256]{1,0:T(8,128)(2,1)} %get-tuple-element.50) | copy-start | bytes 786436
  561.6 0.6 copy-start.17
  562.3 250.8 %reduce-scatter.4.cloned.1.call-start = ((), (), s32[]{:S(2)}) async-start(), calls=%async_computation.6 | async-start | bytes 10027008
  562.4 2.8 copy-start.9
  584.2 0.9 copy-start.13
  584.2 3.0 copy-start.10
  813.1 3.2 slice-start
  817.1 3.3 copy-start.1
Sparse Core Ops, SparseCore 0:
  10.3 37.6 all-gather.7
  50.3 146.1 all-gather.11
  198.7 39.5 all-gather.9
  239.8 49.3 all-gather.5
  562.4 144.1 all-reduce.1
  709.0 104.0 reduce-scatter.3

commit v2 on v1

v2 whole, which is shorter than its diff:
```python
import functools
import math

import jax
import jax.numpy as jnp
from jax import lax
from jax.experimental import pallas as pl
from jax.experimental.pallas import tpu as pltpu
from jax.sharding import PartitionSpec as P

HEAD = 128
BLK = 256
GRP = 4
RING = 4
EPS = 1e-05
NEG = -(2.0 ** 100)
LOG2E = math.log2(math.e)
SCALE = 1.0 / math.sqrt(HEAD)
C1 = LOG2E * SCALE
NN = (((1,), (0,)), ((), ()))
NT = (((1,), (1,)), ((), ()))
TN = (((0,), (0,)), ((), ()))
MESH = pl.DeviceIdType.MESH
VM = pl.BlockSpec(memory_space=pltpu.VMEM)
SM = pl.BlockSpec(memory_space=pltpu.SMEM)
BF = jnp.bfloat16
F32 = jnp.float32
DMA = pltpu.SemaphoreType.DMA


def dg(a, b, dims):
    return lax.dot_general(a, b, dims, preferred_element_type=F32)


def struct(shape, dtype):
    return jax.ShapeDtypeStruct(shape, dtype)


class Eight:
    def __init__(self, axis):
        d, t = lax.axis_index("dp"), lax.axis_index("tensor")
        self.axis, self.d, self.t = axis, d, t
        if axis == "dp":
            self.r, self.p = d // 4, lax.rem(d // 2, 2)
        else:
            self.r, self.p = lax.rem(t, 4), t // 4

    def ring(self, i):
        return lax.rem(self.r + i, RING)

    def index(self, r, p):
        return r * 2 + p if self.axis == "dp" else p * 4 + r

    def device(self, r, p):
        if self.axis == "dp":
            return ((r * 2 + p) * 2 + lax.rem(self.d, 2), self.t)
        return (self.d, p * 4 + r)

    def others(self):
        return [self.device(self.ring(i), self.p) for i in (1, 2, 3)] + [self.device(self.r, 1 - self.p)]


def other_core():
    d = lax.axis_index("dp")
    return (d + 1 - 2 * lax.rem(d, 2), lax.axis_index("tensor"))


def greet(devices):
    barrier = pltpu.get_barrier_semaphore()
    for device in devices:
        pl.semaphore_signal(barrier, inc=1, device_id=device, device_id_type=MESH)
    pl.semaphore_wait(barrier, len(devices))


def send(src, dst, sems, k, device):
    copy = pltpu.make_async_remote_copy(
        src_ref=src, dst_ref=dst, send_sem=sems[0].at[k], recv_sem=sems[1].at[k],
        device_id=device, device_id_type=MESH)
    copy.start()
    return copy


def split_at(rows):
    return max(16, int(rows * 0.4) // 16 * 16)


def copy_of(src, dst, sems, k, device):
    return pltpu.make_async_remote_copy(
        src_ref=src, dst_ref=dst, send_sem=sems[0].at[k], recv_sem=sems[1].at[k],
        device_id=device, device_id_type=MESH)


def send(src, dst, sems, k, device):
    copy = copy_of(src, dst, sems, k, device)
    copy.start()
    return copy


class Gather:
    def __init__(self, group, place, rows, sems, twin=None, twin_sems=None, twin_own=True):
        self.g, self.place, self.sems = group, place, sems
        self.twin, self.twin_sems, self.twin_own = twin, twin_sems, twin_own
        cut = split_at(rows)
        self.low, self.high = pl.ds(0, cut), pl.ds(cut, rows - cut)

    @staticmethod
    def scratch(twin=False):
        return [DMA((10,)), DMA((10,))] + ([DMA((8,)), DMA((8,))] if twin else [])

    def near(self, i):
        g = self.g
        return self.place(g.index(g.ring(RING - i), g.p))

    def far(self, i):
        g = self.g
        return self.place(g.index(g.ring(RING - i), 1 - g.p))

    def first(self, i):
        g = self.g
        own = self.place(g.index(g.r, g.p))
        return copy_of(own, own, self.sems, i, g.device(g.ring(i), g.p))

    def first_pair(self):
        g = self.g
        own = self.place(g.index(g.r, g.p))
        return copy_of(own, own, self.sems, 0, g.device(g.r, 1 - g.p))

    def second_a(self, i):
        g = self.g
        part = self.place(g.index(g.r, 1 - g.p)).at[self.low]
        return copy_of(part, part, self.sems, 3 + i, g.device(g.ring(i), g.p))

    def second_b(self, i):
        g = self.g
        part = self.near(i).at[self.high]
        return copy_of(part, part, self.sems, 6 + i, g.device(g.r, 1 - g.p))

    def over(self, ref, k):
        return copy_of(ref, ref, self.twin_sems, k, self.twin)

    def start(self):
        g = self.g
        self.first_pair().start()
        for i in (1, 2, 3):
            self.first(i).start()
        if self.twin is not None and self.twin_own:
            self.over(self.place(g.index(g.r, g.p)), 0).start()

    def forward_pair(self):
        g = self.g
        self.first_pair().wait_recv()
        for i in (1, 2, 3):
            self.second_a(i).start()
        if self.twin is not None:
            self.over(self.place(g.index(g.r, 1 - g.p)), 1).start()

    def forward_near(self, i):
        self.first(i).wait_recv()
        self.second_b(i).start()
        if self.twin is not None:
            self.over(self.near(i), 1 + i).start()

    def forward(self):
        self.forward_pair()
        for i in (1, 2, 3):
            self.forward_near(i)

    def arrive_far(self, i):
        self.second_a(i).wait_recv()
        self.second_b(i).wait_recv()
        if self.twin is not None:
            self.over(self.far(i), 4 + i).start()

    def settle(self):
        g = self.g
        self.first_pair().wait_send()
        for i in (1, 2, 3):
            self.first(i).wait_send()
            self.second_a(i).wait_send()
            self.second_b(i).wait_send()
        if self.twin is not None:
            own = self.place(g.index(g.r, g.p))
            for k in range(0 if self.twin_own else 1, 8):
                self.over(own, k).wait()

    def finish(self):
        for i in (1, 2, 3):
            self.arrive_far(i)
        self.settle()


class Scatter:
    @staticmethod
    def scratch(rows, width):
        cut = split_at(rows)
        return [
            pltpu.VMEM((3, cut, width), BF), pltpu.VMEM((3, rows - cut, width), BF),
            pltpu.VMEM((4, rows, width), BF), pltpu.VMEM((cut, width), BF),
            pltpu.VMEM((3, rows - cut, width), BF), DMA((14,)), DMA((14,))]

    def __init__(self, group, part, rows, scratch, step):
        self.g, self.part, self.step = group, part, step
        self.at_a, self.at_b, self.last, self.sum_a, self.sum_b = scratch[:5]
        self.sems = scratch[5:]
        self.rows = rows
        self.cut = split_at(rows)
        self.low, self.high = pl.ds(0, self.cut), pl.ds(self.cut, rows - self.cut)

    def pair(self):
        return self.g.device(self.g.r, 1 - self.g.p)

    def ring(self, i):
        return self.g.device(self.g.ring(i), self.g.p)

    def far_part(self, i):
        return self.part(self.g.index(self.g.ring(i), 1 - self.g.p))

    def near_part(self, i):
        return self.part(self.g.index(self.g.ring(i), self.g.p))

    def pair_part(self):
        return self.part(self.g.index(self.g.r, 1 - self.g.p))

    def far_a(self, i):
        return copy_of(self.far_part(i).at[self.low], self.at_a.at[i - 1], self.sems, i - 1, self.ring(i))

    def far_b(self, i):
        return copy_of(self.far_part(i).at[self.high], self.at_b.at[i - 1], self.sems, 2 + i, self.pair())

    def near_own(self, i):
        return copy_of(self.near_part(i).at[self.low], self.last.at[i, self.low], self.sems, 6 + i, self.ring(i))

    def near_sum(self, i):
        return copy_of(self.sum_b.at[i - 1], self.last.at[i, self.high], self.sems, 9 + i, self.ring(i))

    def pair_own(self):
        return copy_of(self.pair_part().at[self.high], self.last.at[0, self.high], self.sems, 6, self.pair())

    def pair_sum(self):
        return copy_of(self.sum_a, self.last.at[0, self.low], self.sems, 13, self.pair())

    def by_rows(self, rows, body):
        step = self.step
        count = rows // step

        @pl.loop(0, count)
        def _(n):
            body(pl.multiple_of(n * step, step), step)

        if rows % step:
            body(count * step, rows % step)

    def send_far(self, i):
        self.far_b(i).start()
        self.far_a(i).start()

    def send_near(self, i):
        self.near_own(i).start()

    def add_near(self, i):
        self.far_b(i).wait_recv()
        mine = self.near_part(i)

        def add(at, n):
            rows = pl.ds(at, n)
            total = mine[pl.ds(self.cut + at, n), :].astype(F32) + self.at_b[i - 1, rows, :].astype(F32)
            self.sum_b[i - 1, rows, :] = total.astype(BF)

        self.by_rows(self.rows - self.cut, add)
        self.near_sum(i).start()

    def send_pair(self):
        self.pair_own().start()

    def add_pair(self):
        for i in (1, 2, 3):
            self.far_a(i).wait_recv()
        mine = self.pair_part()

        def add(at, n):
            rows = pl.ds(at, n)
            total = mine[rows, :].astype(F32)
            for i in range(3):
                total += self.at_a[i, rows, :].astype(F32)
            self.sum_a[rows, :] = total.astype(BF)

        self.by_rows(self.cut, add)
        self.pair_sum().start()

    def start(self):
        for i in (1, 2, 3):
            self.send_far(i)
        for i in (1, 2, 3):
            self.send_near(i)
        self.send_pair()

    def forward(self):
        for i in (1, 2, 3):
            self.add_near(i)
        self.add_pair()

    def finish(self, store):
        g = self.g
        self.pair_own().wait_recv()
        self.pair_sum().wait_recv()
        for i in (1, 2, 3):
            self.near_own(i).wait_recv()
            self.near_sum(i).wait_recv()
        mine = self.part(g.index(g.r, g.p))

        def add(at, n):
            rows = pl.ds(at, n)
            total = mine[rows, :].astype(F32)
            for i in range(4):
                total += self.last[i, rows, :].astype(F32)
            store(rows, total)

        self.by_rows(self.rows, add)
        self.pair_own().wait_send()
        self.pair_sum().wait_send()
        for i in (1, 2, 3):
            self.far_a(i).wait_send()
            self.far_b(i).wait_send()
            self.near_own(i).wait_send()
            self.near_sum(i).wait_send()


class CoreScatter:
    @staticmethod
    def scratch(rows, width):
        return [pltpu.VMEM((8, rows, width), BF), pltpu.VMEM((8, rows, width), BF), DMA((1,)), DMA((1,))] + Scatter.scratch(rows, width)

    def __init__(self, group, part, scratch, step):
        self.part, self.arrived, self.added = part, scratch[0], scratch[1]
        self.c = lax.rem(group.d, 2)
        self.sems = scratch[2:4]
        self.step = step
        self.inner = Scatter(group, lambda m: self.added.at[m], part.shape[2], scratch[4:], step)

    def swap(self):
        return copy_of(self.part.at[:, 1 - self.c], self.arrived, self.sems, 0, other_core())

    def start(self):
        self.swap().start()

    def add(self):
        self.swap().wait_recv()
        rows, step = self.part.shape[2], self.step

        @pl.loop(0, 8)
        def _(m):
            @pl.loop(0, rows // step)
            def _(n):
                at = pl.ds(pl.multiple_of(n * step, step), step)
                self.added[m, at, :] = (self.part[m, self.c, at, :].astype(F32) + self.arrived[m, at, :].astype(F32)).astype(BF)

        self.inner.start()

    def forward(self):
        self.inner.forward()

    def finish(self, store):
        self.inner.finish(store)
        self.swap().wait_send()


def remote_call(kernel, name, cid, outs, ins, scratch, *args, out_specs=None):
    return pl.pallas_call(
        kernel, out_shape=outs, in_specs=ins,
        out_specs=jax.tree.map(lambda _: VM, outs) if out_specs is None else out_specs,
        scratch_shapes=scratch, name=name,
        compiler_params=pltpu.CompilerParams(collective_id=cid, has_side_effects=True, vmem_limit_bytes=58 << 20),
    )(*args)


def weights_kernel(w_ref, n_ref, w_out, n_out, css, crs, *sems):
    g = Eight("dp")
    c = lax.rem(g.d, 2)
    core = other_core()
    greet(g.others() + [core])
    me = g.index(g.r, g.p)
    rows = w_ref.shape[1]
    csems = (css, crs)
    mine = pl.ds(pl.multiple_of(c * rows, rows), rows)
    swap = send(w_ref.at[1 - c], w_out.at[me, mine], csems, 0, core)
    norm = send(n_ref, n_out.at[c], csems, 1, core)
    w_out[me, mine, :] = w_ref[c]
    swap.wait_recv()
    gather = Gather(g, lambda m: w_out.at[m], 2 * rows, sems)
    gather.start()
    n_out[c] = n_ref[...]
    gather.forward()
    gather.finish()
    norm.wait()
    swap.wait_send()


def gather_weights(w, n):
    rows, width = w.shape[1:]
    return remote_call(
        weights_kernel, "weights", 1,
        (struct((8, 2 * rows, width), BF), struct((2, *n.shape), BF)), [VM, VM],
        [DMA((2,)), DMA((2,))] + Gather.scratch(), w, n)


def augment(meta, lanes_ref, q_ref, qa_ref, kx_ref):
    rows = q_ref.shape[0]
    nblk = kx_ref.shape[0] // BLK
    prefix = meta[nblk]
    for a in range(rows // BLK):
        at = slice(a * BLK, (a + 1) * BLK)
        hidden = jnp.where(lanes_ref[...] > meta[meta_first(meta, nblk) + a], NEG, 0.0)
        qa_ref[at, :HEAD] = q_ref[at, :]
        qa_ref[at, HEAD:] = jnp.broadcast_to(hidden, (BLK, HEAD)).astype(BF)
    lane = lax.broadcasted_iota(jnp.int32, (BLK, HEAD), 1)
    inside = lax.broadcasted_iota(jnp.int32, (BLK, HEAD), 0)

    @pl.loop(0, nblk)
    def _(b):
        late = (lane == b) & (inside >= prefix - meta[b] * BLK)
        kx_ref[pl.ds(pl.multiple_of(b * BLK, BLK), BLK), :] = jnp.where(late, 1.0, 0.0).astype(BF)


def meta_first(meta, nblk):
    return lax.axis_index("dp") // 2 * 4


def attend_kernel(meta, lanes_ref, q_ref, k_ref, out_ref, up_ref, kv_out, o_ref, lse_ref, out_all, up_all,
                  qa_ref, kx_ref, m_ref, acc_ref, lsem, *sems):
    g, gt = Eight("dp"), Eight("tensor")
    c = lax.rem(g.d, 2)
    core = other_core()
    me = g.index(g.r, g.p)
    rows = q_ref.shape[0]
    nblk = kx_ref.shape[0] // BLK
    per = rows // BLK
    shard = out_ref.shape[0]
    half = out_all.shape[1] // 2
    greet(g.others() + gt.others() + [core])
    out_place = lambda m: out_all.at[gt.t, pl.ds(pl.multiple_of((m * 2 + c) * shard, shard), shard)]
    up_place = lambda m: up_all.at[pl.ds(pl.multiple_of((m * 2 + c) * shard, shard), shard)]
    half_place = lambda m: out_all.at[m, pl.ds(pl.multiple_of(c * half, half), half)]
    keys = Gather(g, lambda m: kv_out.at[m], rows, sems[:2])
    outs = Gather(g, out_place, shard, sems[2:4], core, sems[4:6])
    ups = Gather(g, up_place, shard, sems[6:8], core, sems[8:10])
    wide = Gather(gt, half_place, half, sems[10:12], core, sems[12:14], twin_own=False)
    local = [pltpu.make_async_copy(out_ref, out_place(me), lsem.at[0]), pltpu.make_async_copy(up_ref, up_place(me), lsem.at[1])]
    for copy in local:
        copy.start()
    kv_out[me] = k_ref[...]
    keys.start()
    for copy in local:
        copy.wait()
    outs.start()
    augment(meta, lanes_ref, q_ref, qa_ref, kx_ref)
    m_ref[...] = jnp.full_like(m_ref, -1e30)
    acc_ref[...] = jnp.zeros_like(acc_ref)
    ones = jnp.ones((BLK, HEAD), BF)
    prefix = meta[nblk]

    def attend(chunk, own):
        @pl.loop(0, per)
        def _(a):
            mine = pl.ds(pl.multiple_of(a * BLK, BLK), BLK)
            q = qa_ref[mine, :]
            ss, vs = [], []
            for i in range(per):
                at = pl.ds(pl.multiple_of(chunk * rows + i * BLK, BLK), BLK)
                ss.append(dg(q, jnp.concatenate([kv_out[chunk, i * BLK:(i + 1) * BLK, :HEAD], kx_ref[at, :]], axis=1), NT))
                vs.append(jnp.concatenate([kv_out[chunk, i * BLK:(i + 1) * BLK, HEAD:], ones], axis=1))
            if own:
                edge = prefix - 1 - meta[meta_first(meta, nblk) + a] * BLK
                lim = jnp.maximum(lax.broadcasted_iota(jnp.int32, (BLK, BLK), 0), edge)
                key = lax.broadcasted_iota(jnp.int32, (BLK, BLK), 1)
                for i in range(per):
                    ss[i] = jnp.where(key <= jnp.where(a == i, lim, BLK), ss[i], NEG)
            top = ss[0]
            for s in ss[1:]:
                top = jnp.maximum(top, s)
            old = m_ref[mine, :1]
            new = jnp.maximum(old, jnp.max(top, axis=1, keepdims=True) * C1)
            alpha = jnp.exp2(old - new)
            add = None
            for s, v in zip(ss, vs):
                t = jnp.dot(jnp.exp2(s * C1 - new).astype(BF), v, preferred_element_type=F32)
                add = t if add is None else add + t
            acc_ref[mine, :] = acc_ref[mine, :] * alpha + add
            m_ref[mine, :] = jnp.broadcast_to(new, (BLK, HEAD))

    attend(me, True)
    keys.forward_pair()
    outs.forward()
    attend(g.index(g.r, 1 - g.p), False)
    outs.finish()
    wide.start()

    @pl.loop(1, RING)
    def _(i):
        keys.forward_near(i)
        attend(g.index(g.ring(RING - i), g.p), False)

    ups.start()
    wide.forward()

    @pl.loop(1, RING)
    def _(i):
        keys.arrive_far(i)
        attend(g.index(g.ring(RING - i), 1 - g.p), False)

    for a in range(per):
        at = slice(a * BLK, (a + 1) * BLK)
        total = acc_ref[at, HEAD:]
        o_ref[at, :] = (acc_ref[at, :HEAD] / total).astype(BF)
        lse_ref[a:a + 1, :] = jnp.transpose(m_ref[at, :] + jnp.log2(total))[:1, :]
    ups.forward()
    wide.finish()
    ups.finish()
    keys.settle()


def attend_call(meta, lanes, q, kv, out_w, up_w):
    rows = q.shape[0]
    shard, hid = up_w.shape
    hbm = pl.BlockSpec(memory_space=pl.ANY)
    return remote_call(
        attend_kernel, "attend", 2,
        (struct((8, *kv.shape), BF), struct((rows, HEAD), BF), struct((rows // BLK, BLK), F32),
         struct((8, 16 * shard, out_w.shape[1]), BF), struct((16 * shard, hid), BF)),
        [SM, VM, VM, VM, hbm, hbm],
        [pltpu.VMEM((rows, 2 * HEAD), BF), pltpu.VMEM((8 * rows, HEAD), BF), pltpu.VMEM((rows, HEAD), F32), pltpu.VMEM((rows, 2 * HEAD), F32),
         DMA((2,))] + Gather.scratch() + Gather.scratch(True) * 3,
        meta, lanes, q, kv, out_w, up_w, out_specs=(VM, VM, VM, hbm, hbm))


def attend_back_kernel(meta, lanes_ref, q_ref, kv_ref, o_ref, do_ref, lse_ref, opart_ref, gbr_ref, mid_ref, bias_ref, dup_ref,
                       dq_ref, dkv_out, lay_out, gb_out, dup_out,
                       qa_ref, kx_ref, part, delta_ref, dq_acc, dk_acc, dv_acc, *scratch):
    g, gt = Eight("dp"), Eight("tensor")
    core = other_core()
    me = g.index(g.r, g.p)
    rows = q_ref.shape[0]
    nblk = kx_ref.shape[0] // BLK
    per = rows // BLK
    greet(g.others() + gt.others() + [core])
    keys = Scatter(g, lambda m: part.at[m], rows, scratch[:7], 128)
    outs = Scatter(gt, lambda m: opart_ref.at[m], opart_ref.shape[1], scratch[7:14], 32)
    ups = CoreScatter(g, dup_ref, scratch[14:25], 32)
    wide = Gather(gt, lambda m: gb_out.at[m], gb_out.shape[1], scratch[25:27])
    layer = Gather(gt, lambda m: lay_out.at[m], lay_out.shape[1], scratch[27:29])
    ups.start()
    outs.start()
    mine_t = gt.index(gt.r, gt.p)
    gb_out[mine_t] = gbr_ref[...]
    wide.start()
    augment(meta, lanes_ref, q_ref, qa_ref, kx_ref)
    for a in range(per):
        at = slice(a * BLK, (a + 1) * BLK)
        prod = do_ref[at, :].astype(F32) * o_ref[at, :].astype(F32)
        delta_ref[0:1, at] = jnp.sum(jnp.transpose(prod), axis=0, keepdims=True)
        delta_ref[1:2, at] = lse_ref[a:a + 1, :]
    dq_acc[...] = jnp.zeros_like(dq_acc)
    prefix = meta[nblk]

    def attend(chunk, own):
        @pl.loop(0, per)
        def _(i):
            at_k = pl.ds(pl.multiple_of(i * BLK, BLK), BLK)
            at_x = pl.ds(pl.multiple_of(chunk * rows + i * BLK, BLK), BLK)
            k = kv_ref[chunk, at_k, :HEAD]
            v = kv_ref[chunk, at_k, HEAD:]
            kk = jnp.concatenate([k, kx_ref[at_x, :]], axis=1)
            dk = dv = None
            for a in range(per):
                at_q = slice(a * BLK, (a + 1) * BLK)
                q = q_ref[at_q, :]
                do = do_ref[at_q, :]
                p = jnp.exp2(dg(kk, qa_ref[at_q, :], NT) * C1 - delta_ref[1:2, at_q])
                if own:
                    edge = prefix - 1 - meta[meta_first(meta, nblk) + a] * BLK
                    lim = jnp.maximum(lax.broadcasted_iota(jnp.int32, (BLK, BLK), 1), edge)
                    key = lax.broadcasted_iota(jnp.int32, (BLK, BLK), 0)
                    p = jnp.where(key <= jnp.where(i == a, lim, BLK), p, 0.0)
                ds = (p * (dg(v, do, NT) - delta_ref[0:1, at_q])).astype(BF)
                tv = jnp.dot(p.astype(BF), do, preferred_element_type=F32)
                tk = jnp.dot(ds, q, preferred_element_type=F32)
                dv = tv if dv is None else dv + tv
                dk = tk if dk is None else dk + tk
                dq_acc[at_q, :] += dg(ds, k, TN)
            part[chunk, at_k, :HEAD] = (dk * SCALE).astype(BF)
            part[chunk, at_k, HEAD:] = dv.astype(BF)

    @pl.loop(1, RING)
    def _(i):
        attend(g.index(g.ring(i), 1 - g.p), False)
        keys.send_far(i)

    ups.add()
    outs.forward()
    wide.forward()

    @pl.loop(1, RING)
    def _(i):
        attend(g.index(g.ring(i), g.p), False)
        keys.send_near(i)
        keys.add_near(i)

    def lay(at, value):
        lay_out[mine_t, at, :] = (mid_ref[at, :] + (value + bias_ref[...])).astype(BF)

    outs.finish(lay)
    layer.start()
    attend(g.index(g.r, 1 - g.p), False)
    keys.send_pair()
    keys.add_pair()
    ups.forward()
    attend(me, True)
    dq_ref[...] = (dq_acc[...] * SCALE).astype(BF)
    layer.forward()
    wide.finish()

    def keep(at, value):
        dkv_out[at, :] = value.astype(BF)

    keys.finish(keep)

    def keep_up(at, value):
        dup_out[at, :] = value

    ups.finish(keep_up)
    layer.finish()


def attend_back_call(meta, lanes, q, kv, o, do, lse, opart, gb, mid, bias, dup):
    rows = q.shape[0]
    tr, width = mid.shape
    sr, sw = dup.shape[2:]
    return remote_call(
        attend_back_kernel, "attend_back", 5,
        (struct(q.shape, BF), struct((rows, 2 * HEAD), BF), struct((8, tr, width), BF), struct((8, tr, width), BF), struct((sr, sw), F32)),
        [SM] + [VM] * 11,
        [pltpu.VMEM((rows, 2 * HEAD), BF), pltpu.VMEM((8 * rows, HEAD), BF), pltpu.VMEM(kv.shape, BF), pltpu.VMEM((8, rows), F32),
         pltpu.VMEM((rows, HEAD), F32), pltpu.VMEM((8, 128), F32), pltpu.VMEM((8, 128), F32)]
        + Scatter.scratch(rows, 2 * HEAD) + Scatter.scratch(tr, width) + CoreScatter.scratch(sr, sw) + Gather.scratch() * 2,
        meta, lanes, q, kv, o, do, lse, opart, gb, mid, bias, dup)


def chip_members():
    d, t = lax.axis_index("dp"), lax.axis_index("tensor")
    c = lax.rem(d, 2)
    out = []
    for dt in range(8):
        for dc in range(2):
            if dt or dc:
                tt = lax.rem(t + dt, 8)
                cc = lax.rem(c + dc, 2)
                out.append((tt, cc, (d - c + cc, tt)))
    return out


def norm_rows(values):
    average = jnp.mean(values, axis=-1, keepdims=True)
    centred = values - average
    variance = jnp.mean(centred * centred, axis=-1, keepdims=True)
    inverse = lax.rsqrt(variance + EPS)
    return centred * inverse, inverse


def norm_back(grad, scaled, inverse, gain):
    e = grad * gain
    first = jnp.mean(e, axis=-1, keepdims=True)
    second = jnp.mean(e * scaled, axis=-1, keepdims=True)
    return inverse * (e - first - scaled * second)


def middle_kernel(o_ref, w_hbm, x_ref, bias_ref, gain_ref, shift_ref, down_ref, n_out, mid_out, own_out, down_all,
                  w_ref, mixed, lsem, asems, arecv, *sems):
    g, gd = Eight("tensor"), Eight("dp")
    c = lax.rem(g.d, 2)
    members = chip_members()
    load = pltpu.make_async_copy(w_hbm, w_ref, lsem.at[0])
    load.start()
    shard = down_ref.shape[0]
    down_place = lambda m: down_all.at[pl.ds(pl.multiple_of((m * 2 + c) * shard, shard), shard)]
    local = pltpu.make_async_copy(down_ref, down_place(gd.index(gd.r, gd.p)), lsem.at[1])
    local.start()
    greet([m[2] for m in members] + gd.others())
    rows = x_ref.shape[0]
    half = o_ref.shape[0] // 2
    asem = (asems, arecv)
    head = pl.ds(pl.multiple_of((2 * g.t + c) * HEAD, HEAD), HEAD)
    mine = pl.ds(pl.multiple_of(c * HEAD, HEAD), HEAD)
    copies = []
    for k, (tt, cc, device) in enumerate(members):
        take = pl.ds(pl.multiple_of(cc * half + tt * rows, rows), rows)
        copies.append(send(o_ref.at[take], mixed.at[:, head], asem, k, device))
    copies.append(send(o_ref.at[pl.ds(pl.multiple_of((1 - c) * half, half), half)], own_out.at[:, mine], asem, 15, other_core()))
    downs = Gather(gd, down_place, shard, sems[2:4], other_core(), sems[4:6])
    local.wait()
    downs.start()
    mixed[:, head] = o_ref[pl.ds(pl.multiple_of(c * half + g.t * rows, rows), rows), :]
    own_out[:, mine] = o_ref[pl.ds(pl.multiple_of(c * half, half), half), :]
    load.wait()
    for copy in copies:
        copy.wait_recv()
    wide = 512
    for n in range(mid_out.shape[1] // wide):
        cols = pl.ds(n * wide, wide)
        total = None
        for t in range(8):
            term = dg(mixed[:, t * 256:(t + 1) * 256], w_ref[t, cols, :], NT)
            total = term if total is None else total + term
        mid_out[:, cols] = total + (x_ref[:, cols].astype(F32) + bias_ref[:, cols])
    scaled, _ = norm_rows(mid_out[...])
    n_out[g.index(g.r, g.p)] = (scaled * gain_ref[...] + shift_ref[...]).astype(BF)
    gather = Gather(g, lambda m: n_out.at[m], rows, sems[:2])
    gather.start()
    downs.forward()
    gather.forward()
    gather.finish()
    downs.finish()
    for copy in copies:
        copy.wait_send()


def middle_call(o, w, x, bias, gain, shift, down):
    rows, width = x.shape
    hbm = pl.BlockSpec(memory_space=pl.ANY)
    return remote_call(
        middle_kernel, "middle", 3,
        (struct((8, rows, width), BF), struct((rows, width), F32), struct((o.shape[0] // 2, 2 * HEAD), BF),
         struct((16 * down.shape[0], down.shape[1]), BF)),
        [VM, hbm, VM, VM, VM, VM, hbm],
        [pltpu.VMEM(w.shape, BF), pltpu.VMEM((rows, width), BF), DMA((2,)), DMA((16,)), DMA((16,))]
        + Gather.scratch() + Gather.scratch(True),
        o, w, x, bias, gain, shift, down, out_specs=(VM, VM, VM, hbm))


def back_kernel(part_ref, mid_ref, g_ref, w_hbm, gain_ref, do_out, gm_out, sums_out, low_out,
                w_ref, total, heads, lsem, asems, arecv, *scratch):
    g = Eight("tensor")
    c = lax.rem(g.d, 2)
    members = chip_members()
    load = pltpu.make_async_copy(w_hbm, w_ref, lsem.at[0])
    load.start()
    greet([m[2] for m in members])
    rows = g_ref.shape[0]
    half = do_out.shape[0] // 2
    first = Scatter(g, lambda m: part_ref.at[m], rows, scratch, 32)
    first.start()
    first.forward()

    def keep(at, value):
        total[at, :] = value

    first.finish(keep)
    scaled, inverse = norm_rows(mid_ref[...])
    grad = total[...]
    gm = g_ref[...].astype(F32) + norm_back(grad, scaled, inverse, gain_ref[...])
    gm_out[...] = gm
    low = gm.astype(BF)
    low_out[...] = low
    load.wait()
    for t in range(8):
        heads[:, t * 256:(t + 1) * 256] = jnp.dot(low, w_ref[t], preferred_element_type=F32).astype(BF)
    sems = (asems, arecv)
    take = pl.ds(pl.multiple_of(c * half + g.t * rows, rows), rows)
    copies = []
    for k, (tt, cc, device) in enumerate(members):
        cols = pl.ds(pl.multiple_of((2 * tt + cc) * HEAD, HEAD), HEAD)
        copies.append(send(heads.at[:, cols], do_out.at[take], sems, k, device))
    do_out[take, :] = heads[:, pl.ds(pl.multiple_of((2 * g.t + c) * HEAD, HEAD), HEAD)]
    sums_out[...] = jnp.zeros_like(sums_out)
    sums_out[0:1, :] = jnp.sum(grad * scaled, axis=0, keepdims=True)
    sums_out[1:2, :] = jnp.sum(grad, axis=0, keepdims=True)
    sums_out[2:3, :] = jnp.sum(low.astype(F32), axis=0, keepdims=True)
    sums_out[3:4, :] = jnp.sum(g_ref[...].astype(F32), axis=0, keepdims=True)
    for copy in copies:
        copy.wait()


def back_call(part, mid, g, w, gain):
    rows, width = g.shape
    return remote_call(
        back_kernel, "back", 4,
        (struct((16 * rows, HEAD), BF), struct((rows, width), F32), struct((8, width), F32), struct((rows, width), BF)),
        [VM, VM, VM, pl.BlockSpec(memory_space=pl.ANY), VM],
        [pltpu.VMEM(w.shape, BF), pltpu.VMEM((rows, width), F32), pltpu.VMEM((rows, width), BF), DMA((1,)), DMA((15,)), DMA((15,))]
        + Scatter.scratch(rows, width),
        part, mid, g, w, gain)


class Sums:
    @staticmethod
    def scratch(count, rows, width):
        return [pltpu.VMEM((count, rows, width), F32), DMA((count - 1,)), DMA((count - 1,))]

    def __init__(self, axis, scratch):
        self.slots, self.sems = scratch[0], scratch[1:]
        self.count = self.slots.shape[0]
        self.axis = axis
        self.d, self.t = lax.axis_index("dp"), lax.axis_index("tensor")
        self.me = self.d if axis == "dp" else self.t

    def device(self, k):
        other = lax.rem(self.me + k, self.count)
        return (other, self.t) if self.axis == "dp" else (self.d, other)

    def copy(self, k):
        own = self.slots.at[self.me]
        return copy_of(own, own, self.sems, k - 1, self.device(k))

    def start(self):
        @pl.loop(1, self.count)
        def _(k):
            self.copy(k).start()

    def finish(self):
        @pl.loop(1, self.count)
        def _(k):
            self.copy(k).wait()
        total = self.slots[0]
        for k in range(1, self.count):
            total = total + self.slots[k]
        return total


def tail_kernel(dw_ref, part_ref, gm_ref, x_ref, gain_ref, ddown_ref, dout_ref, early_ref, lane_ref,
                dw_out, tg_out, ddown_out, dout_out, sums_out, lanes_out,
                summed, arrived, total, mine_w, css, crs, ss, rs, *scratch):
    dp, g = Eight("dp"), Eight("tensor")
    c = lax.rem(g.d, 2)
    core = other_core()
    everyone = [Sums("dp", [scratch[-3], None, None]).device(k) for k in range(1, 16)]
    everyone += [Sums("tensor", [scratch[-6], None, None]).device(k) for k in range(1, 8)]
    greet(everyone)
    csems = (css, crs)
    weights = Scatter(dp, lambda m: dw_ref.at[m], dw_ref.shape[1], scratch[:7], 128)
    tokens = Scatter(g, lambda m: summed.at[m], x_ref.shape[0], scratch[7:14], 32)
    downs = CoreScatter(dp, ddown_ref, scratch[14:25], 32)
    outs = CoreScatter(dp, dout_ref, scratch[25:36], 128)
    early_t, lanes_d, late_t, all_d = (
        Sums("tensor", scratch[36:39]), Sums("dp", scratch[39:42]), Sums("tensor", scratch[42:45]), Sums("dp", scratch[45:48]))
    swap = send(part_ref.at[1 - c], arrived, csems, 0, core)
    weights.start()
    downs.start()
    outs.start()
    early_t.slots[g.t] = early_ref[...]
    early_t.start()
    lanes_d.slots[g.d] = lane_ref[...]
    lanes_d.start()
    swap.wait_recv()
    rows, width = x_ref.shape

    @pl.loop(0, 8)
    def _(t):
        @pl.loop(0, rows // 32)
        def _(n):
            at = pl.ds(pl.multiple_of(n * 32, 32), 32)
            summed[t, at, :] = (part_ref[c, t, at, :].astype(F32) + arrived[t, at, :].astype(F32)).astype(BF)

    tokens.start()
    downs.add()
    outs.add()
    tokens.forward()
    weights.forward()

    def keep(at, value):
        total[at, :] = value

    tokens.finish(keep)
    scaled, inverse = norm_rows(x_ref[...].astype(F32))
    grad = total[...]
    tg = gm_ref[...] + norm_back(grad, scaled, inverse, gain_ref[...])
    tg_out[g.index(g.r, g.p)] = tg.astype(BF)
    gather = Gather(g, lambda m: tg_out.at[m], rows, (ss, rs))
    gather.start()
    late_t.slots[g.t] = jnp.zeros(late_t.slots.shape[1:], F32)
    late_t.slots[g.t, 0:1, :] = jnp.sum(grad * scaled, axis=0, keepdims=True)
    late_t.slots[g.t, 1:2, :] = jnp.sum(grad, axis=0, keepdims=True)
    late_t.start()
    downs.forward()
    outs.forward()
    all_d.slots[g.d, 8:16, :] = early_t.finish()
    all_d.slots[g.d, 0:8, :] = late_t.finish()
    all_d.start()

    def keep_w(at, value):
        mine_w[at, :] = value.astype(BF)

    weights.finish(keep_w)
    share = dw_out.shape[1]
    there = send(mine_w.at[pl.ds(pl.multiple_of((1 - c) * share, share), share)], dw_out.at[c], csems, 1, core)
    dw_out[c] = mine_w[pl.ds(pl.multiple_of(c * share, share), share), :]
    gather.forward()

    def keep_down(at, value):
        ddown_out[at, :] = value

    downs.finish(keep_down)

    def keep_out(at, value):
        dout_out[at, :] = value

    outs.finish(keep_out)
    lanes_out[...] = lanes_d.finish()
    sums_out[...] = all_d.finish()
    gather.finish()
    there.wait()
    swap.wait_send()


def tail_call(dw, part, gm, x, gain, ddown, dout, early, lane):
    rows, width = x.shape
    wr, wc = dw.shape[1:]
    return remote_call(
        tail_kernel, "tail", 6,
        (struct((2, wr // 2, wc), BF), struct((8, rows, width), BF), struct(ddown.shape[2:], F32), struct(dout.shape[2:], F32),
         struct((16, width), F32), struct(lane.shape, F32)),
        [VM] * 9,
        [pltpu.VMEM((8, rows, width), BF), pltpu.VMEM((8, rows, width), BF), pltpu.VMEM((rows, width), F32), pltpu.VMEM((wr, wc), BF),
         DMA((2,)), DMA((2,)), DMA((10,)), DMA((10,))] + Scatter.scratch(wr, wc) + Scatter.scratch(rows, width)
        + CoreScatter.scratch(*ddown.shape[2:]) + CoreScatter.scratch(*dout.shape[2:])
        + Sums.scratch(8, *early.shape) + Sums.scratch(16, *lane.shape) + Sums.scratch(8, 8, width) + Sums.scratch(16, 16, width),
        dw, part, gm, x, gain, ddown, dout, early, lane)


def on_device(tokens, first_gain, first_shift, query_weight, query_bias, key_weight, value_weight, value_bias,
              out_weight, out_bias, second_gain, second_shift, up_weight, up_bias, down_weight, down_bias,
              cotangent, prefix, block_order):
    own, width = tokens.shape
    d, t = lax.axis_index("dp"), lax.axis_index("tensor")
    c = lax.rem(d, 2)
    nblk = block_order.shape[0]
    rows = own // 8
    meta = jnp.concatenate([block_order % nblk, prefix])
    lanes = jnp.pad(block_order % nblk, (0, HEAD - nblk), constant_values=-1).reshape(1, HEAD)
    row = lambda v: v.reshape(1, -1)

    scaled, _ = norm_rows(tokens.astype(F32))
    normed = (scaled * first_gain + first_shift).astype(BF)
    shards = jnp.stack([
        jnp.concatenate([w[:, h * HEAD:(h + 1) * HEAD] for w in (query_weight, key_weight, value_weight)], axis=1).astype(BF)
        for h in range(2)])
    w_all, n_all = gather_weights(shards, normed)
    w_all = w_all.reshape(width, 3 * HEAD)
    n_all = n_all.reshape(2 * own, width)
    pick = lambda v: lax.dynamic_slice_in_dim(v, c * HEAD, HEAD)
    bias = jnp.concatenate([pick(query_bias), jnp.zeros((HEAD,), F32), pick(value_bias)])
    qkv = (dg(n_all, w_all, NN) + bias).astype(BF)
    q = qkv[:, :HEAD]
    kv, o, lse, out_all, up_all = attend_call(meta, lanes, q, qkv[:, HEAD:], out_weight.astype(BF).T, up_weight.astype(BF))

    here = lambda v: lax.dynamic_slice_in_dim(v, t * rows, rows)
    x_rows, g_rows = here(tokens), here(cotangent)
    n2, mid, mixed, down_all = middle_call(
        o, out_all, x_rows, row(out_bias), row(second_gain), row(second_shift), down_weight.astype(BF).T)
    n2 = n2.reshape(own, width)
    pre = dg(n2, up_all, NN) + up_bias
    half_erf = 0.5 + 0.5 * lax.erf(pre * math.sqrt(0.5))
    hidden = (pre * half_erf).astype(BF)
    slope = half_erf + pre * jnp.exp(-0.5 * pre * pre) * (1.0 / math.sqrt(2.0 * math.pi))
    grad_pre = (dg(cotangent, down_all, NN) * slope).astype(BF)
    gn2 = dg(grad_pre, up_all, NT).astype(BF).reshape(8, rows, width)
    out_part = dg(hidden, down_all, NT).astype(BF).reshape(8, rows, width)
    do, gm, sums, low = back_call(gn2, mid, g_rows, out_all, row(second_gain))
    hid = up_weight.shape[1]
    dw_up = dg(n2, grad_pre, TN).astype(BF).reshape(8, 2, width // 16, hid)
    dw_down = dg(cotangent, hidden, TN).astype(BF).reshape(8, 2, width // 16, hid)
    dq, dkv, layer, gb, up_grad = attend_back_call(meta, lanes, q, kv, o, do, lse, out_part, low, mid, row(down_bias), dw_up)
    dw_out = dg(gb.reshape(own, width), mixed, TN).astype(BF).reshape(8, 2, width // 16, 2 * HEAD)

    dqkv = jnp.concatenate([dq, dkv], axis=1)
    dw = dg(n_all, dqkv, TN).astype(BF).reshape(8, width // 8, 3 * HEAD)
    gn1 = dg(dqkv, w_all, NT).astype(BF).reshape(2, 8, rows, width)
    col = jnp.sum(dqkv.astype(F32), axis=0)
    zero = jnp.zeros((HEAD,), F32)
    two = lambda v: jnp.concatenate([jnp.where(c == 0, v, zero), jnp.where(c == 1, v, zero)])
    lane = jnp.concatenate([jnp.sum(grad_pre.astype(F32), axis=0), two(col[:HEAD]), two(col[2 * HEAD:])])
    lane = jnp.pad(lane.reshape(1, -1), ((0, 7), (0, 0)))
    dw_mine, tg, down_grad, out_grad, small, lane = tail_call(
        dw, gn1, gm, x_rows, row(first_gain), dw_down, dw_out, sums, lane)
    pieces = [
        jnp.concatenate([dw_mine[0, :, i * HEAD:(i + 1) * HEAD], dw_mine[1, :, i * HEAD:(i + 1) * HEAD]], axis=1).astype(F32)
        for i in range(3)]
    return (
        layer.reshape(own, width),
        tg.reshape(own, width).astype(F32),
        small[0], small[1],
        pieces[0], lane[0, hid:hid + 2 * HEAD], pieces[1], pieces[2], lane[0, hid + 2 * HEAD:],
        out_grad.T, small[10],
        small[8], small[9],
        up_grad, lane[0, :hid],
        down_grad.T, small[11],
    )


def solution(mesh):
    rows, cols = P("dp", "tensor"), P("tensor", "dp")
    return jax.shard_map(
        on_device,
        mesh=mesh,
        in_specs=(
            P("dp", None), P(), P(), rows, P("tensor"), rows, rows, P("tensor"), cols, P(), P(), P(), rows, P("tensor"),
            cols, P(), P("dp", None), P(), P()),
        out_specs=(
            P("dp", None), P("dp", None), P(), P(), rows, P("tensor"), rows, rows, P("tensor"), cols, P(), P(), P(), rows,
            P("tensor"), cols, P()),
        check_vma=False,
    )
```

time: 832 us -> 576 us (0.69)
  waiting for transfers between devices: 288 us -> 0 us
  Pallas kernels: 408 us -> 479 us
  local copies, waits for them, and re-layouts: 48.3 us -> 23.3 us
  between operations: 15.8 us -> 2.23 us
    pallas_call x6, Pallas kernels: 352 us -> 479 us  [remote_call(): pl.pallas_call(kernel, out_shape=outs, in_specs=ins, out_specs=jax.tree.m...]
    psum x1 -> x0, waiting for transfers between devices: 117 us -> none  [on_device(): vec = lax.psum(vec, ('dp', 'tensor'))]
    unnamed x7 -> x0, waiting for transfers between devices: 103 us -> none
    all_gather x4 -> x0, waiting for transfers between devices: 68.6 us -> none  [the longest x1 38.9 us: on_device(): lax.all_gather(out_weight.astype(BF).T, 'dp', axis=0, tiled=True)]
    pallas_call x2 -> x0, Pallas kernels: 56.1 us -> none  [the longest x1 32.5 us: attn_bwd(): pl.pallas_call(attn_bwd_kernel, out_shape=(struct(q.shape, BF), struct(kv...]
    unnamed x80 -> x54, local copies, waits for them, and re-layouts: 26.3 us -> 6.61 us
    all_gather x1 -> x0, local copies, waits for them, and re-layouts: 12 us -> none  [on_device(): lax.all_gather(lax.all_gather(out_weight.astype(BF).T, 'dp', axis=0, tile...]
  transfers between devices with their start and end apart: 6 -> 0, of which waited for: 5 -> 0; matrix products, arithmetic and copies ran while one was open for 8% -> 0% of each run, Pallas kernels for 20% -> 0%
where the time goes in v2:
time: 576 us; the launch traced here: 565 us
  Pallas kernels  479 us (83%)
  matrix products  43.9 us (8%)
  local copies, waits for them, and re-layouts  23.3 us (4%)
  other arithmetic  16.7 us (3%)
    pallas_call x6, Pallas kernels, remote_call(): pl.pallas_call(kernel, out_shape=outs, in_specs=ins, out_specs=jax.tree.m...  479 us
    dot_general x10, matrix products, dg(): return lax.dot_general(a, b, dims, preferred_element_type=F32)  43.9 us

profile of v2, /device:TPU:1, one launch (start us, length us, event | category | flops | bytes accessed | tf_op | source)
XLA Modules:
  0.0 564.7 jit_solution(11423454279232076799)
XLA Ops:
  0.7 0.0 copy-start
  1.5 0.7 and_select_fusion
  2.1 0.6 pad_add_fusion.meta
  2.7 0.5 pad_bitcast_fusion.lanes_ref
  3.2 0.9 convert.27
  4.1 0.9 convert.26
  5.1 0.9 convert.25
  6.0 0.7 maximum_maximum_fusion.w_ref
  6.7 2.0 convert_reduce_fusion
  8.7 0.7 fusion.2
  9.4 2.2 fusion.5.n_ref
  11.6 27.9 %weights.1 = (bf16[8,256,384]{2,1,0:T(8,128)(2,1)}, bf16[2,512,2048]{2,1,0:T(8,128)(2,1)}) custom-call(bf16[2,128,384]{2,1,0:T(8,128)(2,1)} %maximum_maximum_fusion.w_ref, bf16[512,2048]{1,0:T(8,128)(2,1)} %fusion.5.n_ref), custom_call_target="tpu_custom_call" | custom-call | tf_op jit(solution)/shard_map/weights/pallas_call | solution.py:368
  39.5 0.1 dynamic_slice.13
  39.6 0.1 dynamic_slice.12
  39.7 0.0 copy-start.7
  39.7 5.0 add_convert_fusion
  44.8 0.0 copy-start.2
  44.8 0.7 slice.112.q_ref
  45.5 0.8 slice.113.k_ref
  46.3 0.7 copy.36
  47.1 0.7 convert_element_type.91.up_ref
  47.8 119.2 %attend.1 = (bf16[8,1024,256]{2,1,0:T(8,128)(2,1)}, bf16[1024,128]{1,0:T(8,128)(2,1)}, f32[4,256]{1,0:T(4,128)}, bf16[8,2048,256]{2,1,0:T(8,128)(2,1)}, bf16[2048,1024]{1,0:T(8,128)(2,1)}) custom-call(s32[33]{0:T(128)} %pad_add_fusion.meta, s32[1,128]{1,0:T(1,128)} %pad_bitcast_fusion.lanes_ref, bf16[1024,128]{1,0:T(8,128)(2,1)} %slice.112.q_ref, ...), custom_call_target="tpu_custom_call" | custom-call | tf_op jit(solution)/shard_map/attend/pallas_call | solution.py:368
  167.1 1.8 constant_dynamic-slice_fusion
  168.8 0.0 copy-done.3
  168.8 0.8 copy.37
  169.7 54.4 %middle.1 = (bf16[8,64,2048]{2,1,0:T(8,128)(2,1)}, f32[64,2048]{1,0:T(8,128)}, bf16[512,256]{1,0:T(8,128)(2,1)}, bf16[2048,1024]{1,0:T(8,128)(2,1)}) custom-call(bf16[1024,128]{1,0:T(8,128)(2,1)} %get-tuple-element.46.o_ref, bf16[8,2048,256]{2,1,0:T(8,128)(2,1)} %get-tuple-element.47.w_hbm, bf16[64,2048]{1,0:T(8,128)(2,1)} %get-tuple-element.111.x_ref, ...), custom_call_target="tpu_custom_call" | custom-call | tf_op jit(solution)/shard_map/middle/pallas_call | solution.py:368
  224.1 0.0 copy-start.10
  224.1 0.0 copy-start.18
  224.1 5.3 fusion.15
  229.4 0.0 copy-done.10
  229.4 0.0 copy-done.13
  229.5 0.0 copy-done.18
  229.5 0.0 copy-start.12
  229.5 3.0 convert_reduce_fusion.1
  232.5 0.0 copy-start.21
  232.5 0.0 copy-done.12
  232.5 3.7 convolution_convert_fusion.3
  236.2 34.5 %back.1 = (bf16[1024,128]{1,0:T(8,128)(2,1)}, f32[64,2048]{1,0:T(8,128)}, f32[8,2048]{1,0:T(8,128)}, bf16[64,2048]{1,0:T(8,128)(2,1)}) custom-call(bf16[8,64,2048]{2,1,0:T(8,128)(2,1)} %bitcast.89, f32[64,2048]{1,0:T(8,128)} %get-tuple-element.51.mid_ref, bf16[64,2048]{1,0:T(8,128)(2,1)} %get-tuple-element.110.g_ref, ...), custom_call_target="tpu_custom_call" | custom-call | tf_op jit(solution)/shard_map/back/pallas_call | solution.py:368
  270.7 0.0 copy-start.22
  270.7 6.1 %convolution_convert_fusion.2 = bf16[512,2048]{1,0:T(8,128)(2,1)} fusion(bf16[2048,1024]{1,0:T(8,128)(2,1)} %get-tuple-element.48, f32[512,1024]{1,0:T(8,128)S(1)} %fusion.15, f32[1024]{0:T(1024)S(1)} %copy-done.18), kind=kOutput, calls=%fused_computation.12 | convolution fusion | flops 2151677952 | bytes 8392704 | tf_op jit(solution)/shard_map/dot_general | solution.py:32
  276.8 4.4 convolution_convert_fusion.1
  281.2 115.4 %attend_back.1 = (bf16[1024,128]{1,0:T(8,128)(2,1)}, bf16[1024,256]{1,0:T(8,128)(2,1)}, bf16[8,64,2048]{2,1,0:T(8,128)(2,1)}, bf16[8,64,2048]{2,1,0:T(8,128)(2,1)}, f32[128,1024]{1,0:T(8,128)}) custom-call(s32[33]{0:T(128)} %pad_add_fusion.meta, s32[1,128]{1,0:T(1,128)} %pad_bitcast_fusion.lanes_ref, bf16[1024,128]{1,0:T(8,128)(2,1)} %slice.112.q_ref, ...), custom_call_target="tpu_custom_call" | custom-call | tf_op jit(solution)/shard_map/attend_back/pallas_call | solution.py:368
  396.5 1.0 constant_dynamic-update-slice_fusion.1
  397.5 1.1 constant_dynamic-update-slice_fusion
  398.6 5.9 %convolution_convert_fusion.4 = bf16[2048,384]{1,0:T(8,128)(2,1)} fusion(bf16[1024,2048]{1,0:T(8,128)(2,1)} %bitcast.113, bf16[1024,384]{1,0:T(8,128)(2,1)S(1)} %constant_dynamic-update-slice_fusion), kind=kOutput, calls=%fused_computation.14 | convolution fusion | flops 1611399168 | bytes 6553600 | tf_op jit(solution)/shard_map/dot_general | solution.py:32
  404.5 4.4 convolution_convert_fusion
  408.9 4.4 convert_bitcast_fusion
  413.3 6.5 %copy.38 = bf16[2048,1024]{1,0:T(8,128)(2,1)} copy(bf16[2048,1024]{0,1:T(8,128)(2,1)} %convert_bitcast_fusion) | data formatting | bytes 8388608 | tf_op jit(solution)/shard_map/convert_element_type | solution.py:968
  419.9 1.7 convolution_convert_fusion.5
  421.6 0.2 convert_reduce_fusion.2
  421.8 0.6 pad.9.lane_ref
  422.5 127.2 %tail.1 = (bf16[2,128,384]{2,1,0:T(8,128)(2,1)}, bf16[8,64,2048]{2,1,0:T(8,128)(2,1)}, f32[128,1024]{1,0:T(8,128)}, f32[128,256]{1,0:T(8,128)}, f32[16,2048]{1,0:T(8,128)}, /*index=5*/f32[8,1536]{1,0:T(8,128)}) custom-call(bf16[8,256,384]{2,1,0:T(8,128)(2,1)} %bitcast.91, bf16[2,8,64,2048]{3,2,1,0:T(8,128)(2,1)} %bitcast.86, ...), custom_call_target="tpu_custom_call" | custom-call | tf_op jit(solution)/shard_map/tail/pallas_call | solution.py:368
  549.7 4.2 bitcast_convert_fusion
  553.9 1.8 fusion.13
  555.7 0.7 maximum_convert_fusion
  556.4 1.3 fusion.14
  557.7 0.7 maximum_convert_fusion.1
  558.3 0.7 maximum_convert_fusion.2
  559.0 0.8 copy.39
  559.7 1.4 slice.104
  561.1 1.0 copy.40
  562.1 1.3 copy.49
  563.4 0.1 copy-done.4
  563.5 0.8 copy.50
  (45 shorter events, 0.2 us)
Async XLA Ops:
  0.7 8.0 %copy-start = (bf16[512,2048]{1,0:T(8,128)(2,1)S(1)}, bf16[512,2048]{1,0:T(8,128)(2,1)}, u32[]{:S(2)}) copy-start(bf16[512,2048]{1,0:T(8,128)(2,1)} %param.19) | copy-start | bytes 6291460
  6.7 2.7 copy-start.9
  6.7 2.7 copy-start.11
  11.6 27.9 %copy-start.19 = (f32[256]{0:T(256)S(1)}, f32[256]{0:T(256)}, u32[]{:S(2)}) copy-start(f32[256]{0:T(256)} %param.26) | copy-start | bytes 3076
  11.6 28.0 %copy-start.20 = (f32[256]{0:T(256)S(1)}, f32[256]{0:T(256)}, u32[]{:S(2)}) copy-start(f32[256]{0:T(256)} %param.23) | copy-start | bytes 3076
  39.7 6.6 %copy-start.7 = (f32[256,128]{1,0:T(8,128)S(1)}, f32[256,128]{1,0:T(8,128)}, u32[]{:S(2)}) copy-start(f32[256,128]{1,0:T(8,128)} %param.27) | copy-start | bytes 393220
  44.8 2.3 copy-start.2
  45.5 123.3 %copy-start.3 = (f32[1024,128]{1,0:T(8,128)S(1)}, f32[1024,128]{1,0:T(8,128)}, u32[]{:S(2)}) copy-start(f32[1024,128]{1,0:T(8,128)} %param.33) | copy-start | bytes 1572868
  224.1 5.3 copy-start.10
  224.1 5.3 copy-start.13
  224.1 5.3 copy-start.18
  229.5 3.0 copy-start.12
  232.5 3.7 copy-start.21
  270.7 6.1 %copy-start.15 = (bf16[8,64,2048]{2,1,0:T(8,128)(2,1)S(1)}, bf16[8,64,2048]{2,1,0:T(8,128)(2,1)}, u32[]{:S(2)}) copy-start(bf16[8,64,2048]{2,1,0:T(8,128)(2,1)} %get-tuple-element.49) | copy-start | bytes 6291460
  270.7 6.1 %copy-start.22 = (bf16[512,1024]{1,0:T(8,128)(2,1)S(1)}, bf16[512,1024]{1,0:T(8,128)(2,1)}, u32[]{:S(2)}) copy-start(bf16[512,1024]{1,0:T(8,128)(2,1)} %copy-done.21) | copy-start | bytes 3145732
  398.6 5.9 %copy-start.16 = (bf16[8,256,384]{2,1,0:T(8,128)(2,1)S(1)}, bf16[8,256,384]{2,1,0:T(8,128)(2,1)}, u32[]{:S(2)}) copy-start(bf16[8,256,384]{2,1,0:T(8,128)(2,1)} %get-tuple-element.44) | copy-start | bytes 4718596
  413.3 6.5 %copy-start.14 = (bf16[8,64,2048]{2,1,0:T(8,128)(2,1)S(1)}, bf16[8,64,2048]{2,1,0:T(8,128)(2,1)}, u32[]{:S(2)}) copy-start(bf16[8,64,2048]{2,1,0:T(8,128)(2,1)} %get-tuple-element.59) | copy-start | bytes 6291460
  413.3 6.5 %copy-start.17 = (bf16[512,256]{1,0:T(8,128)(2,1)S(1)}, bf16[512,256]{1,0:T(8,128)(2,1)}, u32[]{:S(2)}) copy-start(bf16[512,256]{1,0:T(8,128)(2,1)} %get-tuple-element.60) | copy-start | bytes 786436
  549.6 6.0 %copy-start.6 = (bf16[2,128,384]{2,1,0:T(8,128)(2,1)S(1)}, bf16[2,128,384]{2,1,0:T(8,128)(2,1)}, u32[]{:S(2)}) copy-start(bf16[2,128,384]{2,1,0:T(8,128)(2,1)} %get-tuple-element.64) | copy-start | bytes 589828
  549.6 9.3 %copy-start.8 = (f32[128,256]{1,0:T(8,128)S(1)}, f32[128,256]{1,0:T(8,128)}, u32[]{:S(2)}) copy-start(f32[128,256]{1,0:T(8,128)} %get-tuple-element.66) | copy-start | bytes 393220
  549.7 11.4 %copy-start.5 = (f32[128,1024]{1,0:T(8,128)S(1)}, f32[128,1024]{1,0:T(8,128)}, u32[]{:S(2)}) copy-start(f32[128,1024]{1,0:T(8,128)} %get-tuple-element.68) | copy-start | bytes 1572868
  553.9 8.2 %copy-start.1 = (bf16[8,64,2048]{2,1,0:T(8,128)(2,1)S(1)}, bf16[8,64,2048]{2,1,0:T(8,128)(2,1)}, u32[]{:S(2)}) copy-start(bf16[8,64,2048]{2,1,0:T(8,128)(2,1)} %get-tuple-element.55) | copy-start | bytes 6291460
  562.1 1.4 copy-start.4

commit v3 on v2

v3 whole, which is shorter than its diff:
```python
import functools
import math

import jax
import jax.numpy as jnp
from jax import lax
from jax.experimental import pallas as pl
from jax.experimental.pallas import tpu as pltpu
from jax.sharding import PartitionSpec as P

HEAD = 128
BLK = 256
GRP = 4
RING = 4
EPS = 1e-05
NEG = -(2.0 ** 100)
LOG2E = math.log2(math.e)
SCALE = 1.0 / math.sqrt(HEAD)
C1 = LOG2E * SCALE
NN = (((1,), (0,)), ((), ()))
NT = (((1,), (1,)), ((), ()))
TN = (((0,), (0,)), ((), ()))
MESH = pl.DeviceIdType.MESH
VM = pl.BlockSpec(memory_space=pltpu.VMEM)
SM = pl.BlockSpec(memory_space=pltpu.SMEM)
BF = jnp.bfloat16
F32 = jnp.float32
DMA = pltpu.SemaphoreType.DMA


def dg(a, b, dims):
    return lax.dot_general(a, b, dims, preferred_element_type=F32)


def struct(shape, dtype):
    return jax.ShapeDtypeStruct(shape, dtype)


class Eight:
    def __init__(self, axis):
        d, t = lax.axis_index("dp"), lax.axis_index("tensor")
        self.axis, self.d, self.t = axis, d, t
        if axis == "dp":
            self.r, self.p = d // 4, lax.rem(d // 2, 2)
        else:
            self.r, self.p = lax.rem(t, 4), t // 4

    def ring(self, i):
        return lax.rem(self.r + i, RING)

    def side(self, s):
        return 1 - self.p if s else self.p

    def index(self, r, p):
        return r * 2 + p if self.axis == "dp" else p * 4 + r

    def device(self, r, p):
        if self.axis == "dp":
            return ((r * 2 + p) * 2 + lax.rem(self.d, 2), self.t)
        return (self.d, p * 4 + r)

    def others(self):
        return [self.device(self.ring(i), self.p) for i in (1, 3)] + [self.device(self.r, 1 - self.p)]


def other_core():
    d = lax.axis_index("dp")
    return (d + 1 - 2 * lax.rem(d, 2), lax.axis_index("tensor"))


def greet(devices):
    barrier = pltpu.get_barrier_semaphore()
    for device in devices:
        pl.semaphore_signal(barrier, inc=1, device_id=device, device_id_type=MESH)
    pl.semaphore_wait(barrier, len(devices))


def send(src, dst, sems, k, device):
    copy = pltpu.make_async_remote_copy(
        src_ref=src, dst_ref=dst, send_sem=sems[0].at[k], recv_sem=sems[1].at[k],
        device_id=device, device_id_type=MESH)
    copy.start()
    return copy


def copy_of(src, dst, sems, k, device):
    return pltpu.make_async_remote_copy(
        src_ref=src, dst_ref=dst, send_sem=sems[0].at[k], recv_sem=sems[1].at[k],
        device_id=device, device_id_type=MESH)


def send(src, dst, sems, k, device):
    copy = copy_of(src, dst, sems, k, device)
    copy.start()
    return copy


class Gather:
    @staticmethod
    def scratch(twin=False):
        return [DMA((9,)), DMA((9,))] + ([DMA((8,)), DMA((8,))] if twin else [])

    def __init__(self, group, place, rows, sems, twin=None, twin_own=True):
        self.g, self.place, self.sems = group, place, sems[:2]
        self.twin, self.twin_sems, self.twin_own = twin, sems[2:4], twin_own
        self.halves = (pl.ds(0, rows // 2), pl.ds(rows // 2, rows // 2))

    def at(self, i, s):
        g = self.g
        return self.place(g.index(g.ring(i), g.side(s)))

    def to(self, i):
        g = self.g
        return g.device(g.ring(i), g.p)

    def pair(self):
        own = self.at(0, 0)
        return copy_of(own, own, self.sems, 0, self.g.device(self.g.r, 1 - self.g.p))

    def near(self, s, way):
        chunk = self.at(0, s)
        return copy_of(chunk, chunk, self.sems, 1 + 4 * s + way, self.to(1 + 2 * way))

    def relay(self, s, way):
        half = self.at(3 - 2 * way, s).at[self.halves[way]]
        return copy_of(half, half, self.sems, 3 + 4 * s + way, self.to(1 + 2 * way))

    def over(self, k, i, s):
        chunk = self.at(i, s)
        return copy_of(chunk, chunk, self.twin_sems, k, self.twin)

    def tell(self, i, s):
        if self.twin is not None and (i or s or self.twin_own):
            self.over(2 * i + s, i, s).start()

    def start(self):
        self.pair().start()
        for way in (0, 1):
            self.near(0, way).start()
        self.tell(0, 0)

    def forward_pair(self):
        self.pair().wait_recv()
        for way in (0, 1):
            self.near(1, way).start()
        self.tell(0, 1)

    def forward(self, s):
        for way in (0, 1):
            self.near(s, way).wait_recv()
            self.relay(s, way).start()
            self.tell(3 - 2 * way, s)

    def arrive(self, s):
        for way in (0, 1):
            self.relay(s, way).wait_recv()
        self.tell(2, s)

    def settle(self):
        self.pair().wait_send()
        for s in (0, 1):
            for way in (0, 1):
                self.near(s, way).wait_send()
                self.relay(s, way).wait_send()
        if self.twin is not None:
            for k in range(0 if self.twin_own else 1, 8):
                self.over(k, 0, 0).wait()

    def rest(self):
        self.forward_pair()
        self.forward(0)
        self.forward(1)
        self.arrive(0)
        self.arrive(1)
        self.settle()


class Scatter:
    COUNT = 9

    @staticmethod
    def scratch(rows, width):
        half = rows // 2
        return [
            pltpu.VMEM((2, 2, half, width), BF), pltpu.VMEM((2, 2, half, width), BF), pltpu.VMEM((2, 2, rows, width), BF),
            pltpu.VMEM((rows, width), BF), pltpu.VMEM((rows, width), BF), DMA((13,)), DMA((13,))]

    def __init__(self, group, part, rows, scratch, step):
        self.g, self.part, self.step, self.rows = group, part, step, rows
        self.mid, self.added, self.last, self.sum, self.end = scratch[:5]
        self.sems = scratch[5:7]
        self.half = rows // 2
        self.halves = (pl.ds(0, self.half), pl.ds(self.half, self.half))

    def at(self, i, s):
        g = self.g
        return self.part(g.index(g.ring(i), g.side(s)))

    def to(self, way):
        g = self.g
        return g.device(g.ring(1 + 2 * way), g.p)

    def far(self, s, way):
        return copy_of(self.at(2, s).at[self.halves[way]], self.mid.at[s, way], self.sems, 2 * s + way, self.to(way))

    def own(self, s, way):
        half = self.halves[1 - way]
        return copy_of(self.at(1 + 2 * way, s).at[half], self.last.at[s, way, half], self.sems, 4 + 2 * s + way, self.to(way))

    def both(self, s, way):
        return copy_of(self.added.at[s, way], self.last.at[s, way, self.halves[way]], self.sems, 8 + 2 * s + way, self.to(way))

    def pair(self):
        return copy_of(self.sum, self.end, self.sems, 12, self.g.device(self.g.r, 1 - self.g.p))

    def by_rows(self, rows, body):
        step = min(self.step, rows)

        @pl.loop(0, rows // step)
        def _(n):
            body(pl.multiple_of(n * step, step), step)

    def send_far(self, s):
        for way in (0, 1):
            self.far(s, way).start()

    def send_near(self, s):
        for way in (0, 1):
            self.own(s, way).start()

    def add_near(self, s):
        for way in (0, 1):
            self.far(s, way).wait_recv()
            mine = self.at(1 + 2 * way, s)
            base = way * self.half

            def add(at, n, way=way, mine=mine, base=base):
                rows = pl.ds(at, n)
                total = mine[pl.ds(base + at, n), :].astype(F32) + self.mid[s, way, rows, :].astype(F32)
                self.added[s, way, rows, :] = total.astype(BF)

            self.by_rows(self.half, add)
            self.both(s, way).start()

    def arrived(self, s):
        for way in (0, 1):
            self.own(s, way).wait_recv()
            self.both(s, way).wait_recv()

    def add_pair(self):
        self.arrived(1)
        mine = self.at(0, 1)

        def add(at, n):
            rows = pl.ds(at, n)
            total = mine[rows, :].astype(F32) + self.last[1, 0, rows, :].astype(F32) + self.last[1, 1, rows, :].astype(F32)
            self.sum[rows, :] = total.astype(BF)

        self.by_rows(self.rows, add)
        self.pair().start()

    def start(self):
        for s in (1, 0):
            self.send_far(s)
            self.send_near(s)

    def forward(self):
        self.add_near(1)
        self.add_near(0)
        self.add_pair()

    def finish(self, store):
        self.arrived(0)
        self.pair().wait_recv()
        mine = self.at(0, 0)

        def add(at, n):
            rows = pl.ds(at, n)
            total = mine[rows, :].astype(F32) + self.last[0, 0, rows, :].astype(F32) + self.last[0, 1, rows, :].astype(F32)
            store(rows, total + self.end[rows, :].astype(F32))

        self.by_rows(self.rows, add)
        self.pair().wait_send()
        for s in (0, 1):
            for way in (0, 1):
                self.far(s, way).wait_send()
                self.own(s, way).wait_send()
                self.both(s, way).wait_send()


class CoreScatter:
    @staticmethod
    def scratch(rows, width):
        return [pltpu.VMEM((8, rows, width), BF), pltpu.VMEM((8, rows, width), BF), DMA((1,)), DMA((1,))] + Scatter.scratch(rows, width)

    def __init__(self, group, part, scratch, step):
        self.part, self.arrived, self.added = part, scratch[0], scratch[1]
        self.c = lax.rem(group.d, 2)
        self.sems = scratch[2:4]
        self.step = step
        self.inner = Scatter(group, lambda m: self.added.at[m], part.shape[2], scratch[4:], step)

    def swap(self):
        return copy_of(self.part.at[:, 1 - self.c], self.arrived, self.sems, 0, other_core())

    def start(self):
        self.swap().start()

    def add(self):
        self.swap().wait_recv()
        rows, step = self.part.shape[2], self.step

        @pl.loop(0, 8)
        def _(m):
            @pl.loop(0, rows // step)
            def _(n):
                at = pl.ds(pl.multiple_of(n * step, step), step)
                self.added[m, at, :] = (self.part[m, self.c, at, :].astype(F32) + self.arrived[m, at, :].astype(F32)).astype(BF)

        self.inner.start()

    def forward(self):
        self.inner.forward()

    def finish(self, store):
        self.inner.finish(store)
        self.swap().wait_send()


def remote_call(kernel, name, cid, outs, ins, scratch, *args, out_specs=None):
    return pl.pallas_call(
        kernel, out_shape=outs, in_specs=ins,
        out_specs=jax.tree.map(lambda _: VM, outs) if out_specs is None else out_specs,
        scratch_shapes=scratch, name=name,
        compiler_params=pltpu.CompilerParams(collective_id=cid, has_side_effects=True, vmem_limit_bytes=58 << 20),
    )(*args)


def chip_members():
    d, t = lax.axis_index("dp"), lax.axis_index("tensor")
    c = lax.rem(d, 2)
    out = []
    for dt in range(8):
        for dc in range(2):
            if dt or dc:
                tt = lax.rem(t + dt, 8)
                cc = lax.rem(c + dc, 2)
                out.append((tt, cc, (d - c + cc, tt)))
    return out


def norm_rows(values):
    average = jnp.mean(values, axis=-1, keepdims=True)
    centred = values - average
    variance = jnp.mean(centred * centred, axis=-1, keepdims=True)
    inverse = lax.rsqrt(variance + EPS)
    return centred * inverse, inverse


def norm_back(grad, scaled, inverse, gain):
    e = grad * gain
    first = jnp.mean(e, axis=-1, keepdims=True)
    second = jnp.mean(e * scaled, axis=-1, keepdims=True)
    return inverse * (e - first - scaled * second)


def augment(meta, lanes_ref, q_ref, qa_ref, kx_ref):
    rows = q_ref.shape[0]
    nblk = kx_ref.shape[0] // BLK
    prefix = meta[nblk]
    for a in range(rows // BLK):
        at = slice(a * BLK, (a + 1) * BLK)
        hidden = jnp.where(lanes_ref[...] > meta[first_block() + a], NEG, 0.0)
        qa_ref[at, :HEAD] = q_ref[at, :]
        qa_ref[at, HEAD:] = jnp.broadcast_to(hidden, (BLK, HEAD)).astype(BF)
    lane = lax.broadcasted_iota(jnp.int32, (BLK, HEAD), 1)
    inside = lax.broadcasted_iota(jnp.int32, (BLK, HEAD), 0)

    @pl.loop(0, nblk)
    def _(b):
        late = (lane == b) & (inside >= prefix - meta[b] * BLK)
        kx_ref[pl.ds(pl.multiple_of(b * BLK, BLK), BLK), :] = jnp.where(late, 1.0, 0.0).astype(BF)


def first_block():
    return lax.axis_index("dp") // 2 * 4


def forward_kernel(meta, lanes_ref, x_ref, gain1_ref, shift1_ref, wq_ref, wk_ref, wv_ref, qb_ref, vb_ref, wo_ref, wu_ref, wd_ref,
                   bias_ref, gain2_ref, shift2_ref,
                   w_hbm, n_hbm, q_out, kv_hbm, o_ref, lse_ref, out_hbm, up_hbm, down_hbm, n2_out, mid_out, own_out,
                   w_vm, n_vm, kv_vm, out_vm, up_vm, down_vm, wsh, qa_ref, kx_ref, m_ref, acc_ref, mixed,
                   lsem, css, crs, ass, ars, *sems):
    gd, gt = Eight("dp"), Eight("tensor")
    t = gt.t
    c = lax.rem(gd.d, 2)
    core = other_core()
    members = chip_members()
    me = gd.index(gd.r, gd.p)
    own = x_ref.shape[0]
    rows = 2 * own
    nblk = kx_ref.shape[0] // BLK
    per = rows // BLK
    shard = wq_ref.shape[0]
    half = out_vm.shape[1] // 2
    small = mid_out.shape[0]
    csem, asem = (css, crs), (ass, ars)
    for h in range(2):
        cols = slice(h * HEAD, (h + 1) * HEAD)
        for i, ref in enumerate((wq_ref, wk_ref, wv_ref)):
            wsh[h, :, i * HEAD:(i + 1) * HEAD] = ref[:, cols].astype(BF)
    greet([m[2] for m in members] + gd.others())

    w_place = lambda m: w_vm.at[pl.ds(pl.multiple_of(m * 2 * shard, 2 * shard), 2 * shard)]
    row_of = lambda m: pl.ds(pl.multiple_of((m * 2 + c) * shard, shard), shard)
    mine = row_of(me)
    swap = send(wsh.at[1 - c], w_vm.at[mine], csem, 0, core)
    w_vm[mine, :] = wsh[c]
    qkv = Gather(gd, w_place, 2 * shard, sems[0:2])
    keys = Gather(gd, lambda m: kv_vm.at[m], rows, sems[2:4])
    outs = Gather(gd, lambda m: out_vm.at[t, row_of(m)], shard, sems[4:8], core)
    ups = Gather(gd, lambda m: up_vm.at[row_of(m)], shard, sems[8:12], core)
    downs = Gather(gd, lambda m: down_vm.at[row_of(m)], shard, sems[12:16], core)
    wide = Gather(gt, lambda m: out_vm.at[m, pl.ds(pl.multiple_of(c * half, half), half)], half, sems[16:20], core, twin_own=False)
    normed = Gather(gt, lambda m: n2_out.at[m], small, sems[20:22])
    swap.wait_recv()
    qkv.start()
    out_vm[t, mine, :] = jnp.transpose(wo_ref[...]).astype(BF)
    outs.start()

    def norm_part(k):
        step = 32

        @pl.loop(0, own // 2 // step)
        def _(n):
            at = pl.ds(pl.multiple_of(k * (own // 2) + n * step, step), step)
            scaled, _ = norm_rows(x_ref[at, :].astype(F32))
            n_vm[c, at, :] = (scaled * gain1_ref[...] + shift1_ref[...]).astype(BF)

        at = pl.ds(k * (own // 2), own // 2)
        return send(n_vm.at[c, at], n_vm.at[c, at], csem, 1 + k, core)

    there = [norm_part(0)]
    outs.forward_pair()
    outs.forward(0)
    qkv.forward_pair()
    qkv.forward(0)
    there.append(norm_part(1))
    outs.forward(1)
    outs.arrive(0)
    qkv.forward(1)
    up_vm[mine, :] = wu_ref[...].astype(BF)
    outs.arrive(1)
    down_vm[mine, :] = jnp.transpose(wd_ref[...]).astype(BF)
    outs.settle()
    wide.start()
    qkv.arrive(0)
    qkv.arrive(1)
    for copy in there:
        copy.wait_recv()
    local = pl.ds(pl.multiple_of(c * HEAD, HEAD), HEAD)
    bias_q, bias_v = qb_ref[:, local], vb_ref[:, local]

    @pl.loop(0, per)
    def _(b):
        at = pl.ds(pl.multiple_of(b * BLK, BLK), BLK)
        piece = dg(n_vm[b // 2, pl.ds(pl.multiple_of(lax.rem(b, 2) * BLK, BLK), BLK), :], w_vm[...], NN)
        q_out[at, :] = (piece[:, :HEAD] + bias_q).astype(BF)
        kv_vm[me, at, :HEAD] = piece[:, HEAD:2 * HEAD].astype(BF)
        kv_vm[me, at, HEAD:] = (piece[:, 2 * HEAD:] + bias_v).astype(BF)

    keys.start()
    saves = [pltpu.make_async_copy(w_vm, w_hbm, lsem.at[0]), pltpu.make_async_copy(n_vm, n_hbm, lsem.at[1])]
    for save in saves:
        save.start()
    augment(meta, lanes_ref, q_out, qa_ref, kx_ref)
    m_ref[...] = jnp.full_like(m_ref, -1e30)
    acc_ref[...] = jnp.zeros_like(acc_ref)
    ones = jnp.ones((BLK, HEAD), BF)
    prefix = meta[nblk]

    def attend(chunk, diagonal):
        @pl.loop(0, per)
        def _(a):
            take = pl.ds(pl.multiple_of(a * BLK, BLK), BLK)
            q = qa_ref[take, :]
            ss, vs = [], []
            for i in range(per):
                at = pl.ds(pl.multiple_of(chunk * rows + i * BLK, BLK), BLK)
                ss.append(dg(q, jnp.concatenate([kv_vm[chunk, i * BLK:(i + 1) * BLK, :HEAD], kx_ref[at, :]], axis=1), NT))
                vs.append(jnp.concatenate([kv_vm[chunk, i * BLK:(i + 1) * BLK, HEAD:], ones], axis=1))
            if diagonal:
                edge = prefix - 1 - meta[first_block() + a] * BLK
                lim = jnp.maximum(lax.broadcasted_iota(jnp.int32, (BLK, BLK), 0), edge)
                key = lax.broadcasted_iota(jnp.int32, (BLK, BLK), 1)
                for i in range(per):
                    ss[i] = jnp.where(key <= jnp.where(a == i, lim, BLK), ss[i], NEG)
            top = ss[0]
            for s in ss[1:]:
                top = jnp.maximum(top, s)
            old = m_ref[take, :1]
            new = jnp.maximum(old, jnp.max(top, axis=1, keepdims=True) * C1)
            alpha = jnp.exp2(old - new)
            add = None
            for s, v in zip(ss, vs):
                term = jnp.dot(jnp.exp2(s * C1 - new).astype(BF), v, preferred_element_type=F32)
                add = term if add is None else add + term
            acc_ref[take, :] = acc_ref[take, :] * alpha + add
            m_ref[take, :] = jnp.broadcast_to(new, (BLK, HEAD))

    attend(me, True)

    @pl.loop(1, 8)
    def _(k):
        kk = lax.rem(k, 4)
        i, s = kk + kk // 2 - 2 * (kk // 3), k // 4

        @pl.when(k == 1)
        def _():
            keys.forward_pair()
            keys.forward(0)

        @pl.when(k == 2)
        def _():
            wide.forward_pair()
            wide.forward(0)

        @pl.when(k == 3)
        def _():
            keys.arrive(0)

        @pl.when(k == 5)
        def _():
            keys.forward(1)
            wide.forward(1)
            ups.start()

        @pl.when(k == 7)
        def _():
            keys.arrive(1)

        attend(gd.index(gd.ring(i), gd.p + s * (1 - 2 * gd.p)), False)

    for a in range(per):
        at = slice(a * BLK, (a + 1) * BLK)
        total = acc_ref[at, HEAD:]
        o_ref[at, :] = (acc_ref[at, :HEAD] / total).astype(BF)
        lse_ref[a:a + 1, :] = jnp.transpose(m_ref[at, :] + jnp.log2(total))[:1, :]
    head = pl.ds(pl.multiple_of((2 * t + c) * HEAD, HEAD), HEAD)
    copies = []
    for k, (tt, cc, device) in enumerate(members):
        take = pl.ds(pl.multiple_of(cc * own + tt * small, small), small)
        copies.append(send(o_ref.at[take], mixed.at[:, head], asem, k, device))
    copies.append(send(o_ref.at[pl.ds(pl.multiple_of((1 - c) * own, own), own)], own_out.at[:, local], asem, 15, core))
    keys.settle()
    save = pltpu.make_async_copy(kv_vm, kv_hbm, lsem.at[2])
    save.start()
    saves.append(save)
    downs.start()
    mixed[:, head] = o_ref[pl.ds(pl.multiple_of(c * own + t * small, small), small), :]
    own_out[:, local] = o_ref[pl.ds(pl.multiple_of(c * own, own), own), :]
    ups.forward_pair()
    ups.forward(0)
    wide.arrive(0)
    wide.arrive(1)
    wide.settle()
    save = pltpu.make_async_copy(out_vm, out_hbm, lsem.at[3])
    save.start()
    saves.append(save)
    for copy in copies:
        copy.wait_recv()
    span = 512
    x_rows = pl.ds(pl.multiple_of(t * small, small), small)
    for n in range(mid_out.shape[1] // span):
        cols = pl.ds(n * span, span)
        total = None
        for k in range(8):
            term = dg(mixed[:, k * 256:(k + 1) * 256], out_vm[k, cols, :], NT)
            total = term if total is None else total + term
        mid_out[:, cols] = total + (x_ref[x_rows, cols].astype(F32) + bias_ref[:, cols])
    scaled, _ = norm_rows(mid_out[...])
    n2_out[t] = (scaled * gain2_ref[...] + shift2_ref[...]).astype(BF)
    normed.start()
    ups.forward(1)
    downs.forward_pair()
    downs.forward(0)
    normed.forward_pair()
    normed.forward(0)
    ups.arrive(0)
    ups.arrive(1)
    ups.settle()
    save = pltpu.make_async_copy(up_vm, up_hbm, lsem.at[4])
    save.start()
    saves.append(save)
    normed.forward(1)
    downs.forward(1)
    downs.arrive(0)
    downs.arrive(1)
    downs.settle()
    save = pltpu.make_async_copy(down_vm, down_hbm, lsem.at[5])
    save.start()
    saves.append(save)
    normed.arrive(0)
    normed.arrive(1)
    normed.settle()
    qkv.settle()
    swap.wait_send()
    for copy in there + copies:
        copy.wait_send()
    for save in saves:
        save.wait()


def forward_call(meta, lanes, x, gain1, shift1, wq, wk, wv, qb, vb, wo, wu, wd, bias, gain2, shift2):
    own, width = x.shape
    rows, shard, hid, small = 2 * own, wq.shape[0], wu.shape[1], own // 8
    hbm = pl.BlockSpec(memory_space=pl.ANY)
    big = [(width, 3 * HEAD), (2, own, width), (8, rows, 2 * HEAD), (8, width, 2 * HEAD), (width, hid), (width, hid)]
    w, n, kv, out, up, down = (struct(s, BF) for s in big)
    outs = (w, n, struct((rows, HEAD), BF), kv, struct((rows, HEAD), BF), struct((rows // BLK, BLK), F32), out, up, down,
            struct((8, small, width), BF), struct((small, width), F32), struct((own, 2 * HEAD), BF))
    return remote_call(
        forward_kernel, "forward", 1, outs, [SM] + [VM] * 15,
        [pltpu.VMEM(s, BF) for s in big]
        + [pltpu.VMEM((2, shard, 3 * HEAD), BF), pltpu.VMEM((rows, 2 * HEAD), BF), pltpu.VMEM((8 * rows, HEAD), BF),
           pltpu.VMEM((rows, HEAD), F32), pltpu.VMEM((rows, 2 * HEAD), F32), pltpu.VMEM((small, width), BF),
           DMA((6,)), DMA((3,)), DMA((3,)), DMA((16,)), DMA((16,))]
        + Gather.scratch() * 2 + Gather.scratch(True) * 4 + Gather.scratch(),
        meta, lanes, x, gain1, shift1, wq, wk, wv, qb, vb, wo, wu, wd, bias, gain2, shift2,
        out_specs=(hbm, hbm, VM, hbm, VM, VM, hbm, hbm, hbm, VM, VM, VM))


def attend_back_kernel(meta, lanes_ref, q_ref, kv_ref, o_ref, do_ref, lse_ref, opart_ref, gbr_ref, mid_ref, bias_ref, dup_ref,
                       dq_ref, dkv_out, lay_out, gb_out, dup_out,
                       qa_ref, kx_ref, part, delta_ref, dq_acc, *scratch):
    g, gt = Eight("dp"), Eight("tensor")
    core = other_core()
    me = g.index(g.r, g.p)
    rows = q_ref.shape[0]
    nblk = kx_ref.shape[0] // BLK
    per = rows // BLK
    greet(g.others() + gt.others() + [core])
    keys = Scatter(g, lambda m: part.at[m], rows, scratch[:7], 128)
    outs = Scatter(gt, lambda m: opart_ref.at[m], opart_ref.shape[1], scratch[7:14], 32)
    ups = CoreScatter(g, dup_ref, scratch[14:25], 32)
    wide = Gather(gt, lambda m: gb_out.at[m], gb_out.shape[1], scratch[25:27])
    layer = Gather(gt, lambda m: lay_out.at[m], lay_out.shape[1], scratch[27:29])
    ups.start()
    outs.start()
    mine_t = gt.index(gt.r, gt.p)
    gb_out[mine_t] = gbr_ref[...]
    wide.start()
    augment(meta, lanes_ref, q_ref, qa_ref, kx_ref)
    for a in range(per):
        at = slice(a * BLK, (a + 1) * BLK)
        prod = do_ref[at, :].astype(F32) * o_ref[at, :].astype(F32)
        delta_ref[0:1, at] = jnp.sum(jnp.transpose(prod), axis=0, keepdims=True)
        delta_ref[1:2, at] = lse_ref[a:a + 1, :]
    dq_acc[...] = jnp.zeros_like(dq_acc)
    prefix = meta[nblk]

    def attend(chunk, own):
        @pl.loop(0, per)
        def _(i):
            at_k = pl.ds(pl.multiple_of(i * BLK, BLK), BLK)
            at_x = pl.ds(pl.multiple_of(chunk * rows + i * BLK, BLK), BLK)
            k = kv_ref[chunk, at_k, :HEAD]
            v = kv_ref[chunk, at_k, HEAD:]
            kk = jnp.concatenate([k, kx_ref[at_x, :]], axis=1)
            dk = dv = None
            for a in range(per):
                at_q = slice(a * BLK, (a + 1) * BLK)
                q = q_ref[at_q, :]
                do = do_ref[at_q, :]
                p = jnp.exp2(dg(kk, qa_ref[at_q, :], NT) * C1 - delta_ref[1:2, at_q])
                if own:
                    edge = prefix - 1 - meta[first_block() + a] * BLK
                    lim = jnp.maximum(lax.broadcasted_iota(jnp.int32, (BLK, BLK), 1), edge)
                    key = lax.broadcasted_iota(jnp.int32, (BLK, BLK), 0)
                    p = jnp.where(key <= jnp.where(i == a, lim, BLK), p, 0.0)
                ds = (p * (dg(v, do, NT) - delta_ref[0:1, at_q])).astype(BF)
                tv = jnp.dot(p.astype(BF), do, preferred_element_type=F32)
                tk = jnp.dot(ds, q, preferred_element_type=F32)
                dv = tv if dv is None else dv + tv
                dk = tk if dk is None else dk + tk
                dq_acc[at_q, :] += dg(ds, k, TN)
            part[chunk, at_k, :HEAD] = (dk * SCALE).astype(BF)
            part[chunk, at_k, HEAD:] = dv.astype(BF)

    @pl.loop(0, 7)
    def _(k):
        kk = lax.rem(k, 3)
        i = (2 - kk + 3 * (kk // 2)) * (1 - k // 6)
        s = 1 - k // 3 + 2 * (k // 6)
        attend(g.index(g.ring(i), g.p + s * (1 - 2 * g.p)), False)

        @pl.when(k == 0)
        def _():
            keys.send_far(1)
            ups.add()

        @pl.when(k == 1)
        def _():
            wide.forward_pair()
            wide.forward(0)
            outs.add_near(1)

        @pl.when(k == 2)
        def _():
            keys.send_near(1)
            keys.add_near(1)
            outs.add_near(0)

        @pl.when(k == 3)
        def _():
            keys.send_far(0)
            outs.add_pair()
            wide.forward(1)

        @pl.when(k == 4)
        def _():
            ups.inner.add_near(1)
            ups.inner.add_near(0)

        @pl.when(k == 5)
        def _():
            keys.send_near(0)
            keys.add_near(0)

        @pl.when(k == 6)
        def _():
            keys.add_pair()

    def lay(at, value):
        lay_out[mine_t, at, :] = (mid_ref[at, :] + (value + bias_ref[...])).astype(BF)

    outs.finish(lay)
    layer.start()
    ups.inner.add_pair()
    attend(me, True)
    dq_ref[...] = (dq_acc[...] * SCALE).astype(BF)
    layer.forward_pair()
    layer.forward(0)
    wide.arrive(0)
    wide.arrive(1)
    wide.settle()

    def keep(at, value):
        dkv_out[at, :] = value.astype(BF)

    keys.finish(keep)
    layer.forward(1)

    def keep_up(at, value):
        dup_out[at, :] = value

    ups.finish(keep_up)
    layer.arrive(0)
    layer.arrive(1)
    layer.settle()


def attend_back_call(meta, lanes, q, kv, o, do, lse, opart, gb, mid, bias, dup):
    rows = q.shape[0]
    tr, width = mid.shape
    sr, sw = dup.shape[2:]
    return remote_call(
        attend_back_kernel, "attend_back", 5,
        (struct(q.shape, BF), struct((rows, 2 * HEAD), BF), struct((8, tr, width), BF), struct((8, tr, width), BF), struct((sr, sw), F32)),
        [SM] + [VM] * 11,
        [pltpu.VMEM((rows, 2 * HEAD), BF), pltpu.VMEM((8 * rows, HEAD), BF), pltpu.VMEM(kv.shape, BF), pltpu.VMEM((8, rows), F32),
         pltpu.VMEM((rows, HEAD), F32)]
        + Scatter.scratch(rows, 2 * HEAD) + Scatter.scratch(tr, width) + CoreScatter.scratch(sr, sw) + Gather.scratch() * 2,
        meta, lanes, q, kv, o, do, lse, opart, gb, mid, bias, dup)


def back_kernel(part_ref, mid_ref, g_ref, w_hbm, gain_ref, do_out, gm_out, sums_out, low_out,
                w_ref, total, heads, lsem, asems, arecv, *scratch):
    g = Eight("tensor")
    c = lax.rem(g.d, 2)
    members = chip_members()
    load = pltpu.make_async_copy(w_hbm, w_ref, lsem.at[0])
    load.start()
    greet([m[2] for m in members])
    rows = g_ref.shape[0]
    half = do_out.shape[0] // 2
    first = Scatter(g, lambda m: part_ref.at[m], rows, scratch, 32)
    first.start()
    first.forward()

    def keep(at, value):
        total[at, :] = value

    first.finish(keep)
    scaled, inverse = norm_rows(mid_ref[...])
    grad = total[...]
    gm = g_ref[...].astype(F32) + norm_back(grad, scaled, inverse, gain_ref[...])
    gm_out[...] = gm
    low = gm.astype(BF)
    low_out[...] = low
    load.wait()
    for t in range(8):
        heads[:, t * 256:(t + 1) * 256] = jnp.dot(low, w_ref[t], preferred_element_type=F32).astype(BF)
    sems = (asems, arecv)
    take = pl.ds(pl.multiple_of(c * half + g.t * rows, rows), rows)
    copies = []
    for k, (tt, cc, device) in enumerate(members):
        cols = pl.ds(pl.multiple_of((2 * tt + cc) * HEAD, HEAD), HEAD)
        copies.append(send(heads.at[:, cols], do_out.at[take], sems, k, device))
    do_out[take, :] = heads[:, pl.ds(pl.multiple_of((2 * g.t + c) * HEAD, HEAD), HEAD)]
    sums_out[...] = jnp.zeros_like(sums_out)
    sums_out[0:1, :] = jnp.sum(grad * scaled, axis=0, keepdims=True)
    sums_out[1:2, :] = jnp.sum(grad, axis=0, keepdims=True)
    sums_out[2:3, :] = jnp.sum(low.astype(F32), axis=0, keepdims=True)
    sums_out[3:4, :] = jnp.sum(g_ref[...].astype(F32), axis=0, keepdims=True)
    for copy in copies:
        copy.wait()


def back_call(part, mid, g, w, gain):
    rows, width = g.shape
    return remote_call(
        back_kernel, "back", 4,
        (struct((16 * rows, HEAD), BF), struct((rows, width), F32), struct((8, width), F32), struct((rows, width), BF)),
        [VM, VM, VM, pl.BlockSpec(memory_space=pl.ANY), VM],
        [pltpu.VMEM(w.shape, BF), pltpu.VMEM((rows, width), F32), pltpu.VMEM((rows, width), BF), DMA((1,)), DMA((15,)), DMA((15,))]
        + Scatter.scratch(rows, width),
        part, mid, g, w, gain)


class Sums:
    @staticmethod
    def scratch(count, rows, width):
        return [pltpu.VMEM((count, rows, width), F32), DMA((count - 1,)), DMA((count - 1,))]

    def __init__(self, axis, scratch):
        self.slots, self.sems = scratch[0], scratch[1:]
        self.count = self.slots.shape[0]
        self.axis = axis
        self.d, self.t = lax.axis_index("dp"), lax.axis_index("tensor")
        self.me = self.d if axis == "dp" else self.t

    def device(self, k):
        other = lax.rem(self.me + k, self.count)
        return (other, self.t) if self.axis == "dp" else (self.d, other)

    def copy(self, k):
        own = self.slots.at[self.me]
        return copy_of(own, own, self.sems, k - 1, self.device(k))

    def start(self):
        @pl.loop(1, self.count)
        def _(k):
            self.copy(k).start()

    def finish(self):
        @pl.loop(1, self.count)
        def _(k):
            self.copy(k).wait()
        total = self.slots[0]
        for k in range(1, self.count):
            total = total + self.slots[k]
        return total


def tail_kernel(dw_ref, part_ref, gm_ref, x_ref, gain_ref, ddown_ref, dout_ref, early_ref, lane_ref,
                dw_out, tg_out, ddown_out, dout_out, sums_out, lanes_out,
                summed, arrived, total, mine_w, css, crs, ss, rs, *scratch):
    dp, g = Eight("dp"), Eight("tensor")
    c = lax.rem(g.d, 2)
    core = other_core()
    everyone = [Sums("dp", [scratch[-3], None, None]).device(k) for k in range(1, 16)]
    everyone += [Sums("tensor", [scratch[-6], None, None]).device(k) for k in range(1, 8)]
    greet(everyone)
    csems = (css, crs)
    weights = Scatter(dp, lambda m: dw_ref.at[m], dw_ref.shape[1], scratch[:7], 128)
    tokens = Scatter(g, lambda m: summed.at[m], x_ref.shape[0], scratch[7:14], 32)
    downs = CoreScatter(dp, ddown_ref, scratch[14:25], 32)
    outs = CoreScatter(dp, dout_ref, scratch[25:36], 128)
    early_t, lanes_d, late_t, all_d = (
        Sums("tensor", scratch[36:39]), Sums("dp", scratch[39:42]), Sums("tensor", scratch[42:45]), Sums("dp", scratch[45:48]))
    swap = send(part_ref.at[1 - c], arrived, csems, 0, core)
    weights.start()
    downs.start()
    outs.start()
    early_t.slots[g.t] = early_ref[...]
    early_t.start()
    lanes_d.slots[g.d] = lane_ref[...]
    lanes_d.start()
    swap.wait_recv()
    rows, width = x_ref.shape

    @pl.loop(0, 8)
    def _(t):
        @pl.loop(0, rows // 32)
        def _(n):
            at = pl.ds(pl.multiple_of(n * 32, 32), 32)
            summed[t, at, :] = (part_ref[c, t, at, :].astype(F32) + arrived[t, at, :].astype(F32)).astype(BF)

    tokens.start()
    downs.add()
    outs.add()
    tokens.forward()
    weights.forward()

    def keep(at, value):
        total[at, :] = value

    tokens.finish(keep)
    scaled, inverse = norm_rows(x_ref[...].astype(F32))
    grad = total[...]
    tg = gm_ref[...] + norm_back(grad, scaled, inverse, gain_ref[...])
    tg_out[g.index(g.r, g.p)] = tg.astype(BF)
    gather = Gather(g, lambda m: tg_out.at[m], rows, (ss, rs))
    gather.start()
    late_t.slots[g.t] = jnp.zeros(late_t.slots.shape[1:], F32)
    late_t.slots[g.t, 0:1, :] = jnp.sum(grad * scaled, axis=0, keepdims=True)
    late_t.slots[g.t, 1:2, :] = jnp.sum(grad, axis=0, keepdims=True)
    late_t.start()
    downs.forward()
    outs.forward()
    all_d.slots[g.d, 8:16, :] = early_t.finish()
    all_d.slots[g.d, 0:8, :] = late_t.finish()
    all_d.start()

    def keep_w(at, value):
        mine_w[at, :] = value.astype(BF)

    weights.finish(keep_w)
    share = dw_out.shape[1]
    there = send(mine_w.at[pl.ds(pl.multiple_of((1 - c) * share, share), share)], dw_out.at[c], csems, 1, core)
    dw_out[c] = mine_w[pl.ds(pl.multiple_of(c * share, share), share), :]
    gather.forward_pair()
    gather.forward(0)

    def keep_down(at, value):
        ddown_out[at, :] = value

    downs.finish(keep_down)

    def keep_out(at, value):
        dout_out[at, :] = value

    outs.finish(keep_out)
    gather.forward(1)
    lanes_out[...] = lanes_d.finish()
    sums_out[...] = all_d.finish()
    gather.arrive(0)
    gather.arrive(1)
    gather.settle()
    there.wait()
    swap.wait_send()


def tail_call(dw, part, gm, x, gain, ddown, dout, early, lane):
    rows, width = x.shape
    wr, wc = dw.shape[1:]
    return remote_call(
        tail_kernel, "tail", 6,
        (struct((2, wr // 2, wc), BF), struct((8, rows, width), BF), struct(ddown.shape[2:], F32), struct(dout.shape[2:], F32),
         struct((16, width), F32), struct(lane.shape, F32)),
        [VM] * 9,
        [pltpu.VMEM((8, rows, width), BF), pltpu.VMEM((8, rows, width), BF), pltpu.VMEM((rows, width), F32), pltpu.VMEM((wr, wc), BF),
         DMA((2,)), DMA((2,)), DMA((9,)), DMA((9,))] + Scatter.scratch(wr, wc) + Scatter.scratch(rows, width)
        + CoreScatter.scratch(*ddown.shape[2:]) + CoreScatter.scratch(*dout.shape[2:])
        + Sums.scratch(8, *early.shape) + Sums.scratch(16, *lane.shape) + Sums.scratch(8, 8, width) + Sums.scratch(16, 16, width),
        dw, part, gm, x, gain, ddown, dout, early, lane)


def on_device(tokens, first_gain, first_shift, query_weight, query_bias, key_weight, value_weight, value_bias,
              out_weight, out_bias, second_gain, second_shift, up_weight, up_bias, down_weight, down_bias,
              cotangent, prefix, block_order):
    own, width = tokens.shape
    d, t = lax.axis_index("dp"), lax.axis_index("tensor")
    c = lax.rem(d, 2)
    nblk = block_order.shape[0]
    rows = own // 8
    meta = jnp.concatenate([block_order % nblk, prefix])
    lanes = jnp.pad(block_order % nblk, (0, HEAD - nblk), constant_values=-1).reshape(1, HEAD)
    row = lambda v: v.reshape(1, -1)

    w_all, n_all, q, kv, o, lse, out_all, up_all, down_all, n2, mid, mixed = forward_call(
        meta, lanes, tokens, row(first_gain), row(first_shift), query_weight, key_weight, value_weight, row(query_bias), row(value_bias),
        out_weight, up_weight, down_weight, row(out_bias), row(second_gain), row(second_shift))
    n_all = n_all.reshape(2 * own, width)
    here = lambda v: lax.dynamic_slice_in_dim(v, t * rows, rows)
    x_rows, g_rows = here(tokens), here(cotangent)
    n2 = n2.reshape(own, width)
    pre = dg(n2, up_all, NN) + up_bias
    half_erf = 0.5 + 0.5 * lax.erf(pre * math.sqrt(0.5))
    hidden = (pre * half_erf).astype(BF)
    slope = half_erf + pre * jnp.exp(-0.5 * pre * pre) * (1.0 / math.sqrt(2.0 * math.pi))
    grad_pre = (dg(cotangent, down_all, NN) * slope).astype(BF)
    gn2 = dg(grad_pre, up_all, NT).astype(BF).reshape(8, rows, width)
    out_part = dg(hidden, down_all, NT).astype(BF).reshape(8, rows, width)
    do, gm, sums, low = back_call(gn2, mid, g_rows, out_all, row(second_gain))
    hid = up_weight.shape[1]
    dw_up = dg(n2, grad_pre, TN).astype(BF).reshape(8, 2, width // 16, hid)
    dw_down = dg(cotangent, hidden, TN).astype(BF).reshape(8, 2, width // 16, hid)
    dq, dkv, layer, gb, up_grad = attend_back_call(meta, lanes, q, kv, o, do, lse, out_part, low, mid, row(down_bias), dw_up)
    dw_out = dg(gb.reshape(own, width), mixed, TN).astype(BF).reshape(8, 2, width // 16, 2 * HEAD)

    dqkv = jnp.concatenate([dq, dkv], axis=1)
    dw = dg(n_all, dqkv, TN).astype(BF).reshape(8, width // 8, 3 * HEAD)
    gn1 = dg(dqkv, w_all, NT).astype(BF).reshape(2, 8, rows, width)
    col = jnp.sum(dqkv.astype(F32), axis=0)
    zero = jnp.zeros((HEAD,), F32)
    two = lambda v: jnp.concatenate([jnp.where(c == 0, v, zero), jnp.where(c == 1, v, zero)])
    lane = jnp.concatenate([jnp.sum(grad_pre.astype(F32), axis=0), two(col[:HEAD]), two(col[2 * HEAD:])])
    lane = jnp.pad(lane.reshape(1, -1), ((0, 7), (0, 0)))
    dw_mine, tg, down_grad, out_grad, small, lane = tail_call(
        dw, gn1, gm, x_rows, row(first_gain), dw_down, dw_out, sums, lane)
    pieces = [
        jnp.concatenate([dw_mine[0, :, i * HEAD:(i + 1) * HEAD], dw_mine[1, :, i * HEAD:(i + 1) * HEAD]], axis=1).astype(F32)
        for i in range(3)]
    return (
        layer.reshape(own, width),
        tg.reshape(own, width).astype(F32),
        small[0], small[1],
        pieces[0], lane[0, hid:hid + 2 * HEAD], pieces[1], pieces[2], lane[0, hid + 2 * HEAD:],
        out_grad.T, small[10],
        small[8], small[9],
        up_grad, lane[0, :hid],
        down_grad.T, small[11],
    )


def solution(mesh):
    rows, cols = P("dp", "tensor"), P("tensor", "dp")
    return jax.shard_map(
        on_device,
        mesh=mesh,
        in_specs=(
            P("dp", None), P(), P(), rows, P("tensor"), rows, rows, P("tensor"), cols, P(), P(), P(), rows, P("tensor"),
            cols, P(), P("dp", None), P(), P()),
        out_specs=(
            P("dp", None), P("dp", None), P(), P(), rows, P("tensor"), rows, rows, P("tensor"), cols, P(), P(), P(), rows,
            P("tensor"), cols, P()),
        check_vma=False,
    )
```

time: 576 us -> 422 us (0.73); the launches traced: 565 us -> 418 us
  Pallas kernels: 479 us -> 353 us
  other arithmetic: 16.7 us -> 7.73 us
  matrix products: 43.9 us -> 35.9 us
    pallas_call x6 -> x4, Pallas kernels: 479 us -> 353 us  [remote_call(): pl.pallas_call(kernel, out_shape=outs, in_specs=ins, out_specs=jax.tree.m...]
    dot_general x10 -> x9, matrix products: 43.9 us -> 35.9 us  [dg(): return lax.dot_general(a, b, dims, preferred_element_type=F32)]
where the time goes in v3:
time: 422 us; the launch traced here: 418 us
  Pallas kernels  353 us (84%)
  matrix products  35.9 us (9%)
  local copies, waits for them, and re-layouts  20.6 us (5%)
  other arithmetic  7.73 us (2%)
    pallas_call x4, Pallas kernels, remote_call(): pl.pallas_call(kernel, out_shape=outs, in_specs=ins, out_specs=jax.tree.m...  353 us
    dot_general x9, matrix products, dg(): return lax.dot_general(a, b, dims, preferred_element_type=F32)  35.9 us

profile of v3, /device:TPU:1, one launch (start us, length us, event | category | flops | bytes accessed | tf_op | source)
XLA Modules:
  0.0 418.4 jit_solution(18183209570206521905)
XLA Ops:
  0.7 0.7 and_select_fusion
  2.0 0.6 pad_add_fusion.meta
  2.6 0.5 pad_bitcast_fusion.lanes_ref
  3.1 135.5 %forward.1 = (bf16[2048,384]{1,0:T(8,128)(2,1)}, bf16[2,512,2048]{2,1,0:T(8,128)(2,1)}, bf16[1024,128]{1,0:T(8,128)(2,1)}, bf16[8,1024,256]{2,1,0:T(8,128)(2,1)}...) custom-call(s32[33]{0:T(128)} %pad_add_fusion.meta, ...), custom_call_target="tpu_custom_call" | custom-call | tf_op jit(solution)/shard_map/forward/pallas_call | solution.py:331
  138.6 0.0 copy-start.4
  138.6 0.0 copy-start.6
  138.6 0.0 copy-start.12
  138.6 5.3 %fusion.9 = f32[512,1024]{1,0:T(8,128)S(1)} fusion(bf16[512,2048]{1,0:T(8,128)(2,1)} %bitcast.98, bf16[2048,1024]{1,0:T(8,128)(2,1)} %get-tuple-element.49), kind=kOutput, calls=%fused_computation.49 | convolution fusion | flops 2147483648 | bytes 8388608 | tf_op jit(solution)/shard_map/dot_general | solution.py:32
  143.9 0.0 copy-start.13
  143.9 0.0 copy-done.4
  143.9 0.0 copy-done.6
  143.9 0.0 copy-done.12
  143.9 0.0 copy-start.8
  143.9 3.0 convert_reduce_fusion
  146.9 0.0 copy-done.13
  146.9 0.0 copy-done.8
  147.0 3.7 convolution_convert_fusion.3
  150.7 1.8 constant_dynamic-slice_fusion
  152.4 0.0 copy-start.9
  152.4 37.0 %back.1 = (bf16[1024,128]{1,0:T(8,128)(2,1)}, f32[64,2048]{1,0:T(8,128)}, f32[8,2048]{1,0:T(8,128)}, bf16[64,2048]{1,0:T(8,128)(2,1)}) custom-call(bf16[8,64,2048]{2,1,0:T(8,128)(2,1)} %bitcast.70, f32[64,2048]{1,0:T(8,128)} %get-tuple-element.50.mid_ref, bf16[64,2048]{1,0:T(8,128)(2,1)} %get-tuple-element.105.g_ref, ...), custom_call_target="tpu_custom_call" | custom-call | tf_op jit(solution)/shard_map/back/pallas_call | solution.py:331
  189.4 0.0 copy-done.9
  189.4 0.0 copy-start.7
  189.5 0.0 copy-start.14
  189.5 4.4 %convolution_convert_fusion.1 = bf16[2048,1024]{1,0:T(8,128)(2,1)} fusion(bf16[512,2048]{1,0:T(8,128)(2,1)S(1)} %bitcast.99, bf16[512,1024]{1,0:T(8,128)(2,1)S(1)} %get-tuple-element.103), kind=kOutput, calls=%fused_computation.2 | convolution fusion | flops 2149580800 | bytes 7340032 | tf_op jit(solution)/shard_map/dot_general | solution.py:32
  193.9 0.0 copy-done.7
  193.9 0.0 copy-done.14
  193.9 3.7 convolution_convert_fusion.2
  197.6 81.1 %attend_back.1 = (bf16[1024,128]{1,0:T(8,128)(2,1)}, bf16[1024,256]{1,0:T(8,128)(2,1)}, bf16[8,64,2048]{2,1,0:T(8,128)(2,1)}, bf16[8,64,2048]{2,1,0:T(8,128)(2,1)}, f32[128,1024]{1,0:T(8,128)}) custom-call(s32[33]{0:T(128)} %pad_add_fusion.meta, s32[1,128]{1,0:T(1,128)} %pad_bitcast_fusion.lanes_ref, bf16[1024,128]{1,0:T(8,128)(2,1)} %get-tuple-element.44.q_ref, ...), custom_call_target="tpu_custom_call" | custom-call | tf_op jit(solution)/shard_map/attend_back/pallas_call | solution.py:331
  278.7 0.0 copy-start.11
  278.7 1.0 constant_dynamic-update-slice_fusion.1
  279.8 1.1 constant_dynamic-update-slice_fusion
  280.8 0.2 convert_reduce_fusion.1
  281.1 0.6 pad.9.lane_ref
  281.7 0.0 copy-done.11
  281.7 0.0 copy-start.10
  281.7 3.4 convolution_convert_fusion.5
  285.2 0.0 copy-done.10
  285.2 0.0 copy-start.5
  285.2 4.4 %convolution_convert_fusion = bf16[1024,2048]{1,0:T(8,128)(2,1)} fusion(bf16[1024,384]{1,0:T(8,128)(2,1)S(1)} %constant_dynamic-update-slice_fusion, bf16[2048,384]{1,0:T(8,128)(2,1)S(1)} %copy-done.10), kind=kOutput, calls=%fused_computation.1 | convolution fusion | flops 1612709888 | bytes 6553600 | tf_op jit(solution)/shard_map/dot_general | solution.py:32
  289.6 0.0 copy-done.5
  289.6 0.0 copy-start.15
  289.6 3.5 convolution_convert_fusion.4
  293.1 0.0 copy-done.15
  293.1 4.4 %convert_bitcast_fusion = bf16[2048,1024]{0,1:T(8,128)(2,1)} fusion(bf16[512,2048]{1,0:T(8,128)(2,1)S(1)} %copy-done.4, f32[512,1024]{1,0:T(8,128)S(1)} %copy-done.15, f32[1024]{0:T(1024)S(1)} %copy-done.12), kind=kOutput, calls=%fused_computation | convolution fusion | flops 2152726528 | bytes 8392704 | tf_op jit(solution)/shard_map/dot_general | solution.py:32
  297.5 6.4 %copy.36 = bf16[2048,1024]{1,0:T(8,128)(2,1)} copy(bf16[2048,1024]{0,1:T(8,128)(2,1)} %convert_bitcast_fusion) | data formatting | bytes 8388608 | tf_op jit(solution)/shard_map/convert_element_type | solution.py:999
  303.9 99.1 %tail.1 = (bf16[2,128,384]{2,1,0:T(8,128)(2,1)}, bf16[8,64,2048]{2,1,0:T(8,128)(2,1)}, f32[128,1024]{1,0:T(8,128)}, f32[128,256]{1,0:T(8,128)}, f32[16,2048]{1,0:T(8,128)}, /*index=5*/f32[8,1536]{1,0:T(8,128)}) custom-call(bf16[8,256,384]{2,1,0:T(8,128)(2,1)} %bitcast.73, bf16[2,8,64,2048]{3,2,1,0:T(8,128)(2,1)} %bitcast.68, ...), custom_call_target="tpu_custom_call" | custom-call | tf_op jit(solution)/shard_map/tail/pallas_call | solution.py:331
  403.0 0.9 slice_bitcast_fusion.1
  403.9 0.7 maximum_convert_fusion.2
  404.6 0.7 maximum_convert_fusion.1
  405.2 0.7 maximum_convert_fusion
  405.9 0.0 copy-start.2
  405.9 0.0 copy-start.3
  405.9 4.3 %bitcast_convert_fusion = f32[512,2048]{1,0:T(8,128)} fusion(bf16[8,64,2048]{2,1,0:T(8,128)(2,1)} %get-tuple-element.64), kind=kLoop, calls=%fused_computation.14 | loop fusion | flops 1048576 | bytes 6291456 | tf_op jit(solution)/shard_map/convert_element_type | solution.py:1018
  410.2 0.0 copy-done.2
  410.2 1.0 copy.38
  411.2 0.0 copy-done.3
  411.2 0.8 copy.37
  411.9 1.6 fusion.7
  413.6 1.4 slice.66
  414.9 1.3 fusion.8
  416.2 0.0 copy-done
  416.2 1.3 copy.47
  417.5 0.1 copy-done.1
  417.6 0.8 copy.48
  (8 shorter events, 0.0 us)
Async XLA Ops:
  138.6 5.3 %copy-start.4 = (bf16[512,2048]{1,0:T(8,128)(2,1)S(1)}, bf16[512,2048]{1,0:T(8,128)(2,1)}, u32[]{:S(2)}) copy-start(bf16[512,2048]{1,0:T(8,128)(2,1)} %param.35) | copy-start | bytes 6291460
  138.6 5.3 %copy-start.6 = (bf16[2048,1024]{1,0:T(8,128)(2,1)S(1)}, bf16[2048,1024]{1,0:T(8,128)(2,1)}, u32[]{:S(2)}) copy-start(bf16[2048,1024]{1,0:T(8,128)(2,1)} %get-tuple-element.47) | copy-start | bytes 12582916
  138.6 5.3 %copy-start.12 = (f32[1024]{0:T(1024)S(1)}, f32[1024]{0:T(1024)}, u32[]{:S(2)}) copy-start(f32[1024]{0:T(1024)} %param.32) | copy-start | bytes 12292
  143.9 3.0 copy-start.13
  143.9 3.0 copy-start.8
  152.4 37.0 %copy-start.9 = (bf16[8,64,2048]{2,1,0:T(8,128)(2,1)S(1)}, bf16[8,64,2048]{2,1,0:T(8,128)(2,1)}, u32[]{:S(2)}) copy-start(bf16[8,64,2048]{2,1,0:T(8,128)(2,1)} %get-tuple-element.48) | copy-start | bytes 6291460
  189.4 4.4 %copy-start.7 = (bf16[2048,1024]{1,0:T(8,128)(2,1)S(1)}, bf16[2048,1024]{1,0:T(8,128)(2,1)}, u32[]{:S(2)}) copy-start(bf16[2048,1024]{1,0:T(8,128)(2,1)} %get-tuple-element.47) | copy-start | bytes 12582916
  189.5 4.4 %copy-start.14 = (f32[512,1024]{1,0:T(8,128)S(1)}, f32[512,1024]{1,0:T(8,128)}, u32[]{:S(2)}) copy-start(f32[512,1024]{1,0:T(8,128)} %copy-done.13) | copy-start | bytes 6291460
  278.7 3.0 copy-start.11
  281.7 3.4 copy-start.10
  285.2 4.4 %copy-start.5 = (bf16[2,512,2048]{2,1,0:T(8,128)(2,1)S(1)}, bf16[2,512,2048]{2,1,0:T(8,128)(2,1)}, u32[]{:S(2)}) copy-start(bf16[2,512,2048]{2,1,0:T(8,128)(2,1)} %get-tuple-element.56) | copy-start | bytes 12582916
  289.6 3.5 copy-start.15
  405.9 4.3 %copy-start.2 = (f32[128,1024]{1,0:T(8,128)S(1)}, f32[128,1024]{1,0:T(8,128)}, u32[]{:S(2)}) copy-start(f32[128,1024]{1,0:T(8,128)} %get-tuple-element.70) | copy-start | bytes 1572868
  405.9 5.3 %copy-start.3 = (f32[128,256]{1,0:T(8,128)S(1)}, f32[128,256]{1,0:T(8,128)}, u32[]{:S(2)}) copy-start(f32[128,256]{1,0:T(8,128)} %get-tuple-element.68) | copy-start | bytes 393220
  405.9 10.3 %copy-start = (bf16[8,64,2048]{2,1,0:T(8,128)(2,1)S(1)}, bf16[8,64,2048]{2,1,0:T(8,128)(2,1)}, u32[]{:S(2)}) copy-start(bf16[8,64,2048]{2,1,0:T(8,128)(2,1)} %get-tuple-element.55) | copy-start | bytes 6291460
  416.2 1.4 copy-start.1

commit v4 on v3

--- a/solution.py
+++ b/solution.py
@@ -176,19 +176,19 @@
 
 
 class Scatter:
-    COUNT = 9
+    COUNT = 6
 
     @staticmethod
     def scratch(rows, width):
         half = rows // 2
         return [
-            pltpu.VMEM((2, 2, half, width), BF), pltpu.VMEM((2, 2, half, width), BF), pltpu.VMEM((2, 2, rows, width), BF),
+            pltpu.VMEM((2, 2, half, width), BF), pltpu.VMEM((2, 2, rows, width), BF),
             pltpu.VMEM((rows, width), BF), pltpu.VMEM((rows, width), BF), DMA((13,)), DMA((13,))]
 
     def __init__(self, group, part, rows, scratch, step):
         self.g, self.part, self.step, self.rows = group, part, step, rows
-        self.mid, self.added, self.last, self.sum, self.end = scratch[:5]
-        self.sems = scratch[5:7]
+        self.mid, self.last, self.sum, self.end = scratch[:4]
+        self.sems = scratch[4:6]
         self.half = rows // 2
         self.halves = (pl.ds(0, self.half), pl.ds(self.half, self.half))
 
@@ -208,7 +208,7 @@
         return copy_of(self.at(1 + 2 * way, s).at[half], self.last.at[s, way, half], self.sems, 4 + 2 * s + way, self.to(way))
 
     def both(self, s, way):
-        return copy_of(self.added.at[s, way], self.last.at[s, way, self.halves[way]], self.sems, 8 + 2 * s + way, self.to(way))
+        return copy_of(self.mid.at[s, way], self.last.at[s, way, self.halves[way]], self.sems, 8 + 2 * s + way, self.to(way))
 
     def pair(self):
         return copy_of(self.sum, self.end, self.sems, 12, self.g.device(self.g.r, 1 - self.g.p))
@@ -237,7 +237,7 @@
             def add(at, n, way=way, mine=mine, base=base):
                 rows = pl.ds(at, n)
                 total = mine[pl.ds(base + at, n), :].astype(F32) + self.mid[s, way, rows, :].astype(F32)
-                self.added[s, way, rows, :] = total.astype(BF)
+                self.mid[s, way, rows, :] = total.astype(BF)
 
             self.by_rows(self.half, add)
             self.both(s, way).start()
@@ -289,42 +289,129 @@
 
 
 class CoreScatter:
+    COUNT = 9
+
     @staticmethod
     def scratch(rows, width):
-        return [pltpu.VMEM((8, rows, width), BF), pltpu.VMEM((8, rows, width), BF), DMA((1,)), DMA((1,))] + Scatter.scratch(rows, width)
-
-    def __init__(self, group, part, scratch, step):
-        self.part, self.arrived, self.added = part, scratch[0], scratch[1]
+        return [pltpu.VMEM((8, rows, width), BF), DMA((8,)), DMA((8,))] + Scatter.scratch(rows, width)
+
+    def __init__(self, group, part, rows, scratch, step):
+        self.part, self.total, self.sems = part, scratch[0], scratch[1:3]
         self.c = lax.rem(group.d, 2)
-        self.sems = scratch[2:4]
-        self.step = step
-        self.inner = Scatter(group, lambda m: self.added.at[m], part.shape[2], scratch[4:], step)
-
-    def swap(self):
-        return copy_of(self.part.at[:, 1 - self.c], self.arrived, self.sems, 0, other_core())
+        self.rows, self.step = rows, step
+        self.inner = Scatter(group, lambda m: self.total.at[m], rows, scratch[3:], step)
+
+    def swap(self, m):
+        return copy_of(self.part(m, 1 - self.c), self.total.at[m], self.sems, m, other_core())
 
     def start(self):
-        self.swap().start()
+        for m in range(8):
+            self.swap(m).start()
 
     def add(self):
-        self.swap().wait_recv()
-        rows, step = self.part.shape[2], self.step
+        step = self.step
 
         @pl.loop(0, 8)
         def _(m):
-            @pl.loop(0, rows // step)
+            self.swap(m).wait_recv()
+            mine = self.part(m, self.c)
+
+            @pl.loop(0, self.rows // step)
             def _(n):
                 at = pl.ds(pl.multiple_of(n * step, step), step)
-                self.added[m, at, :] = (self.part[m, self.c, at, :].astype(F32) + self.arrived[m, at, :].astype(F32)).astype(BF)
+                self.total[m, at, :] = (mine[at, :].astype(F32) + self.total[m, at, :].astype(F32)).astype(BF)
 
         self.inner.start()
-
-    def forward(self):
-        self.inner.forward()
 
     def finish(self, store):
         self.inner.finish(store)
-        self.swap().wait_send()
+        for m in range(8):
+            self.swap(m).wait_send()
+
+
+class RowSums:
+    @staticmethod
+    def scratch(width):
+        cols = width // 8
+        return [pltpu.VMEM((8, 8, cols), F32), pltpu.VMEM((16, 8, cols), F32)] + [DMA((7,)), DMA((7,)), DMA((15,)), DMA((15,)), DMA((7,)), DMA((7,))]
+
+    def __init__(self, rows, out, scratch):
+        self.rows, self.out = rows, out
+        self.one, self.two = scratch[:2]
+        self.sems = (scratch[2:4], scratch[4:6], scratch[6:8])
+        self.d, self.t = lax.axis_index("dp"), lax.axis_index("tensor")
+        self.cols = rows.shape[1] // 8
+
+    def columns(self, t):
+        return pl.ds(pl.multiple_of(t * self.cols, self.cols), self.cols)
+
+    def first(self, k):
+        other = lax.rem(self.t + k, 8)
+        return copy_of(self.rows.at[:, self.columns(other)], self.one.at[self.t], self.sems[0], k - 1, (self.d, other))
+
+    def second(self, k):
+        own = self.two.at[self.d]
+        return copy_of(own, own, self.sems[1], k - 1, (lax.rem(self.d + k, 16), self.t))
+
+    def third(self, k):
+        own = self.out.at[:, self.columns(self.t)]
+        return copy_of(own, own, self.sems[2], k - 1, (self.d, lax.rem(self.t + k, 8)))
+
+    def run(self, step, last):
+        @pl.loop(1, last)
+        def _(k):
+            step(k)
+
+    def start(self):
+        self.run(lambda k: self.first(k).start(), 8)
+        self.one[self.t] = self.rows[:, self.columns(self.t)]
+
+    def middle(self):
+        self.run(lambda k: self.first(k).wait(), 8)
+        total = self.one[0]
+        for k in range(1, 8):
+            total = total + self.one[k]
+        self.two[self.d] = total
+        self.run(lambda k: self.second(k).start(), 16)
+
+    def finish(self):
+        self.run(lambda k: self.second(k).wait(), 16)
+        total = self.two[0]
+        for k in range(1, 16):
+            total = total + self.two[k]
+        self.out[:, self.columns(self.t)] = total
+        self.run(lambda k: self.third(k).start(), 8)
+
+    def settle(self):
+        self.run(lambda k: self.third(k).wait(), 8)
+
+
+class Sums:
+    @staticmethod
+    def scratch(rows, width):
+        return [pltpu.VMEM((16, rows, width), F32), DMA((15,)), DMA((15,))]
+
+    def __init__(self, scratch):
+        self.slots, self.sems = scratch[0], scratch[1:3]
+        self.d, self.t = lax.axis_index("dp"), lax.axis_index("tensor")
+
+    def copy(self, k):
+        own = self.slots.at[self.d]
+        return copy_of(own, own, self.sems, k - 1, (lax.rem(self.d + k, 16), self.t))
+
+    def start(self):
+        @pl.loop(1, 16)
+        def _(k):
+            self.copy(k).start()
+
+    def finish(self):
+        @pl.loop(1, 16)
+        def _(k):
+            self.copy(k).wait()
+        total = self.slots[0]
+        for k in range(1, 16):
+            total = total + self.slots[k]
+        return total
 
 
 def remote_call(kernel, name, cid, outs, ins, scratch, *args, out_specs=None):
@@ -403,6 +490,7 @@
     per = rows // BLK
     shard = wq_ref.shape[0]
     half = out_vm.shape[1] // 2
+    hid = wd_ref.shape[0]
     small = mid_out.shape[0]
     csem, asem = (css, crs), (ass, ars)
     for h in range(2):
@@ -418,14 +506,14 @@
     w_vm[mine, :] = wsh[c]
     qkv = Gather(gd, w_place, 2 * shard, sems[0:2])
     keys = Gather(gd, lambda m: kv_vm.at[m], rows, sems[2:4])
-    outs = Gather(gd, lambda m: out_vm.at[t, row_of(m)], shard, sems[4:8], core)
+    outs = Gather(gd, lambda m: out_vm.at[t, :, row_of(m)], 2 * half, sems[4:8], core)
     ups = Gather(gd, lambda m: up_vm.at[row_of(m)], shard, sems[8:12], core)
-    downs = Gather(gd, lambda m: down_vm.at[row_of(m)], shard, sems[12:16], core)
+    downs = Gather(gd, lambda m: down_vm.at[:, row_of(m)], hid, sems[12:16], core)
     wide = Gather(gt, lambda m: out_vm.at[m, pl.ds(pl.multiple_of(c * half, half), half)], half, sems[16:20], core, twin_own=False)
     normed = Gather(gt, lambda m: n2_out.at[m], small, sems[20:22])
     swap.wait_recv()
     qkv.start()
-    out_vm[t, mine, :] = jnp.transpose(wo_ref[...]).astype(BF)
+    out_vm[t, :, mine] = wo_ref[...].astype(BF)
     outs.start()
 
     def norm_part(k):
@@ -451,7 +539,7 @@
     qkv.forward(1)
     up_vm[mine, :] = wu_ref[...].astype(BF)
     outs.arrive(1)
-    down_vm[mine, :] = jnp.transpose(wd_ref[...]).astype(BF)
+    down_vm[:, mine] = wd_ref[...].astype(BF)
     outs.settle()
     wide.start()
     qkv.arrive(0)
@@ -575,7 +663,7 @@
         cols = pl.ds(n * span, span)
         total = None
         for k in range(8):
-            term = dg(mixed[:, k * 256:(k + 1) * 256], out_vm[k, cols, :], NT)
+            term = dg(mixed[:, k * 256:(k + 1) * 256], out_vm[k, :, cols], NN)
             total = term if total is None else total + term
         mid_out[:, cols] = total + (x_ref[x_rows, cols].astype(F32) + bias_ref[:, cols])
     scaled, _ = norm_rows(mid_out[...])
@@ -615,7 +703,7 @@
     own, width = x.shape
     rows, shard, hid, small = 2 * own, wq.shape[0], wu.shape[1], own // 8
     hbm = pl.BlockSpec(memory_space=pl.ANY)
-    big = [(width, 3 * HEAD), (2, own, width), (8, rows, 2 * HEAD), (8, width, 2 * HEAD), (width, hid), (width, hid)]
+    big = [(width, 3 * HEAD), (2, own, width), (8, rows, 2 * HEAD), (8, 2 * HEAD, width), (width, hid), (hid, width)]
     w, n, kv, out, up, down = (struct(s, BF) for s in big)
     outs = (w, n, struct((rows, HEAD), BF), kv, struct((rows, HEAD), BF), struct((rows // BLK, BLK), F32), out, up, down,
             struct((8, small, width), BF), struct((small, width), F32), struct((own, 2 * HEAD), BF))
@@ -630,25 +718,127 @@
         out_specs=(hbm, hbm, VM, hbm, VM, VM, hbm, hbm, hbm, VM, VM, VM))
 
 
-def attend_back_kernel(meta, lanes_ref, q_ref, kv_ref, o_ref, do_ref, lse_ref, opart_ref, gbr_ref, mid_ref, bias_ref, dup_ref,
-                       dq_ref, dkv_out, lay_out, gb_out, dup_out,
-                       qa_ref, kx_ref, part, delta_ref, dq_acc, *scratch):
+def back_kernel(part_ref, mid_ref, g_hbm, w_hbm, gain_ref, dd_ref, do_out, gm_out, sums_out, low_out, dd_out,
+                w_ref, g_ref, total, heads, lsem, asems, arecv, *scratch):
+    g, gd = Eight("tensor"), Eight("dp")
+    c = lax.rem(g.d, 2)
+    members = chip_members()
+    rows = g_ref.shape[0]
+    loads = [pltpu.make_async_copy(w_hbm, w_ref, lsem.at[0]),
+             pltpu.make_async_copy(g_hbm.at[pl.ds(pl.multiple_of(g.t * rows, rows), rows)], g_ref, lsem.at[1])]
+    for load in loads:
+        load.start()
+    greet([m[2] for m in members] + gd.others())
+    half = do_out.shape[0] // 2
+    first = Scatter(g, lambda m: part_ref.at[m], rows, scratch, 32)
+    first.start()
+    share = dd_out.shape[1]
+    downs = CoreScatter(
+        gd, lambda m, cc: dd_ref.at[:, pl.ds(pl.multiple_of((m * 2 + cc) * share, share), share)], dd_out.shape[0], scratch[6:], 128)
+    downs.start()
+    first.add_near(1)
+    first.add_near(0)
+    first.add_pair()
+    downs.add()
+
+    def keep(at, value):
+        total[at, :] = value
+
+    first.finish(keep)
+    scaled, inverse = norm_rows(mid_ref[...])
+    grad = total[...]
+    for load in loads:
+        load.wait()
+    gm = g_ref[...].astype(F32) + norm_back(grad, scaled, inverse, gain_ref[...])
+    gm_out[...] = gm
+    low = gm.astype(BF)
+    low_out[...] = low
+    for t in range(8):
+        heads[:, t * 256:(t + 1) * 256] = dg(low, w_ref[t], NT).astype(BF)
+    sems = (asems, arecv)
+    take = pl.ds(pl.multiple_of(c * half + g.t * rows, rows), rows)
+    copies = []
+    for k, (tt, cc, device) in enumerate(members):
+        cols = pl.ds(pl.multiple_of((2 * tt + cc) * HEAD, HEAD), HEAD)
+        copies.append(send(heads.at[:, cols], do_out.at[take], sems, k, device))
+    do_out[take, :] = heads[:, pl.ds(pl.multiple_of((2 * g.t + c) * HEAD, HEAD), HEAD)]
+    downs.inner.add_near(1)
+    downs.inner.add_near(0)
+    sums_out[...] = jnp.zeros_like(sums_out)
+    sums_out[0:1, :] = jnp.sum(grad * scaled, axis=0, keepdims=True)
+    sums_out[1:2, :] = jnp.sum(grad, axis=0, keepdims=True)
+    sums_out[2:3, :] = jnp.sum(low.astype(F32), axis=0, keepdims=True)
+    sums_out[3:4, :] = jnp.sum(g_ref[...].astype(F32), axis=0, keepdims=True)
+    downs.inner.add_pair()
+
+    def keep_down(at, value):
+        dd_out[at, :] = value
+
+    downs.finish(keep_down)
+    for copy in copies:
+        copy.wait()
+
+
+def back_call(part, mid, g, w, gain, dd):
+    rows, width = mid.shape
+    hbm = pl.BlockSpec(memory_space=pl.ANY)
+    share = (dd.shape[0], dd.shape[1] // 16)
+    return remote_call(
+        back_kernel, "back", 4,
+        (struct((16 * rows, HEAD), BF), struct((rows, width), F32), struct((8, width), F32), struct((rows, width), BF), struct(share, F32)),
+        [VM, VM, hbm, hbm, VM, VM],
+        [pltpu.VMEM(w.shape, BF), pltpu.VMEM((rows, width), BF), pltpu.VMEM((rows, width), F32), pltpu.VMEM((rows, width), BF),
+         DMA((2,)), DMA((15,)), DMA((15,))] + Scatter.scratch(rows, width) + CoreScatter.scratch(*share),
+        part, mid, g, w, gain, dd)
+
+
+def rear_kernel(meta, lanes_ref, q_ref, kv_ref, o_ref, do_ref, lse_ref, opart_ref, gbr_ref, mid_ref, bias_ref, dup_ref,
+                mixed_ref, n_hbm, w_ref, gm_ref, x_hbm, gain_ref, early_ref, lane_ref,
+                lay_out, dup_out, dwo_out, dwq_out, dwk_out, dwv_out, tg_out, sums_out, lanes_out,
+                qa_ref, kx_ref, part, delta_ref, dq_acc, gb, dqkv, dwo, n_buf, dw, away, arrived, summed, total, mine_w, there_w, vec, x_ref,
+                lsem, css, crs, *scratch):
     g, gt = Eight("dp"), Eight("tensor")
+    c = lax.rem(g.d, 2)
     core = other_core()
-    me = g.index(g.r, g.p)
+    me, mine_t = g.index(g.r, g.p), gt.index(gt.r, gt.p)
     rows = q_ref.shape[0]
+    own = rows // 2
     nblk = kx_ref.shape[0] // BLK
     per = rows // BLK
-    greet(g.others() + gt.others() + [core])
-    keys = Scatter(g, lambda m: part.at[m], rows, scratch[:7], 128)
-    outs = Scatter(gt, lambda m: opart_ref.at[m], opart_ref.shape[1], scratch[7:14], 32)
-    ups = CoreScatter(g, dup_ref, scratch[14:25], 32)
-    wide = Gather(gt, lambda m: gb_out.at[m], gb_out.shape[1], scratch[25:27])
-    layer = Gather(gt, lambda m: lay_out.at[m], lay_out.shape[1], scratch[27:29])
+    small, width = mid_ref.shape
+    everyone = [(lax.rem(g.d + k, 16), g.t) for k in range(1, 16)] + [(g.d, lax.rem(g.t + k, 8)) for k in range(1, 8)]
+    greet(everyone)
+    take = list(scratch)
+
+    def some(count):
+        out = take[:count]
+        del take[:count]
+        return out
+
+    share = dwo_out.shape[1]
+    by_columns = lambda m, cc: dwo.at[:, pl.ds(pl.multiple_of((m * 2 + cc) * share, share), share)]
+    keys = Scatter(g, lambda m: part.at[m], rows, some(6), 128)
+    outs = Scatter(gt, lambda m: opart_ref.at[m], small, some(6), 32)
+    ups = CoreScatter(g, lambda m, cc: dup_ref.at[m, cc], dup_out.shape[0], some(9), 32)
+    dwos = CoreScatter(g, by_columns, dwo_out.shape[0], some(9), 128)
+    tokens = Scatter(gt, lambda m: summed.at[m], small, some(6), 32)
+    weights = Scatter(g, lambda m: dw.at[m], dw.shape[1], some(6), 128)
+    wide = Gather(gt, lambda m: gb.at[pl.ds(pl.multiple_of(m * small, small), small)], small, some(2))
+    layer = Gather(gt, lambda m: lay_out.at[m], small, some(2))
+    final = Gather(gt, lambda m: tg_out.at[m], small, some(2))
+    sums = RowSums(vec, sums_out, some(8))
+    lane_sums = Sums(some(3))
+    csem = (css, crs)
+    x_load = pltpu.make_async_copy(x_hbm.at[pl.ds(pl.multiple_of(g.t * small, small), small)], x_ref, lsem.at[2])
+    x_load.start()
+
+    def n_load(m):
+        slot = lax.rem(m, 2)
+        return pltpu.make_async_copy(n_hbm.at[:, pl.ds(pl.multiple_of(m * BLK, BLK), BLK)], n_buf.at[slot], lsem.at[slot])
+
     ups.start()
     outs.start()
-    mine_t = gt.index(gt.r, gt.p)
-    gb_out[mine_t] = gbr_ref[...]
+    gb[pl.ds(pl.multiple_of(mine_t * small, small), small), :] = gbr_ref[...]
     wide.start()
     augment(meta, lanes_ref, q_ref, qa_ref, kx_ref)
     for a in range(per):
@@ -659,7 +849,7 @@
     dq_acc[...] = jnp.zeros_like(dq_acc)
     prefix = meta[nblk]
 
-    def attend(chunk, own):
+    def attend(chunk, diagonal):
         @pl.loop(0, per)
         def _(i):
             at_k = pl.ds(pl.multiple_of(i * BLK, BLK), BLK)
@@ -673,7 +863,7 @@
                 q = q_ref[at_q, :]
                 do = do_ref[at_q, :]
                 p = jnp.exp2(dg(kk, qa_ref[at_q, :], NT) * C1 - delta_ref[1:2, at_q])
-                if own:
+                if diagonal:
                     edge = prefix - 1 - meta[first_block() + a] * BLK
                     lim = jnp.maximum(lax.broadcasted_iota(jnp.int32, (BLK, BLK), 1), edge)
                     key = lax.broadcasted_iota(jnp.int32, (BLK, BLK), 0)
@@ -698,28 +888,28 @@
         def _():
             keys.send_far(1)
             ups.add()
-
-        @pl.when(k == 1)
-        def _():
+            outs.add_near(1)
             wide.forward_pair()
             wide.forward(0)
-            outs.add_near(1)
+
+        @pl.when(k == 1)
+        def _():
+            outs.add_near(0)
 
         @pl.when(k == 2)
         def _():
             keys.send_near(1)
             keys.add_near(1)
-            outs.add_near(0)
-
-        @pl.when(k == 3)
-        def _():
-            keys.send_far(0)
             outs.add_pair()
             wide.forward(1)
 
+        @pl.when(k == 3)
+        def _():
+            keys.send_far(0)
+            ups.inner.add_near(1)
+
         @pl.when(k == 4)
         def _():
-            ups.inner.add_near(1)
             ups.inner.add_near(0)
 
         @pl.when(k == 5)
@@ -737,234 +927,153 @@
     outs.finish(lay)
     layer.start()
     ups.inner.add_pair()
+    n_load(0).start()
     attend(me, True)
-    dq_ref[...] = (dq_acc[...] * SCALE).astype(BF)
+    dqkv[:, :HEAD] = (dq_acc[...] * SCALE).astype(BF)
     layer.forward_pair()
     layer.forward(0)
     wide.arrive(0)
     wide.arrive(1)
     wide.settle()
-
-    def keep(at, value):
-        dkv_out[at, :] = value.astype(BF)
-
-    keys.finish(keep)
+    span = 512
+    for n in range(width // span):
+        cols = pl.ds(n * span, span)
+        dwo[:, cols] = dg(mixed_ref[...], gb[:, cols], TN).astype(BF)
+    dwos.start()
     layer.forward(1)
 
-    def keep_up(at, value):
-        dup_out[at, :] = value
-
-    ups.finish(keep_up)
-    layer.arrive(0)
-    layer.arrive(1)
-    layer.settle()
-
-
-def attend_back_call(meta, lanes, q, kv, o, do, lse, opart, gb, mid, bias, dup):
-    rows = q.shape[0]
-    tr, width = mid.shape
-    sr, sw = dup.shape[2:]
-    return remote_call(
-        attend_back_kernel, "attend_back", 5,
-        (struct(q.shape, BF), struct((rows, 2 * HEAD), BF), struct((8, tr, width), BF), struct((8, tr, width), BF), struct((sr, sw), F32)),
-        [SM] + [VM] * 11,
-        [pltpu.VMEM((rows, 2 * HEAD), BF), pltpu.VMEM((8 * rows, HEAD), BF), pltpu.VMEM(kv.shape, BF), pltpu.VMEM((8, rows), F32),
-         pltpu.VMEM((rows, HEAD), F32)]
-        + Scatter.scratch(rows, 2 * HEAD) + Scatter.scratch(tr, width) + CoreScatter.scratch(sr, sw) + Gather.scratch() * 2,
-        meta, lanes, q, kv, o, do, lse, opart, gb, mid, bias, dup)
-
-
-def back_kernel(part_ref, mid_ref, g_ref, w_hbm, gain_ref, do_out, gm_out, sums_out, low_out,
-                w_ref, total, heads, lsem, asems, arecv, *scratch):
-    g = Eight("tensor")
-    c = lax.rem(g.d, 2)
-    members = chip_members()
-    load = pltpu.make_async_copy(w_hbm, w_ref, lsem.at[0])
-    load.start()
-    greet([m[2] for m in members])
-    rows = g_ref.shape[0]
-    half = do_out.shape[0] // 2
-    first = Scatter(g, lambda m: part_ref.at[m], rows, scratch, 32)
-    first.start()
-    first.forward()
+    def keep_keys(at, value):
+        dqkv[at, HEAD:] = value.astype(BF)
+
+    keys.finish(keep_keys)
+
+    def project(into, half):
+        @pl.loop(0, own // BLK)
+        def _(b):
+            at = pl.ds(pl.multiple_of(half * own + b * BLK, BLK), BLK)
+            for n in range(width // span):
+                cols = pl.ds(n * span, span)
+                piece = dg(dqkv[at, :], w_ref[cols, :], NT).astype(BF)
+                for j in range(BLK // small):
+                    into[b * (BLK // small) + j, :, cols] = piece[j * small:(j + 1) * small]
+
+    project(away, 1 - c)
+    swap = send(away, arrived, csem, 0, core)
+    project(summed, c)
+    swap.wait_recv()
+
+    @pl.loop(0, 8)
+    def _(m):
+        @pl.loop(0, small // 32)
+        def _(n):
+            at = pl.ds(pl.multiple_of(n * 32, 32), 32)
+            summed[m, at, :] = (summed[m, at, :].astype(F32) + arrived[m, at, :].astype(F32)).astype(BF)
+
+    tokens.start()
+
+    @pl.loop(0, 8)
+    def _(m):
+        @pl.when(m < 7)
+        def _():
+            n_load(m + 1).start()
+
+        n_load(m).wait()
+        dw[m] = dg(n_buf[lax.rem(m, 2)], dqkv[...], TN).astype(BF)
+
+    weights.start()
+    dwos.add()
+    slot = lane_sums.slots
+    slot[g.d] = lane_ref[...]
+    local = pl.ds(pl.multiple_of(c * HEAD, HEAD), HEAD)
+    slot[g.d, 4:5, local] = jnp.sum(dqkv[:, :HEAD].astype(F32), axis=0, keepdims=True)
+    slot[g.d, 5:6, local] = jnp.sum(dqkv[:, 2 * HEAD:].astype(F32), axis=0, keepdims=True)
+    lane_sums.start()
+    tokens.add_near(1)
+    tokens.add_near(0)
+    tokens.add_pair()
+    weights.add_near(1)
+    weights.add_near(0)
+    dwos.inner.add_near(1)
+    dwos.inner.add_near(0)
 
     def keep(at, value):
         total[at, :] = value
 
-    first.finish(keep)
-    scaled, inverse = norm_rows(mid_ref[...])
-    grad = total[...]
-    gm = g_ref[...].astype(F32) + norm_back(grad, scaled, inverse, gain_ref[...])
-    gm_out[...] = gm
-    low = gm.astype(BF)
-    low_out[...] = low
-    load.wait()
-    for t in range(8):
-        heads[:, t * 256:(t + 1) * 256] = jnp.dot(low, w_ref[t], preferred_element_type=F32).astype(BF)
-    sems = (asems, arecv)
-    take = pl.ds(pl.multiple_of(c * half + g.t * rows, rows), rows)
-    copies = []
-    for k, (tt, cc, device) in enumerate(members):
-        cols = pl.ds(pl.multiple_of((2 * tt + cc) * HEAD, HEAD), HEAD)
-        copies.append(send(heads.at[:, cols], do_out.at[take], sems, k, device))
-    do_out[take, :] = heads[:, pl.ds(pl.multiple_of((2 * g.t + c) * HEAD, HEAD), HEAD)]
-    sums_out[...] = jnp.zeros_like(sums_out)
-    sums_out[0:1, :] = jnp.sum(grad * scaled, axis=0, keepdims=True)
-    sums_out[1:2, :] = jnp.sum(grad, axis=0, keepdims=True)
-    sums_out[2:3, :] = jnp.sum(low.astype(F32), axis=0, keepdims=True)
-    sums_out[3:4, :] = jnp.sum(g_ref[...].astype(F32), axis=0, keepdims=True)
-    for copy in copies:
-        copy.wait()
-
-
-def back_call(part, mid, g, w, gain):
-    rows, width = g.shape
-    return remote_call(
-        back_kernel, "back", 4,
-        (struct((16 * rows, HEAD), BF), struct((rows, width), F32), struct((8, width), F32), struct((rows, width), BF)),
-        [VM, VM, VM, pl.BlockSpec(memory_space=pl.ANY), VM],
-        [pltpu.VMEM(w.shape, BF), pltpu.VMEM((rows, width), F32), pltpu.VMEM((rows, width), BF), DMA((1,)), DMA((15,)), DMA((15,))]
-        + Scatter.scratch(rows, width),
-        part, mid, g, w, gain)
-
-
-class Sums:
-    @staticmethod
-    def scratch(count, rows, width):
-        return [pltpu.VMEM((count, rows, width), F32), DMA((count - 1,)), DMA((count - 1,))]
-
-    def __init__(self, axis, scratch):
-        self.slots, self.sems = scratch[0], scratch[1:]
-        self.count = self.slots.shape[0]
-        self.axis = axis
-        self.d, self.t = lax.axis_index("dp"), lax.axis_index("tensor")
-        self.me = self.d if axis == "dp" else self.t
-
-    def device(self, k):
-        other = lax.rem(self.me + k, self.count)
-        return (other, self.t) if self.axis == "dp" else (self.d, other)
-
-    def copy(self, k):
-        own = self.slots.at[self.me]
-        return copy_of(own, own, self.sems, k - 1, self.device(k))
-
-    def start(self):
-        @pl.loop(1, self.count)
-        def _(k):
-            self.copy(k).start()
-
-    def finish(self):
-        @pl.loop(1, self.count)
-        def _(k):
-            self.copy(k).wait()
-        total = self.slots[0]
-        for k in range(1, self.count):
-            total = total + self.slots[k]
-        return total
-
-
-def tail_kernel(dw_ref, part_ref, gm_ref, x_ref, gain_ref, ddown_ref, dout_ref, early_ref, lane_ref,
-                dw_out, tg_out, ddown_out, dout_out, sums_out, lanes_out,
-                summed, arrived, total, mine_w, css, crs, ss, rs, *scratch):
-    dp, g = Eight("dp"), Eight("tensor")
-    c = lax.rem(g.d, 2)
-    core = other_core()
-    everyone = [Sums("dp", [scratch[-3], None, None]).device(k) for k in range(1, 16)]
-    everyone += [Sums("tensor", [scratch[-6], None, None]).device(k) for k in range(1, 8)]
-    greet(everyone)
-    csems = (css, crs)
-    weights = Scatter(dp, lambda m: dw_ref.at[m], dw_ref.shape[1], scratch[:7], 128)
-    tokens = Scatter(g, lambda m: summed.at[m], x_ref.shape[0], scratch[7:14], 32)
-    downs = CoreScatter(dp, ddown_ref, scratch[14:25], 32)
-    outs = CoreScatter(dp, dout_ref, scratch[25:36], 128)
-    early_t, lanes_d, late_t, all_d = (
-        Sums("tensor", scratch[36:39]), Sums("dp", scratch[39:42]), Sums("tensor", scratch[42:45]), Sums("dp", scratch[45:48]))
-    swap = send(part_ref.at[1 - c], arrived, csems, 0, core)
-    weights.start()
-    downs.start()
-    outs.start()
-    early_t.slots[g.t] = early_ref[...]
-    early_t.start()
-    lanes_d.slots[g.d] = lane_ref[...]
-    lanes_d.start()
-    swap.wait_recv()
-    rows, width = x_ref.shape
-
-    @pl.loop(0, 8)
-    def _(t):
-        @pl.loop(0, rows // 32)
-        def _(n):
-            at = pl.ds(pl.multiple_of(n * 32, 32), 32)
-            summed[t, at, :] = (part_ref[c, t, at, :].astype(F32) + arrived[t, at, :].astype(F32)).astype(BF)
-
-    tokens.start()
-    downs.add()
-    outs.add()
-    tokens.forward()
-    weights.forward()
-
-    def keep(at, value):
-        total[at, :] = value
-
+    x_load.wait()
     tokens.finish(keep)
     scaled, inverse = norm_rows(x_ref[...].astype(F32))
     grad = total[...]
     tg = gm_ref[...] + norm_back(grad, scaled, inverse, gain_ref[...])
-    tg_out[g.index(g.r, g.p)] = tg.astype(BF)
-    gather = Gather(g, lambda m: tg_out.at[m], rows, (ss, rs))
-    gather.start()
-    late_t.slots[g.t] = jnp.zeros(late_t.slots.shape[1:], F32)
-    late_t.slots[g.t, 0:1, :] = jnp.sum(grad * scaled, axis=0, keepdims=True)
-    late_t.slots[g.t, 1:2, :] = jnp.sum(grad, axis=0, keepdims=True)
-    late_t.start()
-    downs.forward()
-    outs.forward()
-    all_d.slots[g.d, 8:16, :] = early_t.finish()
-    all_d.slots[g.d, 0:8, :] = late_t.finish()
-    all_d.start()
+    tg_out[mine_t] = tg.astype(BF)
+    final.start()
+    vec[...] = early_ref[...]
+    vec[4:5, :] = jnp.sum(grad * scaled, axis=0, keepdims=True)
+    vec[5:6, :] = jnp.sum(grad, axis=0, keepdims=True)
+    sums.start()
+    weights.add_pair()
+    dwos.inner.add_pair()
+
+    def keep_up(at, value):
+        dup_out[at, :] = value
+
+    ups.finish(keep_up)
+    sums.middle()
 
     def keep_w(at, value):
         mine_w[at, :] = value.astype(BF)
 
     weights.finish(keep_w)
-    share = dw_out.shape[1]
-    there = send(mine_w.at[pl.ds(pl.multiple_of((1 - c) * share, share), share)], dw_out.at[c], csems, 1, core)
-    dw_out[c] = mine_w[pl.ds(pl.multiple_of(c * share, share), share), :]
-    gather.forward_pair()
-    gather.forward(0)
-
-    def keep_down(at, value):
-        ddown_out[at, :] = value
-
-    downs.finish(keep_down)
-
-    def keep_out(at, value):
-        dout_out[at, :] = value
-
-    outs.finish(keep_out)
-    gather.forward(1)
-    lanes_out[...] = lanes_d.finish()
-    sums_out[...] = all_d.finish()
-    gather.arrive(0)
-    gather.arrive(1)
-    gather.settle()
+    part_rows = there_w.shape[0]
+    there = send(mine_w.at[pl.ds(pl.multiple_of((1 - c) * part_rows, part_rows), part_rows)], there_w, csem, 1, core)
+    final.forward_pair()
+    final.forward(0)
+    kept = mine_w[pl.ds(pl.multiple_of(c * part_rows, part_rows), part_rows), :].astype(F32)
+    sums.finish()
+    far = pl.ds(pl.multiple_of((1 - c) * HEAD, HEAD), HEAD)
     there.wait()
+    for i, ref in enumerate((dwq_out, dwk_out, dwv_out)):
+        ref[:, local] = kept[:, i * HEAD:(i + 1) * HEAD]
+        ref[:, far] = there_w[:, i * HEAD:(i + 1) * HEAD].astype(F32)
+    final.forward(1)
+    layer.arrive(0)
+    layer.arrive(1)
+    layer.settle()
+
+    def keep_o(at, value):
+        dwo_out[at, :] = value
+
+    dwos.finish(keep_o)
+    lanes_out[...] = lane_sums.finish()
+    sums.settle()
+    final.arrive(0)
+    final.arrive(1)
+    final.settle()
     swap.wait_send()
 
 
-def tail_call(dw, part, gm, x, gain, ddown, dout, early, lane):
-    rows, width = x.shape
-    wr, wc = dw.shape[1:]
+def rear_call(meta, lanes, q, kv, o, do, lse, opart, gb, mid, bias, dup, mixed, n, w, gm, x, gain, early, lane):
+    rows = q.shape[0]
+    small, width = mid.shape
+    sr, sw = dup.shape[2:]
+    hbm = pl.BlockSpec(memory_space=pl.ANY)
+    chunks = (8, small, width)
+    wc = 3 * HEAD
+    share = width // 16
+    head_grad = struct((share, 2 * HEAD), F32)
     return remote_call(
-        tail_kernel, "tail", 6,
-        (struct((2, wr // 2, wc), BF), struct((8, rows, width), BF), struct(ddown.shape[2:], F32), struct(dout.shape[2:], F32),
-         struct((16, width), F32), struct(lane.shape, F32)),
-        [VM] * 9,
-        [pltpu.VMEM((8, rows, width), BF), pltpu.VMEM((8, rows, width), BF), pltpu.VMEM((rows, width), F32), pltpu.VMEM((wr, wc), BF),
-         DMA((2,)), DMA((2,)), DMA((9,)), DMA((9,))] + Scatter.scratch(wr, wc) + Scatter.scratch(rows, width)
-        + CoreScatter.scratch(*ddown.shape[2:]) + CoreScatter.scratch(*dout.shape[2:])
-        + Sums.scratch(8, *early.shape) + Sums.scratch(16, *lane.shape) + Sums.scratch(8, 8, width) + Sums.scratch(16, 16, width),
-        dw, part, gm, x, gain, ddown, dout, early, lane)
+        rear_kernel, "rear", 5,
+        (struct(chunks, BF), struct((sr, sw), F32), struct((2 * HEAD, share), F32), head_grad, head_grad, head_grad,
+         struct(chunks, BF), struct((8, width), F32), struct(lane.shape, F32)),
+        [SM] + [VM] * 12 + [hbm, VM, VM, hbm] + [VM] * 3,
+        [pltpu.VMEM((rows, 2 * HEAD), BF), pltpu.VMEM((8 * rows, HEAD), BF), pltpu.VMEM(kv.shape, BF), pltpu.VMEM((8, rows), F32),
+         pltpu.VMEM((rows, HEAD), F32), pltpu.VMEM((8 * small, width), BF), pltpu.VMEM((rows, wc), BF), pltpu.VMEM((2 * HEAD, width), BF),
+         pltpu.VMEM((2, rows, BLK), BF), pltpu.VMEM((8, width // 8, wc), BF), pltpu.VMEM(chunks, BF), pltpu.VMEM(chunks, BF),
+         pltpu.VMEM(chunks, BF), pltpu.VMEM((small, width), F32), pltpu.VMEM((width // 8, wc), BF), pltpu.VMEM((share, wc), BF),
+         pltpu.VMEM((8, width), F32), pltpu.VMEM((small, width), BF), DMA((3,)), DMA((2,)), DMA((2,))]
+        + Scatter.scratch(rows, 2 * HEAD) + Scatter.scratch(small, width) + CoreScatter.scratch(sr, sw)
+        + CoreScatter.scratch(2 * HEAD, share) + Scatter.scratch(small, width) + Scatter.scratch(width // 8, wc)
+        + Gather.scratch() * 3 + RowSums.scratch(width) + Sums.scratch(*lane.shape),
+        meta, lanes, q, kv, o, do, lse, opart, gb, mid, bias, dup, mixed, n, w, gm, x, gain, early, lane)
 
 
 def on_device(tokens, first_gain, first_shift, query_weight, query_bias, key_weight, value_weight, value_bias,
@@ -983,45 +1092,30 @@
         meta, lanes, tokens, row(first_gain), row(first_shift), query_weight, key_weight, value_weight, row(query_bias), row(value_bias),
         out_weight, up_weight, down_weight, row(out_bias), row(second_gain), row(second_shift))
     n_all = n_all.reshape(2 * own, width)
-    here = lambda v: lax.dynamic_slice_in_dim(v, t * rows, rows)
-    x_rows, g_rows = here(tokens), here(cotangent)
     n2 = n2.reshape(own, width)
     pre = dg(n2, up_all, NN) + up_bias
     half_erf = 0.5 + 0.5 * lax.erf(pre * math.sqrt(0.5))
     hidden = (pre * half_erf).astype(BF)
     slope = half_erf + pre * jnp.exp(-0.5 * pre * pre) * (1.0 / math.sqrt(2.0 * math.pi))
-    grad_pre = (dg(cotangent, down_all, NN) * slope).astype(BF)
+    grad_pre = (dg(cotangent, down_all, NT) * slope).astype(BF)
     gn2 = dg(grad_pre, up_all, NT).astype(BF).reshape(8, rows, width)
-    out_part = dg(hidden, down_all, NT).astype(BF).reshape(8, rows, width)
-    do, gm, sums, low = back_call(gn2, mid, g_rows, out_all, row(second_gain))
+    out_part = dg(hidden, down_all, NN).astype(BF).reshape(8, rows, width)
     hid = up_weight.shape[1]
     dw_up = dg(n2, grad_pre, TN).astype(BF).reshape(8, 2, width // 16, hid)
-    dw_down = dg(cotangent, hidden, TN).astype(BF).reshape(8, 2, width // 16, hid)
-    dq, dkv, layer, gb, up_grad = attend_back_call(meta, lanes, q, kv, o, do, lse, out_part, low, mid, row(down_bias), dw_up)
-    dw_out = dg(gb.reshape(own, width), mixed, TN).astype(BF).reshape(8, 2, width // 16, 2 * HEAD)
-
-    dqkv = jnp.concatenate([dq, dkv], axis=1)
-    dw = dg(n_all, dqkv, TN).astype(BF).reshape(8, width // 8, 3 * HEAD)
-    gn1 = dg(dqkv, w_all, NT).astype(BF).reshape(2, 8, rows, width)
-    col = jnp.sum(dqkv.astype(F32), axis=0)
-    zero = jnp.zeros((HEAD,), F32)
-    two = lambda v: jnp.concatenate([jnp.where(c == 0, v, zero), jnp.where(c == 1, v, zero)])
-    lane = jnp.concatenate([jnp.sum(grad_pre.astype(F32), axis=0), two(col[:HEAD]), two(col[2 * HEAD:])])
-    lane = jnp.pad(lane.reshape(1, -1), ((0, 7), (0, 0)))
-    dw_mine, tg, down_grad, out_grad, small, lane = tail_call(
-        dw, gn1, gm, x_rows, row(first_gain), dw_down, dw_out, sums, lane)
-    pieces = [
-        jnp.concatenate([dw_mine[0, :, i * HEAD:(i + 1) * HEAD], dw_mine[1, :, i * HEAD:(i + 1) * HEAD]], axis=1).astype(F32)
-        for i in range(3)]
+    dw_down = dg(hidden, cotangent, TN).astype(BF)
+    do, gm, sums, low, down_grad = back_call(gn2, mid, cotangent, out_all, row(second_gain), dw_down)
+    lane = jnp.pad(jnp.sum(grad_pre.astype(F32), axis=0).reshape(hid // 256, 256), ((0, 8 - hid // 256), (0, 0)))
+    layer, up_grad, out_grad, dwq, dwk, dwv, tg, small, lane = rear_call(
+        meta, lanes, q, kv, o, do, lse, out_part, low, mid, row(down_bias), dw_up, mixed, n_all, w_all, gm, tokens, row(first_gain), sums, lane)
     return (
         layer.reshape(own, width),
         tg.reshape(own, width).astype(F32),
+        small[4], small[5],
+        dwq, lane[4], dwk, dwv, lane[5],
+        out_grad, small[2],
         small[0], small[1],
-        pieces[0], lane[0, hid:hid + 2 * HEAD], pieces[1], pieces[2], lane[0, hid + 2 * HEAD:],
-        out_grad.T, small[10],
-        small[8], small[9],
-        up_grad, lane[0, :hid],
-        down_grad.T, small[11],
+        up_grad, lane[:hid // 256].reshape(hid),
+        down_grad, small[3],
     )
 
 

time: 422 us -> 379 us (0.90)
  Pallas kernels: 353 us -> 334 us
  matrix products: 35.9 us -> 26.5 us
  local copies, waits for them, and re-layouts: 20.6 us -> 11.3 us
    pallas_call x4 -> x3, Pallas kernels: 353 us -> 334 us  [remote_call(): pl.pallas_call(kernel, out_shape=outs, in_specs=ins, out_specs=jax.tree.m...]
    dot_general x9 -> x6, matrix products: 35.9 us -> 26.5 us  [dg(): return lax.dot_general(a, b, dims, preferred_element_type=F32)]
    convert_element_type x1 -> x0, local copies, waits for them, and re-layouts: 6.39 us -> none  [on_device(): dg(cotangent, hidden, TN).astype(BF).reshape(8, 2, width // 16, hid)]
where the time goes in v4:
time: 379 us
  Pallas kernels  334 us (88%)
  matrix products  26.5 us (7%)
  local copies, waits for them, and re-layouts  11.3 us (3%)
  other arithmetic  5.53 us (1%)
    pallas_call x3, Pallas kernels, remote_call(): pl.pallas_call(kernel, out_shape=outs, in_specs=ins, out_specs=jax.tree.m...  334 us
    dot_general x6, matrix products, dg(): return lax.dot_general(a, b, dims, preferred_element_type=F32)  26.5 us

profile of v4, /device:TPU:1, one launch (start us, length us, event | category | flops | bytes accessed | tf_op | source)
XLA Modules:
  0.0 378.8 jit_solution(11339868816677338348)
XLA Ops:
  1.3 0.7 and_select_fusion
  2.0 0.6 pad_add_fusion.meta
  2.6 0.5 pad_bitcast_fusion.lanes_ref
  3.1 135.4 %forward.1 = (bf16[2048,384]{1,0:T(8,128)(2,1)}, bf16[2,512,2048]{2,1,0:T(8,128)(2,1)}, bf16[1024,128]{1,0:T(8,128)(2,1)}, bf16[8,1024,256]{2,1,0:T(8,128)(2,1)}...) custom-call(s32[33]{0:T(128)} %pad_add_fusion.meta, ...), custom_call_target="tpu_custom_call" | custom-call | tf_op jit(solution)/shard_map/forward/pallas_call | solution.py:418
  138.5 0.0 copy-start.1
  138.5 0.0 copy-start.9
  138.5 0.0 copy-start.10
  138.5 5.3 %fusion.9 = f32[512,1024]{1,0:T(8,128)S(1)} fusion(bf16[512,2048]{1,0:T(8,128)(2,1)} %bitcast.66, bf16[2048,1024]{1,0:T(8,128)(2,1)} %get-tuple-element.48), kind=kOutput, calls=%fused_computation.24 | convolution fusion | flops 2147483648 | bytes 8388608 | tf_op jit(solution)/shard_map/dot_general | solution.py:32
  143.8 0.0 copy-done.1
  143.8 0.0 copy-done.9
  143.8 0.0 copy-done.10
  143.8 0.0 copy-start.11
  143.8 3.0 convert_reduce_fusion
  146.9 0.0 copy-done.11
  146.9 0.0 copy-start.8
  146.9 3.7 convolution_convert_fusion.2
  150.6 0.0 copy-done.8
  150.6 3.7 convolution_convert_fusion.3
  154.3 0.6 pad.9.lane_ref
  154.9 0.0 copy-start.12
  154.9 6.4 %convolution_convert_fusion = bf16[2048,1024]{1,0:T(8,128)(2,1)} fusion(bf16[512,2048]{1,0:T(8,128)(2,1)} %bitcast.67, bf16[512,1024]{1,0:T(8,128)(2,1)S(1)} %get-tuple-element.78), kind=kOutput, calls=%fused_computation | convolution fusion | flops 2149580800 | bytes 7340032 | tf_op jit(solution)/shard_map/dot_general | solution.py:32
  161.3 0.0 copy-done.12
  161.3 4.4 %convolution_convert_fusion.1.dd_ref = bf16[1024,2048]{1,0:T(8,128)(2,1)} fusion(bf16[512,2048]{1,0:T(8,128)(2,1)S(1)} %copy-done.1, f32[512,1024]{1,0:T(8,128)S(1)} %copy-done.12, f32[1024]{0:T(1024)S(1)} %copy-done.10), kind=kOutput, calls=%fused_computation.1 | convolution fusion | flops 2152726528 | bytes 8392704 | tf_op jit(solution)/shard_map/dot_general | solution.py:32
  165.7 44.8 %back.1 = (bf16[1024,128]{1,0:T(8,128)(2,1)}, f32[64,2048]{1,0:T(8,128)}, f32[8,2048]{1,0:T(8,128)}, bf16[64,2048]{1,0:T(8,128)(2,1)}, f32[1024,128]{1,0:T(8,128)}) custom-call(bf16[8,64,2048]{2,1,0:T(8,128)(2,1)} %bitcast.46, f32[64,2048]{1,0:T(8,128)} %get-tuple-element.49.mid_ref, bf16[512,2048]{1,0:T(8,128)(2,1)} %g_hbm.1, ...), custom_call_target="tpu_custom_call" | custom-call | tf_op jit(solution)/shard_map/back/pallas_call | solution.py:418
  210.5 153.9 %rear.1 = (bf16[8,64,2048]{2,1,0:T(8,128)(2,1)}, f32[128,1024]{1,0:T(8,128)}, f32[256,128]{1,0:T(8,128)}, f32[128,256]{1,0:T(8,128)}, f32[128,256]{1,0:T(8,128)}...) custom-call(s32[33]{0:T(128)} %pad_add_fusion.meta, ...), custom_call_target="tpu_custom_call" | custom-call | tf_op jit(solution)/shard_map/rear/pallas_call | solution.py:418
  364.4 1.3 fusion.8
  365.7 0.7 slice_bitcast_fusion
  366.4 0.6 copy.36
  367.0 1.9 fusion.7
  369.0 0.0 copy-start
  369.0 4.3 %bitcast_convert_fusion = f32[512,2048]{1,0:T(8,128)} fusion(bf16[8,64,2048]{2,1,0:T(8,128)(2,1)} %get-tuple-element.60), kind=kLoop, calls=%fused_computation.11 | loop fusion | flops 1048576 | bytes 6291456 | tf_op jit(solution)/shard_map/convert_element_type | solution.py:1112
  373.2 0.0 copy-done
  373.2 0.0 copy-start.7
  373.3 0.0 copy-start.6
  373.3 0.0 copy-start.5
  373.3 0.0 copy-start.4
  373.3 0.0 copy-start.3
  373.3 1.3 copy.45
  374.6 0.0 copy-done.7
  374.6 0.0 copy-start.2
  374.6 0.7 copy.46
  375.3 0.0 copy-done.6
  375.3 0.7 copy.47
  375.9 0.0 copy-done.5
  375.9 0.7 copy.48
  376.6 0.0 copy-done.4
  376.6 0.7 copy.49
  377.2 0.0 copy-done.3
  377.2 0.8 copy.50
  378.0 0.0 copy-done.2
  378.0 0.8 copy.51
  (1 shorter events, 0.0 us)
Async XLA Ops:
  138.5 5.3 %copy-start.1 = (bf16[512,2048]{1,0:T(8,128)(2,1)S(1)}, bf16[512,2048]{1,0:T(8,128)(2,1)}, u32[]{:S(2)}) copy-start(bf16[512,2048]{1,0:T(8,128)(2,1)} %g_hbm.1) | copy-start | bytes 6291460
  138.5 5.3 %copy-start.9 = (bf16[1024,2048]{1,0:T(8,128)(2,1)S(1)}, bf16[1024,2048]{1,0:T(8,128)(2,1)}, u32[]{:S(2)}) copy-start(bf16[1024,2048]{1,0:T(8,128)(2,1)} %get-tuple-element.46) | copy-start | bytes 12582916
  138.5 5.3 %copy-start.10 = (f32[1024]{0:T(1024)S(1)}, f32[1024]{0:T(1024)}, u32[]{:S(2)}) copy-start(f32[1024]{0:T(1024)} %param.32) | copy-start | bytes 12292
  143.8 3.0 copy-start.11
  146.9 3.8 copy-start.8
  154.9 6.4 %copy-start.12 = (f32[512,1024]{1,0:T(8,128)S(1)}, f32[512,1024]{1,0:T(8,128)}, u32[]{:S(2)}) copy-start(f32[512,1024]{1,0:T(8,128)} %copy-done.11) | copy-start | bytes 6291460
  369.0 4.3 %copy-start = (bf16[8,64,2048]{2,1,0:T(8,128)(2,1)S(1)}, bf16[8,64,2048]{2,1,0:T(8,128)(2,1)}, u32[]{:S(2)}) copy-start(bf16[8,64,2048]{2,1,0:T(8,128)(2,1)} %get-tuple-element.59) | copy-start | bytes 6291460
  373.2 1.4 copy-start.7
  373.3 2.0 copy-start.6
  373.3 2.7 copy-start.5
  373.3 3.3 copy-start.4
  373.3 4.0 %copy-start.3 = (f32[128,1024]{1,0:T(8,128)S(1)}, f32[128,1024]{1,0:T(8,128)}, u32[]{:S(2)}) copy-start(f32[128,1024]{1,0:T(8,128)} %get-tuple-element.109) | copy-start | bytes 1572868
  374.6 3.4 copy-start.2

commit v5 on v4

--- a/solution.py
+++ b/solution.py
@@ -289,37 +289,47 @@
 
 
 class CoreScatter:
-    COUNT = 9
+    COUNT = 11
 
     @staticmethod
     def scratch(rows, width):
-        return [pltpu.VMEM((8, rows, width), BF), DMA((8,)), DMA((8,))] + Scatter.scratch(rows, width)
+        return [pltpu.VMEM((8, rows, width), BF), DMA((8,)), DMA((8,)), pltpu.VMEM((2, rows, width), BF), DMA((2,))] + Scatter.scratch(rows, width)
 
     def __init__(self, group, part, rows, scratch, step):
-        self.part, self.total, self.sems = part, scratch[0], scratch[1:3]
+        self.part, self.total, self.sems, self.buf, self.load_sems = part, scratch[0], scratch[1:3], scratch[3], scratch[4]
         self.c = lax.rem(group.d, 2)
         self.rows, self.step = rows, step
-        self.inner = Scatter(group, lambda m: self.total.at[m], rows, scratch[3:], step)
+        self.inner = Scatter(group, lambda m: self.total.at[m], rows, scratch[5:], step)
 
     def swap(self, m):
         return copy_of(self.part(m, 1 - self.c), self.total.at[m], self.sems, m, other_core())
+
+    def load(self, m):
+        slot = lax.rem(m, 2)
+        return pltpu.make_async_copy(self.part(m, self.c), self.buf.at[slot], self.load_sems.at[slot])
 
     def start(self):
         for m in range(8):
             self.swap(m).start()
+        self.load(0).start()
 
     def add(self):
         step = self.step
 
         @pl.loop(0, 8)
         def _(m):
+            @pl.when(m < 7)
+            def _():
+                self.load(m + 1).start()
+
+            self.load(m).wait()
             self.swap(m).wait_recv()
-            mine = self.part(m, self.c)
+            slot = lax.rem(m, 2)
 
             @pl.loop(0, self.rows // step)
             def _(n):
                 at = pl.ds(pl.multiple_of(n * step, step), step)
-                self.total[m, at, :] = (mine[at, :].astype(F32) + self.total[m, at, :].astype(F32)).astype(BF)
+                self.total[m, at, :] = (self.buf[slot, at, :].astype(F32) + self.total[m, at, :].astype(F32)).astype(BF)
 
         self.inner.start()
 
@@ -419,7 +429,7 @@
         kernel, out_shape=outs, in_specs=ins,
         out_specs=jax.tree.map(lambda _: VM, outs) if out_specs is None else out_specs,
         scratch_shapes=scratch, name=name,
-        compiler_params=pltpu.CompilerParams(collective_id=cid, has_side_effects=True, vmem_limit_bytes=58 << 20),
+        compiler_params=pltpu.CompilerParams(collective_id=cid, has_side_effects=True, vmem_limit_bytes=60 << 20),
     )(*args)
 
 
@@ -473,11 +483,12 @@
     return lax.axis_index("dp") // 2 * 4
 
 
-def forward_kernel(meta, lanes_ref, x_ref, gain1_ref, shift1_ref, wq_ref, wk_ref, wv_ref, qb_ref, vb_ref, wo_ref, wu_ref, wd_ref,
-                   bias_ref, gain2_ref, shift2_ref,
-                   w_hbm, n_hbm, q_out, kv_hbm, o_ref, lse_ref, out_hbm, up_hbm, down_hbm, n2_out, mid_out, own_out,
-                   w_vm, n_vm, kv_vm, out_vm, up_vm, down_vm, wsh, qa_ref, kx_ref, m_ref, acc_ref, mixed,
-                   lsem, css, crs, ass, ars, *sems):
+def front_kernel(meta, lanes_ref, x_ref, gain1_ref, shift1_ref, wq_ref, wk_ref, wv_ref, qb_ref, vb_ref, wo_ref, wu_ref, wd_ref,
+                 bias_ref, gain2_ref, shift2_ref, cot_ref, ub_ref,
+                 w_hbm, n_hbm, q_out, kv_hbm, o_ref, lse_ref, mid_out, own_out, do_out, gm_out, sums_out, low_out, lane_out, opart_out, du_hbm, dd_hbm,
+                 w_vm, n_vm, kv_vm, out_vm, up_vm, down_vm, wsh, qa_ref, kx_ref, m_ref, acc_ref, mixed,
+                 n2, gh, hidden, gp, gpart, gsum, colsum, du_buf, dd_buf,
+                 lsem, css, crs, ass, ars, hss, hrs, *sems):
     gd, gt = Eight("dp"), Eight("tensor")
     t = gt.t
     c = lax.rem(gd.d, 2)
@@ -510,7 +521,8 @@
     ups = Gather(gd, lambda m: up_vm.at[row_of(m)], shard, sems[8:12], core)
     downs = Gather(gd, lambda m: down_vm.at[:, row_of(m)], hid, sems[12:16], core)
     wide = Gather(gt, lambda m: out_vm.at[m, pl.ds(pl.multiple_of(c * half, half), half)], half, sems[16:20], core, twin_own=False)
-    normed = Gather(gt, lambda m: n2_out.at[m], small, sems[20:22])
+    normed = Gather(gt, lambda m: n2.at[pl.ds(pl.multiple_of(m * small, small), small)], small, sems[20:22])
+    back = Scatter(gt, lambda m: gpart.at[m], small, sems[22:28], 32)
     swap.wait_recv()
     qkv.start()
     out_vm[t, :, mine] = wo_ref[...].astype(BF)
@@ -568,21 +580,20 @@
     prefix = meta[nblk]
 
     def attend(chunk, diagonal):
-        @pl.loop(0, per)
-        def _(a):
-            take = pl.ds(pl.multiple_of(a * BLK, BLK), BLK)
+        ks, vs = [], []
+        for i in range(per):
+            at = pl.ds(pl.multiple_of(chunk * rows + i * BLK, BLK), BLK)
+            ks.append(jnp.concatenate([kv_vm[chunk, i * BLK:(i + 1) * BLK, :HEAD], kx_ref[at, :]], axis=1))
+            vs.append(jnp.concatenate([kv_vm[chunk, i * BLK:(i + 1) * BLK, HEAD:], ones], axis=1))
+        for a in range(per):
+            take = slice(a * BLK, (a + 1) * BLK)
             q = qa_ref[take, :]
-            ss, vs = [], []
-            for i in range(per):
-                at = pl.ds(pl.multiple_of(chunk * rows + i * BLK, BLK), BLK)
-                ss.append(dg(q, jnp.concatenate([kv_vm[chunk, i * BLK:(i + 1) * BLK, :HEAD], kx_ref[at, :]], axis=1), NT))
-                vs.append(jnp.concatenate([kv_vm[chunk, i * BLK:(i + 1) * BLK, HEAD:], ones], axis=1))
+            ss = [dg(q, k, NT) for k in ks]
             if diagonal:
                 edge = prefix - 1 - meta[first_block() + a] * BLK
                 lim = jnp.maximum(lax.broadcasted_iota(jnp.int32, (BLK, BLK), 0), edge)
                 key = lax.broadcasted_iota(jnp.int32, (BLK, BLK), 1)
-                for i in range(per):
-                    ss[i] = jnp.where(key <= jnp.where(a == i, lim, BLK), ss[i], NEG)
+                ss[a] = jnp.where(key <= lim, ss[a], NEG)
             top = ss[0]
             for s in ss[1:]:
                 top = jnp.maximum(top, s)
@@ -652,9 +663,6 @@
     wide.arrive(0)
     wide.arrive(1)
     wide.settle()
-    save = pltpu.make_async_copy(out_vm, out_hbm, lsem.at[3])
-    save.start()
-    saves.append(save)
     for copy in copies:
         copy.wait_recv()
     span = 512
@@ -667,134 +675,161 @@
             total = term if total is None else total + term
         mid_out[:, cols] = total + (x_ref[x_rows, cols].astype(F32) + bias_ref[:, cols])
     scaled, _ = norm_rows(mid_out[...])
-    n2_out[t] = (scaled * gain2_ref[...] + shift2_ref[...]).astype(BF)
+    n2[pl.ds(pl.multiple_of(t * small, small), small), :] = (scaled * gain2_ref[...] + shift2_ref[...]).astype(BF)
     normed.start()
     ups.forward(1)
+    normed.forward_pair()
+    normed.forward(0)
     downs.forward_pair()
     downs.forward(0)
-    normed.forward_pair()
-    normed.forward(0)
     ups.arrive(0)
     ups.arrive(1)
     ups.settle()
-    save = pltpu.make_async_copy(up_vm, up_hbm, lsem.at[4])
-    save.start()
-    saves.append(save)
     normed.forward(1)
     downs.forward(1)
     downs.arrive(0)
     downs.arrive(1)
     downs.settle()
-    save = pltpu.make_async_copy(down_vm, down_hbm, lsem.at[5])
-    save.start()
-    saves.append(save)
+    blocks = [(slice(n * span, (n + 1) * span)) for n in range(hid // span)]
+
+    @pl.loop(0, own // BLK)
+    def _(b):
+        at = pl.ds(pl.multiple_of(b * BLK, BLK), BLK)
+        for cols in blocks:
+            gh[at, cols] = dg(cot_ref[at, :], down_vm[cols, :], NT)
+
     normed.arrive(0)
     normed.arrive(1)
     normed.settle()
+    colsum[...] = jnp.zeros_like(colsum)
+    wide_blocks = [(slice(n * span, (n + 1) * span)) for n in range(n2.shape[1] // span)]
+
+    @pl.loop(0, own // BLK)
+    def _(b):
+        at = pl.ds(pl.multiple_of(b * BLK, BLK), BLK)
+        for cols in blocks:
+            pre = dg(n2[at, :], up_vm[:, cols], NN) + ub_ref[:, cols]
+            half_erf = 0.5 + 0.5 * lax.erf(pre * math.sqrt(0.5))
+            hidden[at, cols] = (pre * half_erf).astype(BF)
+            slope = half_erf + pre * jnp.exp(-0.5 * pre * pre) * (1.0 / math.sqrt(2.0 * math.pi))
+            low = (gh[at, cols] * slope).astype(BF)
+            gp[at, cols] = low
+            colsum[0:1, cols] += jnp.sum(low.astype(F32), axis=0, keepdims=True)
+        for cols in wide_blocks:
+            piece = dg(gp[at, :], up_vm[cols, :], NT).astype(BF)
+            for j in range(BLK // small):
+                gpart[b * (BLK // small) + j, :, cols] = piece[j * small:(j + 1) * small]
+
+    back.start()
+
+    @pl.loop(0, own // BLK)
+    def _(b):
+        at = pl.ds(pl.multiple_of(b * BLK, BLK), BLK)
+        for cols in wide_blocks:
+            piece = dg(hidden[at, :], down_vm[:, cols], NN).astype(BF)
+            for j in range(BLK // small):
+                opart_out[b * (BLK // small) + j, :, cols] = piece[j * small:(j + 1) * small]
+
+    back.add_near(1)
+    back.add_near(0)
+
+    def du_save(m):
+        slot = lax.rem(m, 2)
+        return pltpu.make_async_copy(du_buf.at[slot], du_hbm.at[pl.ds(pl.multiple_of(m * BLK, BLK), BLK)], lsem.at[3 + slot])
+
+    def dd_save(m):
+        slot = lax.rem(m, 2)
+        return pltpu.make_async_copy(dd_buf.at[slot], dd_hbm.at[:, pl.ds(pl.multiple_of(m * BLK, BLK), BLK)], lsem.at[5 + slot])
+
+    def weight_grads(low, high):
+        @pl.loop(low, high)
+        def _(m):
+            slot = lax.rem(m, 2)
+            cols = pl.ds(pl.multiple_of(m * BLK, BLK), BLK)
+
+            @pl.when(m > 1)
+            def _():
+                du_save(m - 2).wait()
+                dd_save(m - 2).wait()
+
+            du_buf[slot] = dg(n2[:, cols], gp[...], TN).astype(BF)
+            du_save(m).start()
+            dd_buf[slot] = dg(hidden[...], cot_ref[:, cols], TN).astype(BF)
+            dd_save(m).start()
+
+    weight_grads(0, 4)
+    back.add_pair()
+    weight_grads(4, 8)
+
+    def keep(at, value):
+        gsum[at, :] = value
+
+    back.finish(keep)
+    scaled, inverse = norm_rows(mid_out[...])
+    grad = gsum[...]
+    g_rows = cot_ref[x_rows, :].astype(F32)
+    gm = g_rows + norm_back(grad, scaled, inverse, gain2_ref[...])
+    gm_out[...] = gm
+    low = gm.astype(BF)
+    low_out[...] = low
+    for k in range(8):
+        mixed[:, k * 256:(k + 1) * 256] = dg(low, out_vm[k], NT).astype(BF)
+    hsem = (hss, hrs)
+    take = pl.ds(pl.multiple_of(c * own + t * small, small), small)
+    heads = []
+    for k, (tt, cc, device) in enumerate(members):
+        cols = pl.ds(pl.multiple_of((2 * tt + cc) * HEAD, HEAD), HEAD)
+        heads.append(send(mixed.at[:, cols], do_out.at[take], hsem, k, device))
+    do_out[take, :] = mixed[:, head]
+    sums_out[...] = jnp.zeros_like(sums_out)
+    sums_out[0:1, :] = jnp.sum(grad * scaled, axis=0, keepdims=True)
+    sums_out[1:2, :] = jnp.sum(grad, axis=0, keepdims=True)
+    sums_out[2:3, :] = jnp.sum(low.astype(F32), axis=0, keepdims=True)
+    sums_out[3:4, :] = jnp.sum(g_rows, axis=0, keepdims=True)
+    lane_out[...] = jnp.zeros_like(lane_out)
+    for j in range(hid // 256):
+        lane_out[j:j + 1, :] = colsum[0:1, j * 256:(j + 1) * 256]
+    du_save(6).wait()
+    dd_save(6).wait()
+    du_save(7).wait()
+    dd_save(7).wait()
     qkv.settle()
     swap.wait_send()
     for copy in there + copies:
         copy.wait_send()
     for save in saves:
         save.wait()
-
-
-def forward_call(meta, lanes, x, gain1, shift1, wq, wk, wv, qb, vb, wo, wu, wd, bias, gain2, shift2):
+    for copy in heads:
+        copy.wait()
+
+
+def front_call(meta, lanes, x, gain1, shift1, wq, wk, wv, qb, vb, wo, wu, wd, bias, gain2, shift2, cot, ub):
     own, width = x.shape
     rows, shard, hid, small = 2 * own, wq.shape[0], wu.shape[1], own // 8
     hbm = pl.BlockSpec(memory_space=pl.ANY)
     big = [(width, 3 * HEAD), (2, own, width), (8, rows, 2 * HEAD), (8, 2 * HEAD, width), (width, hid), (hid, width)]
     w, n, kv, out, up, down = (struct(s, BF) for s in big)
-    outs = (w, n, struct((rows, HEAD), BF), kv, struct((rows, HEAD), BF), struct((rows // BLK, BLK), F32), out, up, down,
-            struct((8, small, width), BF), struct((small, width), F32), struct((own, 2 * HEAD), BF))
+    chunks = (8, small, width)
+    outs = (w, n, struct((rows, HEAD), BF), kv, struct((rows, HEAD), BF), struct((rows // BLK, BLK), F32),
+            struct((small, width), F32), struct((own, 2 * HEAD), BF), struct((rows, HEAD), BF), struct((small, width), F32),
+            struct((8, width), F32), struct((small, width), BF), struct((8, 256), F32), struct(chunks, BF), up, down)
     return remote_call(
-        forward_kernel, "forward", 1, outs, [SM] + [VM] * 15,
+        front_kernel, "front", 1, outs, [SM] + [VM] * 17,
         [pltpu.VMEM(s, BF) for s in big]
         + [pltpu.VMEM((2, shard, 3 * HEAD), BF), pltpu.VMEM((rows, 2 * HEAD), BF), pltpu.VMEM((8 * rows, HEAD), BF),
            pltpu.VMEM((rows, HEAD), F32), pltpu.VMEM((rows, 2 * HEAD), F32), pltpu.VMEM((small, width), BF),
-           DMA((6,)), DMA((3,)), DMA((3,)), DMA((16,)), DMA((16,))]
-        + Gather.scratch() * 2 + Gather.scratch(True) * 4 + Gather.scratch(),
-        meta, lanes, x, gain1, shift1, wq, wk, wv, qb, vb, wo, wu, wd, bias, gain2, shift2,
-        out_specs=(hbm, hbm, VM, hbm, VM, VM, hbm, hbm, hbm, VM, VM, VM))
-
-
-def back_kernel(part_ref, mid_ref, g_hbm, w_hbm, gain_ref, dd_ref, do_out, gm_out, sums_out, low_out, dd_out,
-                w_ref, g_ref, total, heads, lsem, asems, arecv, *scratch):
-    g, gd = Eight("tensor"), Eight("dp")
-    c = lax.rem(g.d, 2)
-    members = chip_members()
-    rows = g_ref.shape[0]
-    loads = [pltpu.make_async_copy(w_hbm, w_ref, lsem.at[0]),
-             pltpu.make_async_copy(g_hbm.at[pl.ds(pl.multiple_of(g.t * rows, rows), rows)], g_ref, lsem.at[1])]
-    for load in loads:
-        load.start()
-    greet([m[2] for m in members] + gd.others())
-    half = do_out.shape[0] // 2
-    first = Scatter(g, lambda m: part_ref.at[m], rows, scratch, 32)
-    first.start()
-    share = dd_out.shape[1]
-    downs = CoreScatter(
-        gd, lambda m, cc: dd_ref.at[:, pl.ds(pl.multiple_of((m * 2 + cc) * share, share), share)], dd_out.shape[0], scratch[6:], 128)
-    downs.start()
-    first.add_near(1)
-    first.add_near(0)
-    first.add_pair()
-    downs.add()
-
-    def keep(at, value):
-        total[at, :] = value
-
-    first.finish(keep)
-    scaled, inverse = norm_rows(mid_ref[...])
-    grad = total[...]
-    for load in loads:
-        load.wait()
-    gm = g_ref[...].astype(F32) + norm_back(grad, scaled, inverse, gain_ref[...])
-    gm_out[...] = gm
-    low = gm.astype(BF)
-    low_out[...] = low
-    for t in range(8):
-        heads[:, t * 256:(t + 1) * 256] = dg(low, w_ref[t], NT).astype(BF)
-    sems = (asems, arecv)
-    take = pl.ds(pl.multiple_of(c * half + g.t * rows, rows), rows)
-    copies = []
-    for k, (tt, cc, device) in enumerate(members):
-        cols = pl.ds(pl.multiple_of((2 * tt + cc) * HEAD, HEAD), HEAD)
-        copies.append(send(heads.at[:, cols], do_out.at[take], sems, k, device))
-    do_out[take, :] = heads[:, pl.ds(pl.multiple_of((2 * g.t + c) * HEAD, HEAD), HEAD)]
-    downs.inner.add_near(1)
-    downs.inner.add_near(0)
-    sums_out[...] = jnp.zeros_like(sums_out)
-    sums_out[0:1, :] = jnp.sum(grad * scaled, axis=0, keepdims=True)
-    sums_out[1:2, :] = jnp.sum(grad, axis=0, keepdims=True)
-    sums_out[2:3, :] = jnp.sum(low.astype(F32), axis=0, keepdims=True)
-    sums_out[3:4, :] = jnp.sum(g_ref[...].astype(F32), axis=0, keepdims=True)
-    downs.inner.add_pair()
-
-    def keep_down(at, value):
-        dd_out[at, :] = value
-
-    downs.finish(keep_down)
-    for copy in copies:
-        copy.wait()
-
-
-def back_call(part, mid, g, w, gain, dd):
-    rows, width = mid.shape
-    hbm = pl.BlockSpec(memory_space=pl.ANY)
-    share = (dd.shape[0], dd.shape[1] // 16)
-    return remote_call(
-        back_kernel, "back", 4,
-        (struct((16 * rows, HEAD), BF), struct((rows, width), F32), struct((8, width), F32), struct((rows, width), BF), struct(share, F32)),
-        [VM, VM, hbm, hbm, VM, VM],
-        [pltpu.VMEM(w.shape, BF), pltpu.VMEM((rows, width), BF), pltpu.VMEM((rows, width), F32), pltpu.VMEM((rows, width), BF),
-         DMA((2,)), DMA((15,)), DMA((15,))] + Scatter.scratch(rows, width) + CoreScatter.scratch(*share),
-        part, mid, g, w, gain, dd)
-
-
-def rear_kernel(meta, lanes_ref, q_ref, kv_ref, o_ref, do_ref, lse_ref, opart_ref, gbr_ref, mid_ref, bias_ref, dup_ref,
+           pltpu.VMEM((own, width), BF), pltpu.VMEM((own, hid), F32), pltpu.VMEM((own, hid), BF), pltpu.VMEM((own, hid), BF),
+           pltpu.VMEM(chunks, BF), pltpu.VMEM((small, width), F32), pltpu.VMEM((8, hid), F32),
+           pltpu.VMEM((2, BLK, hid), BF), pltpu.VMEM((2, hid, BLK), BF),
+           DMA((7,)), DMA((3,)), DMA((3,)), DMA((16,)), DMA((16,)), DMA((15,)), DMA((15,))]
+        + Gather.scratch() * 2 + Gather.scratch(True) * 4 + Gather.scratch() + Scatter.scratch(small, width),
+        meta, lanes, x, gain1, shift1, wq, wk, wv, qb, vb, wo, wu, wd, bias, gain2, shift2, cot, ub,
+        out_specs=(hbm, hbm, VM, hbm) + (VM,) * 10 + (hbm, hbm))
+
+
+def rear_kernel(meta, lanes_ref, q_ref, kv_ref, o_ref, do_ref, lse_ref, opart_ref, gbr_ref, mid_ref, bias_ref, dup_hbm, ddown_hbm,
                 mixed_ref, n_hbm, w_ref, gm_ref, x_hbm, gain_ref, early_ref, lane_ref,
-                lay_out, dup_out, dwo_out, dwq_out, dwk_out, dwv_out, tg_out, sums_out, lanes_out,
+                lay_out, dup_out, ddown_out, dwo_out, dwq_out, dwk_out, dwv_out, tg_out, sums_out, lanes_out,
                 qa_ref, kx_ref, part, delta_ref, dq_acc, gb, dqkv, dwo, n_buf, dw, away, arrived, summed, total, mine_w, there_w, vec, x_ref,
                 lsem, css, crs, *scratch):
     g, gt = Eight("dp"), Eight("tensor")
@@ -819,8 +854,10 @@
     by_columns = lambda m, cc: dwo.at[:, pl.ds(pl.multiple_of((m * 2 + cc) * share, share), share)]
     keys = Scatter(g, lambda m: part.at[m], rows, some(6), 128)
     outs = Scatter(gt, lambda m: opart_ref.at[m], small, some(6), 32)
-    ups = CoreScatter(g, lambda m, cc: dup_ref.at[m, cc], dup_out.shape[0], some(9), 32)
-    dwos = CoreScatter(g, by_columns, dwo_out.shape[0], some(9), 128)
+    ups = CoreScatter(g, lambda m, cc: dup_hbm.at[pl.ds(pl.multiple_of((m * 2 + cc) * share, share), share)], share, some(CoreScatter.COUNT), 32)
+    downs = CoreScatter(
+        g, lambda m, cc: ddown_hbm.at[:, pl.ds(pl.multiple_of((m * 2 + cc) * share, share), share)], ddown_out.shape[0], some(CoreScatter.COUNT), 128)
+    dwos = CoreScatter(g, by_columns, dwo_out.shape[0], some(CoreScatter.COUNT), 128)
     tokens = Scatter(gt, lambda m: summed.at[m], small, some(6), 32)
     weights = Scatter(g, lambda m: dw.at[m], dw.shape[1], some(6), 128)
     wide = Gather(gt, lambda m: gb.at[pl.ds(pl.multiple_of(m * small, small), small)], small, some(2))
@@ -837,6 +874,7 @@
         return pltpu.make_async_copy(n_hbm.at[:, pl.ds(pl.multiple_of(m * BLK, BLK), BLK)], n_buf.at[slot], lsem.at[slot])
 
     ups.start()
+    downs.start()
     outs.start()
     gb[pl.ds(pl.multiple_of(mine_t * small, small), small), :] = gbr_ref[...]
     wide.start()
@@ -850,30 +888,29 @@
     prefix = meta[nblk]
 
     def attend(chunk, diagonal):
-        @pl.loop(0, per)
-        def _(i):
-            at_k = pl.ds(pl.multiple_of(i * BLK, BLK), BLK)
+        for i in range(per):
+            at_k = slice(i * BLK, (i + 1) * BLK)
             at_x = pl.ds(pl.multiple_of(chunk * rows + i * BLK, BLK), BLK)
             k = kv_ref[chunk, at_k, :HEAD]
             v = kv_ref[chunk, at_k, HEAD:]
             kk = jnp.concatenate([k, kx_ref[at_x, :]], axis=1)
+            turned = jnp.transpose(k.astype(F32)).astype(BF)
             dk = dv = None
             for a in range(per):
                 at_q = slice(a * BLK, (a + 1) * BLK)
                 q = q_ref[at_q, :]
                 do = do_ref[at_q, :]
                 p = jnp.exp2(dg(kk, qa_ref[at_q, :], NT) * C1 - delta_ref[1:2, at_q])
-                if diagonal:
+                if diagonal and i == a:
                     edge = prefix - 1 - meta[first_block() + a] * BLK
                     lim = jnp.maximum(lax.broadcasted_iota(jnp.int32, (BLK, BLK), 1), edge)
-                    key = lax.broadcasted_iota(jnp.int32, (BLK, BLK), 0)
-                    p = jnp.where(key <= jnp.where(i == a, lim, BLK), p, 0.0)
+                    p = jnp.where(lax.broadcasted_iota(jnp.int32, (BLK, BLK), 0) <= lim, p, 0.0)
                 ds = (p * (dg(v, do, NT) - delta_ref[0:1, at_q])).astype(BF)
                 tv = jnp.dot(p.astype(BF), do, preferred_element_type=F32)
                 tk = jnp.dot(ds, q, preferred_element_type=F32)
                 dv = tv if dv is None else dv + tv
                 dk = tk if dk is None else dk + tk
-                dq_acc[at_q, :] += dg(ds, k, TN)
+                dq_acc[:, at_q] += jnp.dot(turned, ds, preferred_element_type=F32)
             part[chunk, at_k, :HEAD] = (dk * SCALE).astype(BF)
             part[chunk, at_k, HEAD:] = dv.astype(BF)
 
@@ -907,6 +944,7 @@
         def _():
             keys.send_far(0)
             ups.inner.add_near(1)
+            downs.add()
 
         @pl.when(k == 4)
         def _():
@@ -920,16 +958,17 @@
         @pl.when(k == 6)
         def _():
             keys.add_pair()
+            ups.inner.add_pair()
 
     def lay(at, value):
         lay_out[mine_t, at, :] = (mid_ref[at, :] + (value + bias_ref[...])).astype(BF)
 
     outs.finish(lay)
     layer.start()
-    ups.inner.add_pair()
+    downs.inner.add_near(1)
     n_load(0).start()
     attend(me, True)
-    dqkv[:, :HEAD] = (dq_acc[...] * SCALE).astype(BF)
+    dqkv[:, :HEAD] = jnp.transpose(dq_acc[...] * SCALE).astype(BF)
     layer.forward_pair()
     layer.forward(0)
     wide.arrive(0)
@@ -941,6 +980,7 @@
         dwo[:, cols] = dg(mixed_ref[...], gb[:, cols], TN).astype(BF)
     dwos.start()
     layer.forward(1)
+    downs.inner.add_near(0)
 
     def keep_keys(at, value):
         dqkv[at, HEAD:] = value.astype(BF)
@@ -1012,11 +1052,17 @@
     sums.start()
     weights.add_pair()
     dwos.inner.add_pair()
+    downs.inner.add_pair()
 
     def keep_up(at, value):
         dup_out[at, :] = value
 
     ups.finish(keep_up)
+
+    def keep_down(at, value):
+        ddown_out[at, :] = value
+
+    downs.finish(keep_down)
     sums.middle()
 
     def keep_w(at, value):
@@ -1051,10 +1097,9 @@
     swap.wait_send()
 
 
-def rear_call(meta, lanes, q, kv, o, do, lse, opart, gb, mid, bias, dup, mixed, n, w, gm, x, gain, early, lane):
+def rear_call(meta, lanes, q, kv, o, do, lse, opart, gb, mid, bias, dup, ddown, mixed, n, w, gm, x, gain, early, lane):
     rows = q.shape[0]
     small, width = mid.shape
-    sr, sw = dup.shape[2:]
     hbm = pl.BlockSpec(memory_space=pl.ANY)
     chunks = (8, small, width)
     wc = 3 * HEAD
@@ -1062,18 +1107,19 @@
     head_grad = struct((share, 2 * HEAD), F32)
     return remote_call(
         rear_kernel, "rear", 5,
-        (struct(chunks, BF), struct((sr, sw), F32), struct((2 * HEAD, share), F32), head_grad, head_grad, head_grad,
+        (struct(chunks, BF), struct((share, dup.shape[1]), F32), struct((ddown.shape[0], share), F32), struct((2 * HEAD, share), F32), head_grad, head_grad, head_grad,
          struct(chunks, BF), struct((8, width), F32), struct(lane.shape, F32)),
-        [SM] + [VM] * 12 + [hbm, VM, VM, hbm] + [VM] * 3,
+        [SM] + [VM] * 10 + [hbm, hbm, VM] + [hbm, VM, VM, hbm] + [VM] * 3,
         [pltpu.VMEM((rows, 2 * HEAD), BF), pltpu.VMEM((8 * rows, HEAD), BF), pltpu.VMEM(kv.shape, BF), pltpu.VMEM((8, rows), F32),
-         pltpu.VMEM((rows, HEAD), F32), pltpu.VMEM((8 * small, width), BF), pltpu.VMEM((rows, wc), BF), pltpu.VMEM((2 * HEAD, width), BF),
+         pltpu.VMEM((HEAD, rows), F32), pltpu.VMEM((8 * small, width), BF), pltpu.VMEM((rows, wc), BF), pltpu.VMEM((2 * HEAD, width), BF),
          pltpu.VMEM((2, rows, BLK), BF), pltpu.VMEM((8, width // 8, wc), BF), pltpu.VMEM(chunks, BF), pltpu.VMEM(chunks, BF),
          pltpu.VMEM(chunks, BF), pltpu.VMEM((small, width), F32), pltpu.VMEM((width // 8, wc), BF), pltpu.VMEM((share, wc), BF),
          pltpu.VMEM((8, width), F32), pltpu.VMEM((small, width), BF), DMA((3,)), DMA((2,)), DMA((2,))]
-        + Scatter.scratch(rows, 2 * HEAD) + Scatter.scratch(small, width) + CoreScatter.scratch(sr, sw)
+        + Scatter.scratch(rows, 2 * HEAD) + Scatter.scratch(small, width) + CoreScatter.scratch(share, dup.shape[1])
+        + CoreScatter.scratch(ddown.shape[0], share)
         + CoreScatter.scratch(2 * HEAD, share) + Scatter.scratch(small, width) + Scatter.scratch(width // 8, wc)
         + Gather.scratch() * 3 + RowSums.scratch(width) + Sums.scratch(*lane.shape),
-        meta, lanes, q, kv, o, do, lse, opart, gb, mid, bias, dup, mixed, n, w, gm, x, gain, early, lane)
+        meta, lanes, q, kv, o, do, lse, opart, gb, mid, bias, dup, ddown, mixed, n, w, gm, x, gain, early, lane)
 
 
 def on_device(tokens, first_gain, first_shift, query_weight, query_bias, key_weight, value_weight, value_bias,
@@ -1088,25 +1134,13 @@
     lanes = jnp.pad(block_order % nblk, (0, HEAD - nblk), constant_values=-1).reshape(1, HEAD)
     row = lambda v: v.reshape(1, -1)
 
-    w_all, n_all, q, kv, o, lse, out_all, up_all, down_all, n2, mid, mixed = forward_call(
+    w_all, n_all, q, kv, o, lse, mid, mixed, do, gm, sums, low, lane, out_part, dw_up, dw_down = front_call(
         meta, lanes, tokens, row(first_gain), row(first_shift), query_weight, key_weight, value_weight, row(query_bias), row(value_bias),
-        out_weight, up_weight, down_weight, row(out_bias), row(second_gain), row(second_shift))
-    n_all = n_all.reshape(2 * own, width)
-    n2 = n2.reshape(own, width)
-    pre = dg(n2, up_all, NN) + up_bias
-    half_erf = 0.5 + 0.5 * lax.erf(pre * math.sqrt(0.5))
-    hidden = (pre * half_erf).astype(BF)
-    slope = half_erf + pre * jnp.exp(-0.5 * pre * pre) * (1.0 / math.sqrt(2.0 * math.pi))
-    grad_pre = (dg(cotangent, down_all, NT) * slope).astype(BF)
-    gn2 = dg(grad_pre, up_all, NT).astype(BF).reshape(8, rows, width)
-    out_part = dg(hidden, down_all, NN).astype(BF).reshape(8, rows, width)
+        out_weight, up_weight, down_weight, row(out_bias), row(second_gain), row(second_shift), cotangent, row(up_bias))
+    layer, up_grad, down_grad, out_grad, dwq, dwk, dwv, tg, small, lane = rear_call(
+        meta, lanes, q, kv, o, do, lse, out_part, low, mid, row(down_bias), dw_up, dw_down, mixed, n_all.reshape(2 * own, width), w_all, gm,
+        tokens, row(first_gain), sums, lane)
     hid = up_weight.shape[1]
-    dw_up = dg(n2, grad_pre, TN).astype(BF).reshape(8, 2, width // 16, hid)
-    dw_down = dg(hidden, cotangent, TN).astype(BF)
-    do, gm, sums, low, down_grad = back_call(gn2, mid, cotangent, out_all, row(second_gain), dw_down)
-    lane = jnp.pad(jnp.sum(grad_pre.astype(F32), axis=0).reshape(hid // 256, 256), ((0, 8 - hid // 256), (0, 0)))
-    layer, up_grad, out_grad, dwq, dwk, dwv, tg, small, lane = rear_call(
-        meta, lanes, q, kv, o, do, lse, out_part, low, mid, row(down_bias), dw_up, mixed, n_all, w_all, gm, tokens, row(first_gain), sums, lane)
     return (
         layer.reshape(own, width),
         tg.reshape(own, width).astype(F32),

time: 379 us -> 343 us (0.905)
  matrix products: 26.5 us -> 0 us
  Pallas kernels: 334 us -> 325 us
    dot_general x6 -> x0, matrix products: 26.5 us -> none  [dg(): return lax.dot_general(a, b, dims, preferred_element_type=F32)]
    pallas_call x3 -> x2, Pallas kernels: 334 us -> 325 us  [remote_call(): pl.pallas_call(kernel, out_shape=outs, in_specs=ins, out_specs=jax.tree.m...]
where the time goes in v5:
time: 343 us
  Pallas kernels  325 us (95%)
  local copies, waits for them, and re-layouts  10.4 us (3%)
  other arithmetic  5.53 us (2%)
    pallas_call x2, Pallas kernels, remote_call(): pl.pallas_call(kernel, out_shape=outs, in_specs=ins, out_specs=jax.tree.m...  325 us

profile of v5, /device:TPU:1, one launch (start us, length us, event | category | flops | bytes accessed | tf_op | source)
XLA Modules:
  0.0 342.6 jit_solution(10385932377102729015)
XLA Ops:
  1.3 0.7 and_select_fusion
  2.0 0.6 pad_add_fusion.meta
  2.6 0.5 pad_bitcast_fusion.lanes_ref
  3.1 169.6 %front.1 = (bf16[2048,384]{1,0:T(8,128)(2,1)}, bf16[2,512,2048]{2,1,0:T(8,128)(2,1)}, bf16[1024,128]{1,0:T(8,128)(2,1)}, bf16[8,1024,256]{2,1,0:T(8,128)(2,1)}, ...) custom-call(s32[33]{0:T(128)} %pad_add_fusion.meta, ...), custom_call_target="tpu_custom_call" | custom-call | tf_op jit(solution)/shard_map/front/pallas_call | solution.py:428
  172.7 155.6 %rear.1 = (bf16[8,64,2048]{2,1,0:T(8,128)(2,1)}, f32[128,1024]{1,0:T(8,128)}, f32[1024,128]{1,0:T(8,128)}, f32[256,128]{1,0:T(8,128)}, f32[128,256]{1,0:T(8,128)...) custom-call(s32[33]{0:T(128)} %pad_add_fusion.meta, ...), custom_call_target="tpu_custom_call" | custom-call | tf_op jit(solution)/shard_map/rear/pallas_call | solution.py:428
  328.3 1.3 fusion.2
  329.7 0.7 slice_bitcast_fusion
  330.4 0.6 copy.36
  331.0 1.7 fusion.1
  332.7 0.0 copy-start
  332.7 4.3 %bitcast_convert_fusion = f32[512,2048]{1,0:T(8,128)} fusion(bf16[8,64,2048]{2,1,0:T(8,128)(2,1)} %get-tuple-element.60), kind=kLoop, calls=%fused_computation | loop fusion | flops 1048576 | bytes 6291456 | tf_op jit(solution)/shard_map/convert_element_type | solution.py:1146
  337.0 0.0 copy-done
  337.0 0.0 copy-start.6
  337.0 0.0 copy-start.5
  337.0 0.0 copy-start.4
  337.0 0.0 copy-start.3
  337.0 0.0 copy-start.2
  337.0 1.3 copy.45
  338.4 0.0 copy-done.6
  338.4 0.0 copy-start.1
  338.4 0.7 copy.46
  339.0 0.0 copy-done.5
  339.0 0.7 copy.47
  339.7 0.0 copy-done.4
  339.7 0.7 copy.48
  340.3 0.0 copy-done.3
  340.3 0.7 copy.49
  341.0 0.0 copy-done.2
  341.0 0.8 copy.50
  341.8 0.0 copy-done.1
  341.8 0.8 copy.51
Async XLA Ops:
  332.7 4.3 %copy-start = (bf16[8,64,2048]{2,1,0:T(8,128)(2,1)S(1)}, bf16[8,64,2048]{2,1,0:T(8,128)(2,1)}, u32[]{:S(2)}) copy-start(bf16[8,64,2048]{2,1,0:T(8,128)(2,1)} %get-tuple-element.59) | copy-start | bytes 6291460
  337.0 1.4 copy-start.6
  337.0 2.0 copy-start.5
  337.0 2.7 copy-start.4
  337.0 3.3 copy-start.3
  337.0 4.0 %copy-start.2 = (f32[128,1024]{1,0:T(8,128)S(1)}, f32[128,1024]{1,0:T(8,128)}, u32[]{:S(2)}) copy-start(f32[128,1024]{1,0:T(8,128)} %get-tuple-element.107) | copy-start | bytes 1572868
  338.4 3.4 %copy-start.1 = (f32[1024,128]{1,0:T(8,128)S(1)}, f32[1024,128]{1,0:T(8,128)}, u32[]{:S(2)}) copy-start(f32[1024,128]{1,0:T(8,128)} %get-tuple-element.109) | copy-start | bytes 1572868

commit v6 on v5

--- a/solution.py
+++ b/solution.py
@@ -484,10 +484,9 @@
 
 
 def front_kernel(meta, lanes_ref, x_ref, gain1_ref, shift1_ref, wq_ref, wk_ref, wv_ref, qb_ref, vb_ref, wo_ref, wu_ref, wd_ref,
-                 bias_ref, gain2_ref, shift2_ref, cot_ref, ub_ref,
-                 w_hbm, n_hbm, q_out, kv_hbm, o_ref, lse_ref, mid_out, own_out, do_out, gm_out, sums_out, low_out, lane_out, opart_out, du_hbm, dd_hbm,
-                 w_vm, n_vm, kv_vm, out_vm, up_vm, down_vm, wsh, qa_ref, kx_ref, m_ref, acc_ref, mixed,
-                 n2, gh, hidden, gp, gpart, gsum, colsum, du_buf, dd_buf,
+                 bias_ref, gain2_ref, shift2_ref, cot_ref, ub_ref, db_ref,
+                 w_hbm, n_hbm, q_out, kv_hbm, o_ref, lse_ref, mid_out, own_out, do_out, gm_out, sums_out, low_out, lane_out, lay_out, du_hbm, dd_hbm, dup_out,
+                 w_vm, n_vm, kv_vm, out_vm, up_vm, down_vm, wsh, mixed, n2, gsum, colsum,
                  lsem, css, crs, ass, ars, hss, hrs, *sems):
     gd, gt = Eight("dp"), Eight("tensor")
     t = gt.t
@@ -497,7 +496,7 @@
     me = gd.index(gd.r, gd.p)
     own = x_ref.shape[0]
     rows = 2 * own
-    nblk = kx_ref.shape[0] // BLK
+    nblk = 8 * rows // BLK
     per = rows // BLK
     shard = wq_ref.shape[0]
     half = out_vm.shape[1] // 2
@@ -522,11 +521,12 @@
     downs = Gather(gd, lambda m: down_vm.at[:, row_of(m)], hid, sems[12:16], core)
     wide = Gather(gt, lambda m: out_vm.at[m, pl.ds(pl.multiple_of(c * half, half), half)], half, sems[16:20], core, twin_own=False)
     normed = Gather(gt, lambda m: n2.at[pl.ds(pl.multiple_of(m * small, small), small)], small, sems[20:22])
-    back = Scatter(gt, lambda m: gpart.at[m], small, sems[22:28], 32)
+    spare = lambda k: (lambda m: n_vm.at[k, pl.ds(pl.multiple_of(m * small, small), small)])
+    back = Scatter(gt, spare(0), small, sems[22:28], 32)
+    result = Scatter(gt, spare(1), small, sems[28:34], 32)
+    grads = CoreScatter(gd, lambda m, cc: du_hbm.at[pl.ds(pl.multiple_of((m * 2 + cc) * shard, shard), shard)], shard, sems[34:45], 32)
     swap.wait_recv()
     qkv.start()
-    out_vm[t, :, mine] = wo_ref[...].astype(BF)
-    outs.start()
 
     def norm_part(k):
         step = 32
@@ -541,23 +541,20 @@
         return send(n_vm.at[c, at], n_vm.at[c, at], csem, 1 + k, core)
 
     there = [norm_part(0)]
+    qkv.forward_pair()
+    qkv.forward(0)
+    out_vm[t, :, mine] = wo_ref[...].astype(BF)
+    outs.start()
+    there.append(norm_part(1))
+    qkv.forward(1)
+    up_vm[mine, :] = wu_ref[...].astype(BF)
+    down_vm[:, mine] = wd_ref[...].astype(BF)
     outs.forward_pair()
     outs.forward(0)
-    qkv.forward_pair()
-    qkv.forward(0)
-    there.append(norm_part(1))
-    outs.forward(1)
-    outs.arrive(0)
-    qkv.forward(1)
-    up_vm[mine, :] = wu_ref[...].astype(BF)
-    outs.arrive(1)
-    down_vm[:, mine] = wd_ref[...].astype(BF)
-    outs.settle()
-    wide.start()
     qkv.arrive(0)
-    qkv.arrive(1)
     for copy in there:
         copy.wait_recv()
+    qkv.arrive(1)
     local = pl.ds(pl.multiple_of(c * HEAD, HEAD), HEAD)
     bias_q, bias_v = qb_ref[:, local], vb_ref[:, local]
 
@@ -570,81 +567,90 @@
         kv_vm[me, at, HEAD:] = (piece[:, 2 * HEAD:] + bias_v).astype(BF)
 
     keys.start()
+    outs.forward(1)
     saves = [pltpu.make_async_copy(w_vm, w_hbm, lsem.at[0]), pltpu.make_async_copy(n_vm, n_hbm, lsem.at[1])]
     for save in saves:
         save.start()
-    augment(meta, lanes_ref, q_out, qa_ref, kx_ref)
-    m_ref[...] = jnp.full_like(m_ref, -1e30)
-    acc_ref[...] = jnp.zeros_like(acc_ref)
-    ones = jnp.ones((BLK, HEAD), BF)
-    prefix = meta[nblk]
-
-    def attend(chunk, diagonal):
-        ks, vs = [], []
-        for i in range(per):
-            at = pl.ds(pl.multiple_of(chunk * rows + i * BLK, BLK), BLK)
-            ks.append(jnp.concatenate([kv_vm[chunk, i * BLK:(i + 1) * BLK, :HEAD], kx_ref[at, :]], axis=1))
-            vs.append(jnp.concatenate([kv_vm[chunk, i * BLK:(i + 1) * BLK, HEAD:], ones], axis=1))
+    def attention(qa_ref, kx_ref, m_ref, acc_ref):
+        augment(meta, lanes_ref, q_out, qa_ref, kx_ref)
+        outs.arrive(0)
+        outs.arrive(1)
+        outs.settle()
+        wide.start()
+        m_ref[...] = jnp.full_like(m_ref, -1e30)
+        acc_ref[...] = jnp.zeros_like(acc_ref)
+        ones = jnp.ones((BLK, HEAD), BF)
+        prefix = meta[nblk]
+
+        def attend(chunk, diagonal):
+            ks, vs = [], []
+            for i in range(per):
+                at = pl.ds(pl.multiple_of(chunk * rows + i * BLK, BLK), BLK)
+                ks.append(jnp.concatenate([kv_vm[chunk, i * BLK:(i + 1) * BLK, :HEAD], kx_ref[at, :]], axis=1))
+                vs.append(jnp.concatenate([kv_vm[chunk, i * BLK:(i + 1) * BLK, HEAD:], ones], axis=1))
+            for a in range(per):
+                take = slice(a * BLK, (a + 1) * BLK)
+                q = qa_ref[take, :]
+                ss = [dg(q, k, NT) for k in ks]
+                if diagonal:
+                    edge = prefix - 1 - meta[first_block() + a] * BLK
+                    lim = jnp.maximum(lax.broadcasted_iota(jnp.int32, (BLK, BLK), 0), edge)
+                    key = lax.broadcasted_iota(jnp.int32, (BLK, BLK), 1)
+                    ss[a] = jnp.where(key <= lim, ss[a], NEG)
+                top = ss[0]
+                for s in ss[1:]:
+                    top = jnp.maximum(top, s)
+                old = m_ref[take, :1]
+                new = jnp.maximum(old, jnp.max(top, axis=1, keepdims=True) * C1)
+                alpha = jnp.exp2(old - new)
+                add = None
+                for s, v in zip(ss, vs):
+                    term = jnp.dot(jnp.exp2(s * C1 - new).astype(BF), v, preferred_element_type=F32)
+                    add = term if add is None else add + term
+                acc_ref[take, :] = acc_ref[take, :] * alpha + add
+                m_ref[take, :] = jnp.broadcast_to(new, (BLK, HEAD))
+
+        attend(me, True)
+
+        @pl.loop(1, 8)
+        def _(k):
+            kk = lax.rem(k, 4)
+            i, s = kk + kk // 2 - 2 * (kk // 3), k // 4
+
+            @pl.when(k == 1)
+            def _():
+                keys.forward_pair()
+                keys.forward(0)
+
+            @pl.when(k == 2)
+            def _():
+                wide.forward_pair()
+                wide.forward(0)
+
+            @pl.when(k == 3)
+            def _():
+                keys.arrive(0)
+
+            @pl.when(k == 5)
+            def _():
+                keys.forward(1)
+                wide.forward(1)
+                ups.start()
+
+            @pl.when(k == 7)
+            def _():
+                keys.arrive(1)
+
+            attend(gd.index(gd.ring(i), gd.p + s * (1 - 2 * gd.p)), False)
+
         for a in range(per):
-            take = slice(a * BLK, (a + 1) * BLK)
-            q = qa_ref[take, :]
-            ss = [dg(q, k, NT) for k in ks]
-            if diagonal:
-                edge = prefix - 1 - meta[first_block() + a] * BLK
-                lim = jnp.maximum(lax.broadcasted_iota(jnp.int32, (BLK, BLK), 0), edge)
-                key = lax.broadcasted_iota(jnp.int32, (BLK, BLK), 1)
-                ss[a] = jnp.where(key <= lim, ss[a], NEG)
-            top = ss[0]
-            for s in ss[1:]:
-                top = jnp.maximum(top, s)
-            old = m_ref[take, :1]
-            new = jnp.maximum(old, jnp.max(top, axis=1, keepdims=True) * C1)
-            alpha = jnp.exp2(old - new)
-            add = None
-            for s, v in zip(ss, vs):
-                term = jnp.dot(jnp.exp2(s * C1 - new).astype(BF), v, preferred_element_type=F32)
-                add = term if add is None else add + term
-            acc_ref[take, :] = acc_ref[take, :] * alpha + add
-            m_ref[take, :] = jnp.broadcast_to(new, (BLK, HEAD))
-
-    attend(me, True)
-
-    @pl.loop(1, 8)
-    def _(k):
-        kk = lax.rem(k, 4)
-        i, s = kk + kk // 2 - 2 * (kk // 3), k // 4
-
-        @pl.when(k == 1)
-        def _():
-            keys.forward_pair()
-            keys.forward(0)
-
-        @pl.when(k == 2)
-        def _():
-            wide.forward_pair()
-            wide.forward(0)
-
-        @pl.when(k == 3)
-        def _():
-            keys.arrive(0)
-
-        @pl.when(k == 5)
-        def _():
-            keys.forward(1)
-            wide.forward(1)
-            ups.start()
-
-        @pl.when(k == 7)
-        def _():
-            keys.arrive(1)
-
-        attend(gd.index(gd.ring(i), gd.p + s * (1 - 2 * gd.p)), False)
-
-    for a in range(per):
-        at = slice(a * BLK, (a + 1) * BLK)
-        total = acc_ref[at, HEAD:]
-        o_ref[at, :] = (acc_ref[at, :HEAD] / total).astype(BF)
-        lse_ref[a:a + 1, :] = jnp.transpose(m_ref[at, :] + jnp.log2(total))[:1, :]
+            at = slice(a * BLK, (a + 1) * BLK)
+            total = acc_ref[at, HEAD:]
+            o_ref[at, :] = (acc_ref[at, :HEAD] / total).astype(BF)
+            lse_ref[a:a + 1, :] = jnp.transpose(m_ref[at, :] + jnp.log2(total))[:1, :]
+
+    pl.run_scoped(
+        attention, pltpu.VMEM((rows, 2 * HEAD), BF), pltpu.VMEM((8 * rows, HEAD), BF), pltpu.VMEM((rows, HEAD), F32), pltpu.VMEM((rows, 2 * HEAD), F32))
     head = pl.ds(pl.multiple_of((2 * t + c) * HEAD, HEAD), HEAD)
     copies = []
     for k, (tt, cc, device) in enumerate(members):
@@ -690,76 +696,81 @@
     downs.arrive(0)
     downs.arrive(1)
     downs.settle()
+    saves.pop(1).wait()
+    for copy in there:
+        copy.wait_send()
     blocks = [(slice(n * span, (n + 1) * span)) for n in range(hid // span)]
-
-    @pl.loop(0, own // BLK)
-    def _(b):
-        at = pl.ds(pl.multiple_of(b * BLK, BLK), BLK)
-        for cols in blocks:
-            gh[at, cols] = dg(cot_ref[at, :], down_vm[cols, :], NT)
-
-    normed.arrive(0)
-    normed.arrive(1)
-    normed.settle()
-    colsum[...] = jnp.zeros_like(colsum)
     wide_blocks = [(slice(n * span, (n + 1) * span)) for n in range(n2.shape[1] // span)]
 
-    @pl.loop(0, own // BLK)
-    def _(b):
-        at = pl.ds(pl.multiple_of(b * BLK, BLK), BLK)
-        for cols in blocks:
-            pre = dg(n2[at, :], up_vm[:, cols], NN) + ub_ref[:, cols]
-            half_erf = 0.5 + 0.5 * lax.erf(pre * math.sqrt(0.5))
-            hidden[at, cols] = (pre * half_erf).astype(BF)
-            slope = half_erf + pre * jnp.exp(-0.5 * pre * pre) * (1.0 / math.sqrt(2.0 * math.pi))
-            low = (gh[at, cols] * slope).astype(BF)
-            gp[at, cols] = low
-            colsum[0:1, cols] += jnp.sum(low.astype(F32), axis=0, keepdims=True)
-        for cols in wide_blocks:
-            piece = dg(gp[at, :], up_vm[cols, :], NT).astype(BF)
-            for j in range(BLK // small):
-                gpart[b * (BLK // small) + j, :, cols] = piece[j * small:(j + 1) * small]
-
-    back.start()
-
-    @pl.loop(0, own // BLK)
-    def _(b):
-        at = pl.ds(pl.multiple_of(b * BLK, BLK), BLK)
-        for cols in wide_blocks:
-            piece = dg(hidden[at, :], down_vm[:, cols], NN).astype(BF)
-            for j in range(BLK // small):
-                opart_out[b * (BLK // small) + j, :, cols] = piece[j * small:(j + 1) * small]
-
-    back.add_near(1)
-    back.add_near(0)
-
-    def du_save(m):
-        slot = lax.rem(m, 2)
-        return pltpu.make_async_copy(du_buf.at[slot], du_hbm.at[pl.ds(pl.multiple_of(m * BLK, BLK), BLK)], lsem.at[3 + slot])
-
-    def dd_save(m):
-        slot = lax.rem(m, 2)
-        return pltpu.make_async_copy(dd_buf.at[slot], dd_hbm.at[:, pl.ds(pl.multiple_of(m * BLK, BLK), BLK)], lsem.at[5 + slot])
-
-    def weight_grads(low, high):
-        @pl.loop(low, high)
-        def _(m):
+    def feed_forward(gh, hidden, gp, du_buf, dd_buf):
+        @pl.loop(0, own // BLK)
+        def _(b):
+            at = pl.ds(pl.multiple_of(b * BLK, BLK), BLK)
+            for cols in blocks:
+                gh[at, cols] = dg(cot_ref[at, :], down_vm[cols, :], NT)
+
+        normed.arrive(0)
+        normed.arrive(1)
+        normed.settle()
+        colsum[...] = jnp.zeros_like(colsum)
+
+        @pl.loop(0, own // BLK)
+        def _(b):
+            at = pl.ds(pl.multiple_of(b * BLK, BLK), BLK)
+            for cols in blocks:
+                pre = dg(n2[at, :], up_vm[:, cols], NN) + ub_ref[:, cols]
+                half_erf = 0.5 + 0.5 * lax.erf(pre * math.sqrt(0.5))
+                hidden[at, cols] = (pre * half_erf).astype(BF)
+                slope = half_erf + pre * jnp.exp(-0.5 * pre * pre) * (1.0 / math.sqrt(2.0 * math.pi))
+                low = (gh[at, cols] * slope).astype(BF)
+                gp[at, cols] = low
+                colsum[0:1, cols] += jnp.sum(low.astype(F32), axis=0, keepdims=True)
+            for cols in wide_blocks:
+                n_vm[0, at, cols] = dg(gp[at, :], up_vm[cols, :], NT).astype(BF)
+
+        back.start()
+
+        def du_save(m):
             slot = lax.rem(m, 2)
-            cols = pl.ds(pl.multiple_of(m * BLK, BLK), BLK)
-
-            @pl.when(m > 1)
-            def _():
-                du_save(m - 2).wait()
-                dd_save(m - 2).wait()
-
-            du_buf[slot] = dg(n2[:, cols], gp[...], TN).astype(BF)
-            du_save(m).start()
-            dd_buf[slot] = dg(hidden[...], cot_ref[:, cols], TN).astype(BF)
-            dd_save(m).start()
-
-    weight_grads(0, 4)
-    back.add_pair()
-    weight_grads(4, 8)
+            return pltpu.make_async_copy(du_buf.at[slot], du_hbm.at[pl.ds(pl.multiple_of(m * BLK, BLK), BLK)], lsem.at[3 + slot])
+
+        def dd_save(m):
+            slot = lax.rem(m, 2)
+            return pltpu.make_async_copy(dd_buf.at[slot], dd_hbm.at[:, pl.ds(pl.multiple_of(m * BLK, BLK), BLK)], lsem.at[5 + slot])
+
+        def blocks_of(save, buf, value):
+            @pl.loop(0, 8)
+            def _(m):
+                @pl.when(m > 1)
+                def _():
+                    save(m - 2).wait()
+
+                buf[lax.rem(m, 2)] = value(pl.ds(pl.multiple_of(m * BLK, BLK), BLK)).astype(BF)
+                save(m).start()
+
+        blocks_of(du_save, du_buf, lambda cols: dg(n2[:, cols], gp[...], TN))
+        back.add_near(1)
+        back.add_near(0)
+        du_save(6).wait()
+        du_save(7).wait()
+        grads.start()
+
+        @pl.loop(0, own // BLK)
+        def _(b):
+            at = pl.ds(pl.multiple_of(b * BLK, BLK), BLK)
+            for cols in wide_blocks:
+                n_vm[1, at, cols] = dg(hidden[at, :], down_vm[:, cols], NN).astype(BF)
+
+        back.add_pair()
+        result.start()
+        grads.add()
+        blocks_of(dd_save, dd_buf, lambda cols: dg(hidden[...], cot_ref[:, cols], TN))
+        dd_save(6).wait()
+        dd_save(7).wait()
+
+    pl.run_scoped(
+        feed_forward, pltpu.VMEM((own, hid), F32), pltpu.VMEM((own, hid), BF), pltpu.VMEM((own, hid), BF), pltpu.VMEM((2, BLK, hid), BF),
+        pltpu.VMEM((2, hid, BLK), BF))
 
     def keep(at, value):
         gsum[at, :] = value
@@ -781,6 +792,11 @@
         cols = pl.ds(pl.multiple_of((2 * tt + cc) * HEAD, HEAD), HEAD)
         heads.append(send(mixed.at[:, cols], do_out.at[take], hsem, k, device))
     do_out[take, :] = mixed[:, head]
+    result.add_near(1)
+    result.add_near(0)
+    grads.inner.add_near(1)
+    grads.inner.add_near(0)
+    result.add_pair()
     sums_out[...] = jnp.zeros_like(sums_out)
     sums_out[0:1, :] = jnp.sum(grad * scaled, axis=0, keepdims=True)
     sums_out[1:2, :] = jnp.sum(grad, axis=0, keepdims=True)
@@ -789,13 +805,20 @@
     lane_out[...] = jnp.zeros_like(lane_out)
     for j in range(hid // 256):
         lane_out[j:j + 1, :] = colsum[0:1, j * 256:(j + 1) * 256]
-    du_save(6).wait()
-    dd_save(6).wait()
-    du_save(7).wait()
-    dd_save(7).wait()
+    grads.inner.add_pair()
+
+    def lay(at, value):
+        lay_out[at, :] = (mid_out[at, :] + (value + db_ref[...])).astype(BF)
+
+    result.finish(lay)
+
+    def keep_up(at, value):
+        dup_out[at, :] = value
+
+    grads.finish(keep_up)
     qkv.settle()
     swap.wait_send()
-    for copy in there + copies:
+    for copy in copies:
         copy.wait_send()
     for save in saves:
         save.wait()
@@ -803,34 +826,30 @@
         copy.wait()
 
 
-def front_call(meta, lanes, x, gain1, shift1, wq, wk, wv, qb, vb, wo, wu, wd, bias, gain2, shift2, cot, ub):
+def front_call(meta, lanes, x, gain1, shift1, wq, wk, wv, qb, vb, wo, wu, wd, bias, gain2, shift2, cot, ub, db):
     own, width = x.shape
     rows, shard, hid, small = 2 * own, wq.shape[0], wu.shape[1], own // 8
     hbm = pl.BlockSpec(memory_space=pl.ANY)
     big = [(width, 3 * HEAD), (2, own, width), (8, rows, 2 * HEAD), (8, 2 * HEAD, width), (width, hid), (hid, width)]
     w, n, kv, out, up, down = (struct(s, BF) for s in big)
-    chunks = (8, small, width)
     outs = (w, n, struct((rows, HEAD), BF), kv, struct((rows, HEAD), BF), struct((rows // BLK, BLK), F32),
             struct((small, width), F32), struct((own, 2 * HEAD), BF), struct((rows, HEAD), BF), struct((small, width), F32),
-            struct((8, width), F32), struct((small, width), BF), struct((8, 256), F32), struct(chunks, BF), up, down)
+            struct((8, width), F32), struct((small, width), BF), struct((8, 256), F32), struct((small, width), BF), up, down, struct((shard, hid), F32))
     return remote_call(
-        front_kernel, "front", 1, outs, [SM] + [VM] * 17,
+        front_kernel, "front", 1, outs, [SM] + [VM] * 18,
         [pltpu.VMEM(s, BF) for s in big]
-        + [pltpu.VMEM((2, shard, 3 * HEAD), BF), pltpu.VMEM((rows, 2 * HEAD), BF), pltpu.VMEM((8 * rows, HEAD), BF),
-           pltpu.VMEM((rows, HEAD), F32), pltpu.VMEM((rows, 2 * HEAD), F32), pltpu.VMEM((small, width), BF),
-           pltpu.VMEM((own, width), BF), pltpu.VMEM((own, hid), F32), pltpu.VMEM((own, hid), BF), pltpu.VMEM((own, hid), BF),
-           pltpu.VMEM(chunks, BF), pltpu.VMEM((small, width), F32), pltpu.VMEM((8, hid), F32),
-           pltpu.VMEM((2, BLK, hid), BF), pltpu.VMEM((2, hid, BLK), BF),
+        + [pltpu.VMEM((2, shard, 3 * HEAD), BF), pltpu.VMEM((small, width), BF), pltpu.VMEM((own, width), BF),
+           pltpu.VMEM((small, width), F32), pltpu.VMEM((8, hid), F32),
            DMA((7,)), DMA((3,)), DMA((3,)), DMA((16,)), DMA((16,)), DMA((15,)), DMA((15,))]
-        + Gather.scratch() * 2 + Gather.scratch(True) * 4 + Gather.scratch() + Scatter.scratch(small, width),
-        meta, lanes, x, gain1, shift1, wq, wk, wv, qb, vb, wo, wu, wd, bias, gain2, shift2, cot, ub,
-        out_specs=(hbm, hbm, VM, hbm) + (VM,) * 10 + (hbm, hbm))
-
-
-def rear_kernel(meta, lanes_ref, q_ref, kv_ref, o_ref, do_ref, lse_ref, opart_ref, gbr_ref, mid_ref, bias_ref, dup_hbm, ddown_hbm,
+        + Gather.scratch() * 2 + Gather.scratch(True) * 4 + Gather.scratch() + Scatter.scratch(small, width) * 2 + CoreScatter.scratch(shard, hid),
+        meta, lanes, x, gain1, shift1, wq, wk, wv, qb, vb, wo, wu, wd, bias, gain2, shift2, cot, ub, db,
+        out_specs=(hbm, hbm, VM, hbm) + (VM,) * 10 + (hbm, hbm, VM))
+
+
+def rear_kernel(meta, lanes_ref, q_ref, kv_hbm, o_ref, do_ref, lse_ref, gbr_ref, layr_ref, ddown_hbm,
                 mixed_ref, n_hbm, w_ref, gm_ref, x_hbm, gain_ref, early_ref, lane_ref,
-                lay_out, dup_out, ddown_out, dwo_out, dwq_out, dwk_out, dwv_out, tg_out, sums_out, lanes_out,
-                qa_ref, kx_ref, part, delta_ref, dq_acc, gb, dqkv, dwo, n_buf, dw, away, arrived, summed, total, mine_w, there_w, vec, x_ref,
+                lay_out, ddown_out, dwo_out, dwq_out, dwk_out, dwv_out, tg_out, sums_out, lanes_out,
+                kv_ref, qa_ref, kx_ref, part, delta_ref, dq_acc, gb, dqkv, dwo, n_buf, dw, away, arrived, summed, total, mine_w, there_w, vec, x_ref,
                 lsem, css, crs, *scratch):
     g, gt = Eight("dp"), Eight("tensor")
     c = lax.rem(g.d, 2)
@@ -840,7 +859,16 @@
     own = rows // 2
     nblk = kx_ref.shape[0] // BLK
     per = rows // BLK
-    small, width = mid_ref.shape
+    small, width = gm_ref.shape
+    order = [(2, 1), (1, 1), (3, 1), (2, 0), (1, 0), (3, 0), (0, 1), (0, 0)]
+
+    def kv_load(n):
+        i, s = order[n]
+        m = g.index(g.ring(i), g.side(s))
+        return pltpu.make_async_copy(kv_hbm.at[m], kv_ref.at[m], lsem.at[3 + n])
+
+    for n in range(8):
+        kv_load(n).start()
     everyone = [(lax.rem(g.d + k, 16), g.t) for k in range(1, 16)] + [(g.d, lax.rem(g.t + k, 8)) for k in range(1, 8)]
     greet(everyone)
     take = list(scratch)
@@ -853,8 +881,6 @@
     share = dwo_out.shape[1]
     by_columns = lambda m, cc: dwo.at[:, pl.ds(pl.multiple_of((m * 2 + cc) * share, share), share)]
     keys = Scatter(g, lambda m: part.at[m], rows, some(6), 128)
-    outs = Scatter(gt, lambda m: opart_ref.at[m], small, some(6), 32)
-    ups = CoreScatter(g, lambda m, cc: dup_hbm.at[pl.ds(pl.multiple_of((m * 2 + cc) * share, share), share)], share, some(CoreScatter.COUNT), 32)
     downs = CoreScatter(
         g, lambda m, cc: ddown_hbm.at[:, pl.ds(pl.multiple_of((m * 2 + cc) * share, share), share)], ddown_out.shape[0], some(CoreScatter.COUNT), 128)
     dwos = CoreScatter(g, by_columns, dwo_out.shape[0], some(CoreScatter.COUNT), 128)
@@ -873,11 +899,11 @@
         slot = lax.rem(m, 2)
         return pltpu.make_async_copy(n_hbm.at[:, pl.ds(pl.multiple_of(m * BLK, BLK), BLK)], n_buf.at[slot], lsem.at[slot])
 
-    ups.start()
     downs.start()
-    outs.start()
+    lay_out[mine_t] = layr_ref[...]
     gb[pl.ds(pl.multiple_of(mine_t * small, small), small), :] = gbr_ref[...]
     wide.start()
+    layer.start()
     augment(meta, lanes_ref, q_ref, qa_ref, kx_ref)
     for a in range(per):
         at = slice(a * BLK, (a + 1) * BLK)
@@ -914,6 +940,9 @@
             part[chunk, at_k, :HEAD] = (dk * SCALE).astype(BF)
             part[chunk, at_k, HEAD:] = dv.astype(BF)
 
+    for n in range(8):
+        kv_load(n).wait()
+
     @pl.loop(0, 7)
     def _(k):
         kk = lax.rem(k, 3)
@@ -924,31 +953,27 @@
         @pl.when(k == 0)
         def _():
             keys.send_far(1)
-            ups.add()
-            outs.add_near(1)
             wide.forward_pair()
             wide.forward(0)
 
         @pl.when(k == 1)
         def _():
-            outs.add_near(0)
+            layer.forward_pair()
+            layer.forward(0)
 
         @pl.when(k == 2)
         def _():
             keys.send_near(1)
             keys.add_near(1)
-            outs.add_pair()
             wide.forward(1)
 
         @pl.when(k == 3)
         def _():
             keys.send_far(0)
-            ups.inner.add_near(1)
-            downs.add()
 
         @pl.when(k == 4)
         def _():
-            ups.inner.add_near(0)
+            layer.forward(1)
 
         @pl.when(k == 5)
         def _():
@@ -958,19 +983,10 @@
         @pl.when(k == 6)
         def _():
             keys.add_pair()
-            ups.inner.add_pair()
-
-    def lay(at, value):
-        lay_out[mine_t, at, :] = (mid_ref[at, :] + (value + bias_ref[...])).astype(BF)
-
-    outs.finish(lay)
-    layer.start()
-    downs.inner.add_near(1)
+
     n_load(0).start()
     attend(me, True)
     dqkv[:, :HEAD] = jnp.transpose(dq_acc[...] * SCALE).astype(BF)
-    layer.forward_pair()
-    layer.forward(0)
     wide.arrive(0)
     wide.arrive(1)
     wide.settle()
@@ -979,8 +995,6 @@
         cols = pl.ds(n * span, span)
         dwo[:, cols] = dg(mixed_ref[...], gb[:, cols], TN).astype(BF)
     dwos.start()
-    layer.forward(1)
-    downs.inner.add_near(0)
 
     def keep_keys(at, value):
         dqkv[at, HEAD:] = value.astype(BF)
@@ -1000,6 +1014,7 @@
     project(away, 1 - c)
     swap = send(away, arrived, csem, 0, core)
     project(summed, c)
+    downs.add()
     swap.wait_recv()
 
     @pl.loop(0, 8)
@@ -1021,6 +1036,9 @@
         dw[m] = dg(n_buf[lax.rem(m, 2)], dqkv[...], TN).astype(BF)
 
     weights.start()
+    tokens.add_near(1)
+    tokens.add_near(0)
+    tokens.add_pair()
     dwos.add()
     slot = lane_sums.slots
     slot[g.d] = lane_ref[...]
@@ -1028,13 +1046,8 @@
     slot[g.d, 4:5, local] = jnp.sum(dqkv[:, :HEAD].astype(F32), axis=0, keepdims=True)
     slot[g.d, 5:6, local] = jnp.sum(dqkv[:, 2 * HEAD:].astype(F32), axis=0, keepdims=True)
     lane_sums.start()
-    tokens.add_near(1)
-    tokens.add_near(0)
-    tokens.add_pair()
-    weights.add_near(1)
-    weights.add_near(0)
-    dwos.inner.add_near(1)
-    dwos.inner.add_near(0)
+    downs.inner.add_near(1)
+    downs.inner.add_near(0)
 
     def keep(at, value):
         total[at, :] = value
@@ -1050,20 +1063,17 @@
     vec[4:5, :] = jnp.sum(grad * scaled, axis=0, keepdims=True)
     vec[5:6, :] = jnp.sum(grad, axis=0, keepdims=True)
     sums.start()
+    weights.add_near(1)
+    weights.add_near(0)
+    final.forward_pair()
+    final.forward(0)
+    dwos.inner.add_near(1)
+    dwos.inner.add_near(0)
+    downs.inner.add_pair()
+    sums.middle()
     weights.add_pair()
+    final.forward(1)
     dwos.inner.add_pair()
-    downs.inner.add_pair()
-
-    def keep_up(at, value):
-        dup_out[at, :] = value
-
-    ups.finish(keep_up)
-
-    def keep_down(at, value):
-        ddown_out[at, :] = value
-
-    downs.finish(keep_down)
-    sums.middle()
 
     def keep_w(at, value):
         mine_w[at, :] = value.astype(BF)
@@ -1071,35 +1081,37 @@
     weights.finish(keep_w)
     part_rows = there_w.shape[0]
     there = send(mine_w.at[pl.ds(pl.multiple_of((1 - c) * part_rows, part_rows), part_rows)], there_w, csem, 1, core)
-    final.forward_pair()
-    final.forward(0)
+
+    def keep_down(at, value):
+        ddown_out[at, :] = value
+
+    downs.finish(keep_down)
+    sums.finish()
+
+    def keep_o(at, value):
+        dwo_out[at, :] = value
+
+    dwos.finish(keep_o)
     kept = mine_w[pl.ds(pl.multiple_of(c * part_rows, part_rows), part_rows), :].astype(F32)
-    sums.finish()
     far = pl.ds(pl.multiple_of((1 - c) * HEAD, HEAD), HEAD)
     there.wait()
     for i, ref in enumerate((dwq_out, dwk_out, dwv_out)):
         ref[:, local] = kept[:, i * HEAD:(i + 1) * HEAD]
         ref[:, far] = there_w[:, i * HEAD:(i + 1) * HEAD].astype(F32)
-    final.forward(1)
+    lanes_out[...] = lane_sums.finish()
     layer.arrive(0)
     layer.arrive(1)
     layer.settle()
-
-    def keep_o(at, value):
-        dwo_out[at, :] = value
-
-    dwos.finish(keep_o)
-    lanes_out[...] = lane_sums.finish()
-    sums.settle()
     final.arrive(0)
     final.arrive(1)
+    sums.settle()
     final.settle()
     swap.wait_send()
 
 
-def rear_call(meta, lanes, q, kv, o, do, lse, opart, gb, mid, bias, dup, ddown, mixed, n, w, gm, x, gain, early, lane):
+def rear_call(meta, lanes, q, kv, o, do, lse, gb, lay, ddown, mixed, n, w, gm, x, gain, early, lane):
     rows = q.shape[0]
-    small, width = mid.shape
+    small, width = gm.shape
     hbm = pl.BlockSpec(memory_space=pl.ANY)
     chunks = (8, small, width)
     wc = 3 * HEAD
@@ -1107,19 +1119,64 @@
     head_grad = struct((share, 2 * HEAD), F32)
     return remote_call(
         rear_kernel, "rear", 5,
-        (struct(chunks, BF), struct((share, dup.shape[1]), F32), struct((ddown.shape[0], share), F32), struct((2 * HEAD, share), F32), head_grad, head_grad, head_grad,
+        (struct(chunks, BF), struct((ddown.shape[0], share), F32), struct((2 * HEAD, share), F32), head_grad, head_grad, head_grad,
          struct(chunks, BF), struct((8, width), F32), struct(lane.shape, F32)),
-        [SM] + [VM] * 10 + [hbm, hbm, VM] + [hbm, VM, VM, hbm] + [VM] * 3,
-        [pltpu.VMEM((rows, 2 * HEAD), BF), pltpu.VMEM((8 * rows, HEAD), BF), pltpu.VMEM(kv.shape, BF), pltpu.VMEM((8, rows), F32),
+        [SM, VM, VM, hbm] + [VM] * 5 + [hbm, VM] + [hbm, VM, VM, hbm] + [VM] * 3,
+        [pltpu.VMEM(kv.shape, BF), pltpu.VMEM((rows, 2 * HEAD), BF), pltpu.VMEM((8 * rows, HEAD), BF), pltpu.VMEM(kv.shape, BF), pltpu.VMEM((8, rows), F32),
          pltpu.VMEM((HEAD, rows), F32), pltpu.VMEM((8 * small, width), BF), pltpu.VMEM((rows, wc), BF), pltpu.VMEM((2 * HEAD, width), BF),
          pltpu.VMEM((2, rows, BLK), BF), pltpu.VMEM((8, width // 8, wc), BF), pltpu.VMEM(chunks, BF), pltpu.VMEM(chunks, BF),
          pltpu.VMEM(chunks, BF), pltpu.VMEM((small, width), F32), pltpu.VMEM((width // 8, wc), BF), pltpu.VMEM((share, wc), BF),
-         pltpu.VMEM((8, width), F32), pltpu.VMEM((small, width), BF), DMA((3,)), DMA((2,)), DMA((2,))]
-        + Scatter.scratch(rows, 2 * HEAD) + Scatter.scratch(small, width) + CoreScatter.scratch(share, dup.shape[1])
-        + CoreScatter.scratch(ddown.shape[0], share)
+         pltpu.VMEM((8, width), F32), pltpu.VMEM((small, width), BF), DMA((11,)), DMA((2,)), DMA((2,))]
+        + Scatter.scratch(rows, 2 * HEAD) + CoreScatter.scratch(ddown.shape[0], share)
         + CoreScatter.scratch(2 * HEAD, share) + Scatter.scratch(small, width) + Scatter.scratch(width // 8, wc)
         + Gather.scratch() * 3 + RowSums.scratch(width) + Sums.scratch(*lane.shape),
-        meta, lanes, q, kv, o, do, lse, opart, gb, mid, bias, dup, ddown, mixed, n, w, gm, x, gain, early, lane)
+        meta, lanes, q, kv, o, do, lse, gb, lay, ddown, mixed, n, w, gm, x, gain, early, lane)
+
+
+def finish_kernel(layer, tg, small_ref, lane_ref, up, down, out, wq, wk, wv,
+                  layer_out, tg_out, gain1, shift1, qb, vb, ob, gain2, shift2, ub, db, up_out, down_out, out_out, wq_out, wk_out, wv_out,
+                  low, high, *scratch):
+    ways = ((layer, layer_out), (up, up_out), (down, down_out), (out, out_out), (wq, wq_out), (wk, wk_out), (wv, wv_out))
+    buffers, (insem, outsem, tin, tout) = scratch[:7], scratch[7:]
+    parts = tg.shape[0]
+    loads = [pltpu.make_async_copy(tg.at[k], low.at[k], tin.at[k]) for k in range(parts)]
+    saves = [pltpu.make_async_copy(high.at[k], tg_out.at[k], tout.at[k]) for k in range(parts)]
+    there = [pltpu.make_async_copy(way[0], buffer, insem.at[k]) for k, (way, buffer) in enumerate(zip(ways, buffers))]
+    back = [pltpu.make_async_copy(buffer, way[1], outsem.at[k]) for k, (way, buffer) in enumerate(zip(ways, buffers))]
+    for copy in loads + there:
+        copy.start()
+    for k, ref in ((4, gain1), (5, shift1), (2, ob), (0, gain2), (1, shift2), (3, db)):
+        ref[...] = small_ref[k:k + 1, :]
+    for j in range(ub.shape[1] // 256):
+        ub[:, j * 256:(j + 1) * 256] = lane_ref[j:j + 1, :]
+    qb[...] = lane_ref[4:5, :]
+    vb[...] = lane_ref[5:6, :]
+    for k in range(parts):
+        loads[k].wait()
+        high[k] = low[k].astype(F32)
+        saves[k].start()
+    for one, two in zip(there, back):
+        one.wait()
+        two.start()
+    for copy in saves + back:
+        copy.wait()
+
+
+def finish_call(layer, tg, small, lane, hid, rest):
+    hbm = pl.BlockSpec(memory_space=pl.ANY)
+    width = small.shape[1]
+    line = lambda n: struct((1, n), F32)
+    return pl.pallas_call(
+        finish_kernel,
+        out_shape=(struct(layer.shape, BF), struct(tg.shape, F32), line(width), line(width), line(256), line(256), line(width), line(width),
+                   line(width), line(hid), line(width)) + tuple(struct(r.shape, F32) for r in rest),
+        in_specs=[hbm, hbm, VM, VM] + [hbm] * 6,
+        out_specs=(hbm, hbm) + (VM,) * 9 + (hbm,) * 6,
+        scratch_shapes=[pltpu.VMEM(tg.shape, BF), pltpu.VMEM(tg.shape, F32), pltpu.VMEM(layer.shape, BF)] + [pltpu.VMEM(r.shape, F32) for r in rest]
+        + [DMA((7,)), DMA((7,)), DMA((tg.shape[0],)), DMA((tg.shape[0],))],
+        compiler_params=pltpu.CompilerParams(vmem_limit_bytes=60 << 20),
+        name="finish",
+    )(layer, tg, small, lane, *rest)
 
 
 def on_device(tokens, first_gain, first_shift, query_weight, query_bias, key_weight, value_weight, value_bias,
@@ -1130,27 +1187,23 @@
     c = lax.rem(d, 2)
     nblk = block_order.shape[0]
     rows = own // 8
-    meta = jnp.concatenate([block_order % nblk, prefix])
-    lanes = jnp.pad(block_order % nblk, (0, HEAD - nblk), constant_values=-1).reshape(1, HEAD)
+    meta = jnp.concatenate([block_order, prefix])
+    lanes = jnp.pad(block_order, (0, HEAD - nblk), constant_values=-1).reshape(1, HEAD)
     row = lambda v: v.reshape(1, -1)
 
-    w_all, n_all, q, kv, o, lse, mid, mixed, do, gm, sums, low, lane, out_part, dw_up, dw_down = front_call(
+    w_all, n_all, q, kv, o, lse, mid, mixed, do, gm, sums, low, lane, layer, dw_up, dw_down, up_grad = front_call(
         meta, lanes, tokens, row(first_gain), row(first_shift), query_weight, key_weight, value_weight, row(query_bias), row(value_bias),
-        out_weight, up_weight, down_weight, row(out_bias), row(second_gain), row(second_shift), cotangent, row(up_bias))
-    layer, up_grad, down_grad, out_grad, dwq, dwk, dwv, tg, small, lane = rear_call(
-        meta, lanes, q, kv, o, do, lse, out_part, low, mid, row(down_bias), dw_up, dw_down, mixed, n_all.reshape(2 * own, width), w_all, gm,
+        out_weight, up_weight, down_weight, row(out_bias), row(second_gain), row(second_shift), cotangent, row(up_bias), row(down_bias))
+    layer, down_grad, out_grad, dwq, dwk, dwv, tg, small, lane = rear_call(
+        meta, lanes, q, kv, o, do, lse, low, layer, dw_down, mixed, n_all.reshape(2 * own, width), w_all, gm,
         tokens, row(first_gain), sums, lane)
     hid = up_weight.shape[1]
+    layer, tg, gain1, shift1, qb, vb, ob, gain2, shift2, ub, db, up_grad, down_grad, out_grad, dwq, dwk, dwv = finish_call(
+        layer, tg, small, lane, hid, (up_grad, down_grad, out_grad, dwq, dwk, dwv))
+    flat = lambda v: v.reshape(-1)
     return (
-        layer.reshape(own, width),
-        tg.reshape(own, width).astype(F32),
-        small[4], small[5],
-        dwq, lane[4], dwk, dwv, lane[5],
-        out_grad, small[2],
-        small[0], small[1],
-        up_grad, lane[:hid // 256].reshape(hid),
-        down_grad, small[3],
-    )
+        layer.reshape(own, width), tg.reshape(own, width), flat(gain1), flat(shift1), dwq, flat(qb), dwk, dwv, flat(vb), out_grad, flat(ob),
+        flat(gain2), flat(shift2), up_grad, flat(ub), down_grad, flat(db))
 
 
 def solution(mesh):

time: 343 us -> 312 us (0.910)
  Pallas kernels: 325 us -> 305 us
  local copies, waits for them, and re-layouts: 10.4 us -> 1.17 us
  other arithmetic: 5.53 us -> 1.24 us
    pallas_call x2, Pallas kernels: 325 us -> 298 us  [remote_call(): pl.pallas_call(kernel, out_shape=outs, in_specs=ins, out_specs=jax.tree.m...]
    pallas_call x0 -> x1, Pallas kernels: none -> 6.87 us  [finish_call(): pl.pallas_call(finish_kernel, out_shape=(struct(layer.shape, BF), struct(...]
    unnamed x23 -> x0, local copies, waits for them, and re-layouts: 6.85 us -> none
    convert_element_type x1 -> x0, other arithmetic: 4.28 us -> none  [on_device(): tg.reshape(own, width).astype(F32)]
where the time goes in v6:
time: 312 us; the launch traced here: 309 us
  Pallas kernels  305 us (98%)
    pallas_call x2, Pallas kernels, remote_call(): pl.pallas_call(kernel, out_shape=outs, in_specs=ins, out_specs=jax.tree.m...  298 us
    pallas_call x1, Pallas kernels, finish_call(): pl.pallas_call(finish_kernel, out_shape=(struct(layer.shape, BF), struct(...  6.87 us

profile of v6, /device:TPU:1, one launch (start us, length us, event | category | flops | bytes accessed | tf_op | source)
XLA Modules:
  0.0 308.8 jit_solution(2230708494586339104)
XLA Ops:
  1.3 1.2 pad_add_fusion.meta
  2.5 1.2 pad_bitcast_fusion.lanes_ref
  3.7 178.8 %front.1 = (bf16[2048,384]{1,0:T(8,128)(2,1)}, bf16[2,512,2048]{2,1,0:T(8,128)(2,1)}, bf16[1024,128]{1,0:T(8,128)(2,1)}, bf16[8,1024,256]{2,1,0:T(8,128)(2,1)}, ...) custom-call(s32[33]{0:T(128)} %pad_add_fusion.meta, ...), custom_call_target="tpu_custom_call" | custom-call | tf_op jit(solution)/shard_map/front/pallas_call | solution.py:428
  182.5 119.2 %rear.1 = (bf16[8,64,2048]{2,1,0:T(8,128)(2,1)}, f32[1024,128]{1,0:T(8,128)}, f32[256,128]{1,0:T(8,128)}, f32[128,256]{1,0:T(8,128)}, f32[128,256]{1,0:T(8,128)}...) custom-call(s32[33]{0:T(128)} %pad_add_fusion.meta, ...), custom_call_target="tpu_custom_call" | custom-call | tf_op jit(solution)/shard_map/rear/pallas_call | solution.py:428
  301.8 6.9 %finish.1 = (bf16[8,64,2048]{2,1,0:T(8,128)(2,1)}, f32[8,64,2048]{2,1,0:T(8,128)}, f32[1,2048]{1,0:T(1,128)}, f32[1,2048]{1,0:T(1,128)}, f32[1,256]{1,0:T(1,128)...) custom-call(bf16[8,64,2048]{2,1,0:T(8,128)(2,1)} %get-tuple-element., ...), custom_call_target="tpu_custom_call" | custom-call | tf_op jit(solution)/shard_map/finish/pallas_call | solution.py:1169

commit v7 on v6

--- a/solution.py
+++ b/solution.py
@@ -461,15 +461,16 @@
     return inverse * (e - first - scaled * second)
 
 
-def augment(meta, lanes_ref, q_ref, qa_ref, kx_ref):
+def augment(meta, edge_ref, lanes_ref, q_ref, qa_ref, kx_ref):
     rows = q_ref.shape[0]
     nblk = kx_ref.shape[0] // BLK
-    prefix = meta[nblk]
+    prefix = edge_ref[0]
     for a in range(rows // BLK):
         at = slice(a * BLK, (a + 1) * BLK)
         hidden = jnp.where(lanes_ref[...] > meta[first_block() + a], NEG, 0.0)
         qa_ref[at, :HEAD] = q_ref[at, :]
-        qa_ref[at, HEAD:] = jnp.broadcast_to(hidden, (BLK, HEAD)).astype(BF)
+        qa_ref[at, HEAD:] = jnp.zeros((BLK, HEAD), BF)
+        qa_ref[at, HEAD:HEAD + nblk] = jnp.broadcast_to(hidden, (BLK, nblk)).astype(BF)
     lane = lax.broadcasted_iota(jnp.int32, (BLK, HEAD), 1)
     inside = lax.broadcasted_iota(jnp.int32, (BLK, HEAD), 0)
 
@@ -483,7 +484,7 @@
     return lax.axis_index("dp") // 2 * 4
 
 
-def front_kernel(meta, lanes_ref, x_ref, gain1_ref, shift1_ref, wq_ref, wk_ref, wv_ref, qb_ref, vb_ref, wo_ref, wu_ref, wd_ref,
+def front_kernel(meta, edge_ref, lanes_ref, x_ref, gain1_ref, shift1_ref, wq_ref, wk_ref, wv_ref, qb_ref, vb_ref, wo_ref, wu_ref, wd_ref,
                  bias_ref, gain2_ref, shift2_ref, cot_ref, ub_ref, db_ref,
                  w_hbm, n_hbm, q_out, kv_hbm, o_ref, lse_ref, mid_out, own_out, do_out, gm_out, sums_out, low_out, lane_out, lay_out, du_hbm, dd_hbm, dup_out,
                  w_vm, n_vm, kv_vm, out_vm, up_vm, down_vm, wsh, mixed, n2, gsum, colsum,
@@ -549,30 +550,43 @@
     qkv.forward(1)
     up_vm[mine, :] = wu_ref[...].astype(BF)
     down_vm[:, mine] = wd_ref[...].astype(BF)
-    outs.forward_pair()
-    outs.forward(0)
-    qkv.arrive(0)
     for copy in there:
         copy.wait_recv()
-    qkv.arrive(1)
     local = pl.ds(pl.multiple_of(c * HEAD, HEAD), HEAD)
     bias_q, bias_v = qb_ref[:, local], vb_ref[:, local]
 
-    @pl.loop(0, per)
-    def _(b):
-        at = pl.ds(pl.multiple_of(b * BLK, BLK), BLK)
-        piece = dg(n_vm[b // 2, pl.ds(pl.multiple_of(lax.rem(b, 2) * BLK, BLK), BLK), :], w_vm[...], NN)
-        q_out[at, :] = (piece[:, :HEAD] + bias_q).astype(BF)
-        kv_vm[me, at, :HEAD] = piece[:, HEAD:2 * HEAD].astype(BF)
-        kv_vm[me, at, HEAD:] = (piece[:, 2 * HEAD:] + bias_v).astype(BF)
-
+    def project(sums):
+        def term(i, s, first=False):
+            m = gd.index(gd.ring(i), gd.side(s))
+            cols = pl.ds(pl.multiple_of(m * 2 * shard, 2 * shard), 2 * shard)
+            for h in range(2):
+                piece = dg(n_vm[h, :, cols], w_vm[cols, :], NN)
+                at = slice(h * own, (h + 1) * own)
+                sums[at, :] = piece if first else sums[at, :] + piece
+
+        term(0, 0, True)
+        for i, s in ((1, 0), (3, 0), (0, 1)):
+            term(i, s)
+        outs.forward_pair()
+        outs.forward(0)
+        for i in (1, 3):
+            term(i, 1)
+        qkv.arrive(0)
+        term(2, 0)
+        qkv.arrive(1)
+        term(2, 1)
+        q_out[...] = (sums[:, :HEAD] + bias_q).astype(BF)
+        kv_vm[me, :, :HEAD] = sums[:, HEAD:2 * HEAD].astype(BF)
+        kv_vm[me, :, HEAD:] = (sums[:, 2 * HEAD:] + bias_v).astype(BF)
+
+    pl.run_scoped(project, pltpu.VMEM((rows, 3 * HEAD), F32))
     keys.start()
     outs.forward(1)
     saves = [pltpu.make_async_copy(w_vm, w_hbm, lsem.at[0]), pltpu.make_async_copy(n_vm, n_hbm, lsem.at[1])]
     for save in saves:
         save.start()
     def attention(qa_ref, kx_ref, m_ref, acc_ref):
-        augment(meta, lanes_ref, q_out, qa_ref, kx_ref)
+        augment(meta, edge_ref, lanes_ref, q_out, qa_ref, kx_ref)
         outs.arrive(0)
         outs.arrive(1)
         outs.settle()
@@ -580,7 +594,7 @@
         m_ref[...] = jnp.full_like(m_ref, -1e30)
         acc_ref[...] = jnp.zeros_like(acc_ref)
         ones = jnp.ones((BLK, HEAD), BF)
-        prefix = meta[nblk]
+        prefix = edge_ref[0]
 
         def attend(chunk, diagonal):
             ks, vs = [], []
@@ -669,6 +683,8 @@
     wide.arrive(0)
     wide.arrive(1)
     wide.settle()
+    ups.forward(1)
+    downs.forward_pair()
     for copy in copies:
         copy.wait_recv()
     span = 512
@@ -683,16 +699,14 @@
     scaled, _ = norm_rows(mid_out[...])
     n2[pl.ds(pl.multiple_of(t * small, small), small), :] = (scaled * gain2_ref[...] + shift2_ref[...]).astype(BF)
     normed.start()
-    ups.forward(1)
-    normed.forward_pair()
-    normed.forward(0)
-    downs.forward_pair()
     downs.forward(0)
     ups.arrive(0)
     ups.arrive(1)
+    normed.forward_pair()
+    normed.forward(0)
+    downs.forward(1)
+    normed.forward(1)
     ups.settle()
-    normed.forward(1)
-    downs.forward(1)
     downs.arrive(0)
     downs.arrive(1)
     downs.settle()
@@ -826,7 +840,7 @@
         copy.wait()
 
 
-def front_call(meta, lanes, x, gain1, shift1, wq, wk, wv, qb, vb, wo, wu, wd, bias, gain2, shift2, cot, ub, db):
+def front_call(meta, edge, lanes, x, gain1, shift1, wq, wk, wv, qb, vb, wo, wu, wd, bias, gain2, shift2, cot, ub, db):
     own, width = x.shape
     rows, shard, hid, small = 2 * own, wq.shape[0], wu.shape[1], own // 8
     hbm = pl.BlockSpec(memory_space=pl.ANY)
@@ -836,17 +850,17 @@
             struct((small, width), F32), struct((own, 2 * HEAD), BF), struct((rows, HEAD), BF), struct((small, width), F32),
             struct((8, width), F32), struct((small, width), BF), struct((8, 256), F32), struct((small, width), BF), up, down, struct((shard, hid), F32))
     return remote_call(
-        front_kernel, "front", 1, outs, [SM] + [VM] * 18,
+        front_kernel, "front", 1, outs, [SM, SM] + [VM] * 18,
         [pltpu.VMEM(s, BF) for s in big]
         + [pltpu.VMEM((2, shard, 3 * HEAD), BF), pltpu.VMEM((small, width), BF), pltpu.VMEM((own, width), BF),
            pltpu.VMEM((small, width), F32), pltpu.VMEM((8, hid), F32),
            DMA((7,)), DMA((3,)), DMA((3,)), DMA((16,)), DMA((16,)), DMA((15,)), DMA((15,))]
         + Gather.scratch() * 2 + Gather.scratch(True) * 4 + Gather.scratch() + Scatter.scratch(small, width) * 2 + CoreScatter.scratch(shard, hid),
-        meta, lanes, x, gain1, shift1, wq, wk, wv, qb, vb, wo, wu, wd, bias, gain2, shift2, cot, ub, db,
+        meta, edge, lanes, x, gain1, shift1, wq, wk, wv, qb, vb, wo, wu, wd, bias, gain2, shift2, cot, ub, db,
         out_specs=(hbm, hbm, VM, hbm) + (VM,) * 10 + (hbm, hbm, VM))
 
 
-def rear_kernel(meta, lanes_ref, q_ref, kv_hbm, o_ref, do_ref, lse_ref, gbr_ref, layr_ref, ddown_hbm,
+def rear_kernel(meta, edge_ref, lanes_ref, q_ref, kv_hbm, o_ref, do_ref, lse_ref, gbr_ref, layr_ref, ddown_hbm,
                 mixed_ref, n_hbm, w_ref, gm_ref, x_hbm, gain_ref, early_ref, lane_ref,
                 lay_out, ddown_out, dwo_out, dwq_out, dwk_out, dwv_out, tg_out, sums_out, lanes_out,
                 kv_ref, qa_ref, kx_ref, part, delta_ref, dq_acc, gb, dqkv, dwo, n_buf, dw, away, arrived, summed, total, mine_w, there_w, vec, x_ref,
@@ -904,41 +918,39 @@
     gb[pl.ds(pl.multiple_of(mine_t * small, small), small), :] = gbr_ref[...]
     wide.start()
     layer.start()
-    augment(meta, lanes_ref, q_ref, qa_ref, kx_ref)
+    augment(meta, edge_ref, lanes_ref, q_ref, qa_ref, kx_ref)
     for a in range(per):
         at = slice(a * BLK, (a + 1) * BLK)
         prod = do_ref[at, :].astype(F32) * o_ref[at, :].astype(F32)
         delta_ref[0:1, at] = jnp.sum(jnp.transpose(prod), axis=0, keepdims=True)
         delta_ref[1:2, at] = lse_ref[a:a + 1, :]
     dq_acc[...] = jnp.zeros_like(dq_acc)
-    prefix = meta[nblk]
+    prefix = edge_ref[0]
 
     def attend(chunk, diagonal):
-        for i in range(per):
-            at_k = slice(i * BLK, (i + 1) * BLK)
-            at_x = pl.ds(pl.multiple_of(chunk * rows + i * BLK, BLK), BLK)
-            k = kv_ref[chunk, at_k, :HEAD]
-            v = kv_ref[chunk, at_k, HEAD:]
-            kk = jnp.concatenate([k, kx_ref[at_x, :]], axis=1)
-            turned = jnp.transpose(k.astype(F32)).astype(BF)
-            dk = dv = None
-            for a in range(per):
-                at_q = slice(a * BLK, (a + 1) * BLK)
-                q = q_ref[at_q, :]
-                do = do_ref[at_q, :]
-                p = jnp.exp2(dg(kk, qa_ref[at_q, :], NT) * C1 - delta_ref[1:2, at_q])
-                if diagonal and i == a:
-                    edge = prefix - 1 - meta[first_block() + a] * BLK
-                    lim = jnp.maximum(lax.broadcasted_iota(jnp.int32, (BLK, BLK), 1), edge)
-                    p = jnp.where(lax.broadcasted_iota(jnp.int32, (BLK, BLK), 0) <= lim, p, 0.0)
-                ds = (p * (dg(v, do, NT) - delta_ref[0:1, at_q])).astype(BF)
-                tv = jnp.dot(p.astype(BF), do, preferred_element_type=F32)
-                tk = jnp.dot(ds, q, preferred_element_type=F32)
-                dv = tv if dv is None else dv + tv
-                dk = tk if dk is None else dk + tk
-                dq_acc[:, at_q] += jnp.dot(turned, ds, preferred_element_type=F32)
-            part[chunk, at_k, :HEAD] = (dk * SCALE).astype(BF)
-            part[chunk, at_k, HEAD:] = dv.astype(BF)
+        k = kv_ref[chunk, :, :HEAD]
+        v = kv_ref[chunk, :, HEAD:]
+        kk = jnp.concatenate([k, kx_ref[pl.ds(pl.multiple_of(chunk * rows, rows), rows), :]], axis=1)
+        turned = jnp.transpose(k.astype(F32)).astype(BF)
+        dk = dv = None
+        for a in range(per):
+            at_q = slice(a * BLK, (a + 1) * BLK)
+            q = q_ref[at_q, :]
+            do = do_ref[at_q, :]
+            p = jnp.exp2(dg(kk, qa_ref[at_q, :], NT) * C1 - delta_ref[1:2, at_q])
+            if diagonal:
+                edge = prefix - 1 - meta[first_block() + a] * BLK
+                lim = jnp.maximum(lax.broadcasted_iota(jnp.int32, (BLK, BLK), 1), edge)
+                mid = jnp.where(lax.broadcasted_iota(jnp.int32, (BLK, BLK), 0) <= lim, p[a * BLK:(a + 1) * BLK], 0.0)
+                p = jnp.concatenate([p[b * BLK:(b + 1) * BLK] if b != a else mid for b in range(per)], axis=0)
+            ds = (p * (dg(v, do, NT) - delta_ref[0:1, at_q])).astype(BF)
+            tv = jnp.dot(p.astype(BF), do, preferred_element_type=F32)
+            tk = jnp.dot(ds, q, preferred_element_type=F32)
+            dv = tv if dv is None else dv + tv
+            dk = tk if dk is None else dk + tk
+            dq_acc[:, at_q] += jnp.dot(turned, ds, preferred_element_type=F32)
+        part[chunk, :, :HEAD] = (dk * SCALE).astype(BF)
+        part[chunk, :, HEAD:] = dv.astype(BF)
 
     for n in range(8):
         kv_load(n).wait()
@@ -1109,7 +1121,7 @@
     swap.wait_send()
 
 
-def rear_call(meta, lanes, q, kv, o, do, lse, gb, lay, ddown, mixed, n, w, gm, x, gain, early, lane):
+def rear_call(meta, edge, lanes, q, kv, o, do, lse, gb, lay, ddown, mixed, n, w, gm, x, gain, early, lane):
     rows = q.shape[0]
     small, width = gm.shape
     hbm = pl.BlockSpec(memory_space=pl.ANY)
@@ -1121,7 +1133,7 @@
         rear_kernel, "rear", 5,
         (struct(chunks, BF), struct((ddown.shape[0], share), F32), struct((2 * HEAD, share), F32), head_grad, head_grad, head_grad,
          struct(chunks, BF), struct((8, width), F32), struct(lane.shape, F32)),
-        [SM, VM, VM, hbm] + [VM] * 5 + [hbm, VM] + [hbm, VM, VM, hbm] + [VM] * 3,
+        [SM, SM, VM, VM, hbm] + [VM] * 5 + [hbm, VM] + [hbm, VM, VM, hbm] + [VM] * 3,
         [pltpu.VMEM(kv.shape, BF), pltpu.VMEM((rows, 2 * HEAD), BF), pltpu.VMEM((8 * rows, HEAD), BF), pltpu.VMEM(kv.shape, BF), pltpu.VMEM((8, rows), F32),
          pltpu.VMEM((HEAD, rows), F32), pltpu.VMEM((8 * small, width), BF), pltpu.VMEM((rows, wc), BF), pltpu.VMEM((2 * HEAD, width), BF),
          pltpu.VMEM((2, rows, BLK), BF), pltpu.VMEM((8, width // 8, wc), BF), pltpu.VMEM(chunks, BF), pltpu.VMEM(chunks, BF),
@@ -1130,7 +1142,7 @@
         + Scatter.scratch(rows, 2 * HEAD) + CoreScatter.scratch(ddown.shape[0], share)
         + CoreScatter.scratch(2 * HEAD, share) + Scatter.scratch(small, width) + Scatter.scratch(width // 8, wc)
         + Gather.scratch() * 3 + RowSums.scratch(width) + Sums.scratch(*lane.shape),
-        meta, lanes, q, kv, o, do, lse, gb, lay, ddown, mixed, n, w, gm, x, gain, early, lane)
+        meta, edge, lanes, q, kv, o, do, lse, gb, lay, ddown, mixed, n, w, gm, x, gain, early, lane)
 
 
 def finish_kernel(layer, tg, small_ref, lane_ref, up, down, out, wq, wk, wv,
@@ -1187,15 +1199,14 @@
     c = lax.rem(d, 2)
     nblk = block_order.shape[0]
     rows = own // 8
-    meta = jnp.concatenate([block_order, prefix])
-    lanes = jnp.pad(block_order, (0, HEAD - nblk), constant_values=-1).reshape(1, HEAD)
+    meta, edge, lanes = block_order, prefix, block_order.reshape(1, nblk)
     row = lambda v: v.reshape(1, -1)
 
     w_all, n_all, q, kv, o, lse, mid, mixed, do, gm, sums, low, lane, layer, dw_up, dw_down, up_grad = front_call(
-        meta, lanes, tokens, row(first_gain), row(first_shift), query_weight, key_weight, value_weight, row(query_bias), row(value_bias),
+        meta, edge, lanes, tokens, row(first_gain), row(first_shift), query_weight, key_weight, value_weight, row(query_bias), row(value_bias),
         out_weight, up_weight, down_weight, row(out_bias), row(second_gain), row(second_shift), cotangent, row(up_bias), row(down_bias))
     layer, down_grad, out_grad, dwq, dwk, dwv, tg, small, lane = rear_call(
-        meta, lanes, q, kv, o, do, lse, low, layer, dw_down, mixed, n_all.reshape(2 * own, width), w_all, gm,
+        meta, edge, lanes, q, kv, o, do, lse, low, layer, dw_down, mixed, n_all.reshape(2 * own, width), w_all, gm,
         tokens, row(first_gain), sums, lane)
     hid = up_weight.shape[1]
     layer, tg, gain1, shift1, qb, vb, ob, gain2, shift2, ub, db, up_grad, down_grad, out_grad, dwq, dwk, dwv = finish_call(

time: 312 us -> 305 us (0.978)
  Pallas kernels: 305 us -> 301 us
    pallas_call x2, Pallas kernels: 298 us -> 294 us  [remote_call(): pl.pallas_call(kernel, out_shape=outs, in_specs=ins, out_specs=jax.tree.m...]
where the time goes in v7:
time: 305 us; the launch traced here: 302 us
  Pallas kernels  301 us (99%)
    pallas_call x2, Pallas kernels, remote_call(): pl.pallas_call(kernel, out_shape=outs, in_specs=ins, out_specs=jax.tree.m...  294 us
    pallas_call x1, Pallas kernels, finish_call(): pl.pallas_call(finish_kernel, out_shape=(struct(layer.shape, BF), struct(...  6.87 us

profile of v7, /device:TPU:1, one launch (start us, length us, event | category | flops | bytes accessed | tf_op | source)
XLA Modules:
  0.0 302.1 jit_solution(392928790684613002)
XLA Ops:
  1.3 174.6 %front.1 = (bf16[2048,384]{1,0:T(8,128)(2,1)}, bf16[2,512,2048]{2,1,0:T(8,128)(2,1)}, bf16[1024,128]{1,0:T(8,128)(2,1)}, bf16[8,1024,256]{2,1,0:T(8,128)(2,1)}, ...) custom-call(s32[32]{0:T(128)} %meta.3, ...), custom_call_target="tpu_custom_call" | custom-call | tf_op jit(solution)/shard_map/front/pallas_call | solution.py:428
  175.9 119.1 %rear.1 = (bf16[8,64,2048]{2,1,0:T(8,128)(2,1)}, f32[1024,128]{1,0:T(8,128)}, f32[256,128]{1,0:T(8,128)}, f32[128,256]{1,0:T(8,128)}, f32[128,256]{1,0:T(8,128)}...) custom-call(s32[32]{0:T(128)} %meta.3, s32[1]{0:T(128)S(6)} %copy.36.edge_ref, ...), custom_call_target="tpu_custom_call" | custom-call | tf_op jit(solution)/shard_map/rear/pallas_call | solution.py:428
  295.1 6.9 %finish.1 = (bf16[8,64,2048]{2,1,0:T(8,128)(2,1)}, f32[8,64,2048]{2,1,0:T(8,128)}, f32[1,2048]{1,0:T(1,128)}, f32[1,2048]{1,0:T(1,128)}, f32[1,256]{1,0:T(1,128)...) custom-call(bf16[8,64,2048]{2,1,0:T(8,128)(2,1)} %get-tuple-element., ...), custom_call_target="tpu_custom_call" | custom-call | tf_op jit(solution)/shard_map/finish/pallas_call | solution.py:1181

commit v8 on v7

--- a/solution.py
+++ b/solution.py
@@ -484,10 +484,11 @@
     return lax.axis_index("dp") // 2 * 4
 
 
-def front_kernel(meta, edge_ref, lanes_ref, x_ref, gain1_ref, shift1_ref, wq_ref, wk_ref, wv_ref, qb_ref, vb_ref, wo_ref, wu_ref, wd_ref,
-                 bias_ref, gain2_ref, shift2_ref, cot_ref, ub_ref, db_ref,
-                 w_hbm, n_hbm, q_out, kv_hbm, o_ref, lse_ref, mid_out, own_out, do_out, gm_out, sums_out, low_out, lane_out, lay_out, du_hbm, dd_hbm, dup_out,
+def front_kernel(meta, edge_ref, lanes_ref, x_hbm, gain1_ref, shift1_ref, wq_ref, wk_ref, wv_ref, qb_ref, vb_ref, wo_hbm, wu_hbm, wd_hbm,
+                 bias_ref, gain2_ref, shift2_ref, cot_hbm, ub_ref, db_ref,
+                 w_hbm, n_hbm, q_out, kv_hbm, o_ref, lse_ref, own_out, do_out, gm_out, sums_out, low_out, lane_out, lay_out, du_hbm, dd_hbm, dup_out,
                  w_vm, n_vm, kv_vm, out_vm, up_vm, down_vm, wsh, mixed, n2, gsum, colsum,
+                 mid_out, x_ref, wo_ref, wu_ref, wd_ref, cot_ref,
                  lsem, css, crs, ass, ars, hss, hrs, *sems):
     gd, gt = Eight("dp"), Eight("tensor")
     t = gt.t
@@ -504,6 +505,11 @@
     hid = wd_ref.shape[0]
     small = mid_out.shape[0]
     csem, asem = (css, crs), (ass, ars)
+    x_load, wo_load, wu_load, wd_load, cot_load = (
+        pltpu.make_async_copy(one, two, lsem.at[7 + k]) for k, (one, two) in enumerate(
+            ((x_hbm, x_ref), (wo_hbm, wo_ref), (wu_hbm, wu_ref), (wd_hbm, wd_ref), (cot_hbm, cot_ref))))
+    for load in (x_load, wo_load, wu_load, wd_load, cot_load):
+        load.start()
     for h in range(2):
         cols = slice(h * HEAD, (h + 1) * HEAD)
         for i, ref in enumerate((wq_ref, wk_ref, wv_ref)):
@@ -541,13 +547,17 @@
         at = pl.ds(k * (own // 2), own // 2)
         return send(n_vm.at[c, at], n_vm.at[c, at], csem, 1 + k, core)
 
+    x_load.wait()
     there = [norm_part(0)]
     qkv.forward_pair()
     qkv.forward(0)
+    wo_load.wait()
     out_vm[t, :, mine] = wo_ref[...].astype(BF)
     outs.start()
     there.append(norm_part(1))
     qkv.forward(1)
+    wu_load.wait()
+    wd_load.wait()
     up_vm[mine, :] = wu_ref[...].astype(BF)
     down_vm[:, mine] = wd_ref[...].astype(BF)
     for copy in there:
@@ -710,6 +720,7 @@
     downs.arrive(0)
     downs.arrive(1)
     downs.settle()
+    cot_load.wait()
     saves.pop(1).wait()
     for copy in there:
         copy.wait_send()
@@ -847,23 +858,25 @@
     big = [(width, 3 * HEAD), (2, own, width), (8, rows, 2 * HEAD), (8, 2 * HEAD, width), (width, hid), (hid, width)]
     w, n, kv, out, up, down = (struct(s, BF) for s in big)
     outs = (w, n, struct((rows, HEAD), BF), kv, struct((rows, HEAD), BF), struct((rows // BLK, BLK), F32),
-            struct((small, width), F32), struct((own, 2 * HEAD), BF), struct((rows, HEAD), BF), struct((small, width), F32),
+            struct((own, 2 * HEAD), BF), struct((rows, HEAD), BF), struct((small, width), F32),
             struct((8, width), F32), struct((small, width), BF), struct((8, 256), F32), struct((small, width), BF), up, down, struct((shard, hid), F32))
     return remote_call(
-        front_kernel, "front", 1, outs, [SM, SM] + [VM] * 18,
+        front_kernel, "front", 1, outs, [SM, SM, VM, hbm] + [VM] * 7 + [hbm] * 3 + [VM] * 3 + [hbm, VM, VM],
         [pltpu.VMEM(s, BF) for s in big]
         + [pltpu.VMEM((2, shard, 3 * HEAD), BF), pltpu.VMEM((small, width), BF), pltpu.VMEM((own, width), BF),
            pltpu.VMEM((small, width), F32), pltpu.VMEM((8, hid), F32),
-           DMA((7,)), DMA((3,)), DMA((3,)), DMA((16,)), DMA((16,)), DMA((15,)), DMA((15,))]
+           pltpu.VMEM((small, width), F32), pltpu.VMEM(x.shape, BF), pltpu.VMEM(wo.shape, F32), pltpu.VMEM(wu.shape, F32), pltpu.VMEM(wd.shape, F32),
+           pltpu.VMEM(cot.shape, BF),
+           DMA((12,)), DMA((3,)), DMA((3,)), DMA((16,)), DMA((16,)), DMA((15,)), DMA((15,))]
         + Gather.scratch() * 2 + Gather.scratch(True) * 4 + Gather.scratch() + Scatter.scratch(small, width) * 2 + CoreScatter.scratch(shard, hid),
         meta, edge, lanes, x, gain1, shift1, wq, wk, wv, qb, vb, wo, wu, wd, bias, gain2, shift2, cot, ub, db,
-        out_specs=(hbm, hbm, VM, hbm) + (VM,) * 10 + (hbm, hbm, VM))
+        out_specs=(hbm, hbm, VM, hbm) + (VM,) * 9 + (hbm, hbm, VM))
 
 
 def rear_kernel(meta, edge_ref, lanes_ref, q_ref, kv_hbm, o_ref, do_ref, lse_ref, gbr_ref, layr_ref, ddown_hbm,
-                mixed_ref, n_hbm, w_ref, gm_ref, x_hbm, gain_ref, early_ref, lane_ref,
+                mixed_hbm, n_hbm, w_hbm, gm_hbm, x_hbm, gain_ref, early_ref, lane_ref,
                 lay_out, ddown_out, dwo_out, dwq_out, dwk_out, dwv_out, tg_out, sums_out, lanes_out,
-                kv_ref, qa_ref, kx_ref, part, delta_ref, dq_acc, gb, dqkv, dwo, n_buf, dw, away, arrived, summed, total, mine_w, there_w, vec, x_ref,
+                kv_ref, qa_ref, kx_ref, part, delta_ref, dq_acc, gb, dqkv, dwo, n_buf, dw, away, arrived, summed, total, mine_w, there_w, vec, x_ref, mixed_ref, w_ref, gm_ref,
                 lsem, css, crs, *scratch):
     g, gt = Eight("dp"), Eight("tensor")
     c = lax.rem(g.d, 2)
@@ -883,6 +896,11 @@
 
     for n in range(8):
         kv_load(n).start()
+    mixed_load, w_load, gm_load = (
+        pltpu.make_async_copy(one, two, lsem.at[11 + k]) for k, (one, two) in enumerate(
+            ((mixed_hbm, mixed_ref), (w_hbm, w_ref), (gm_hbm, gm_ref))))
+    for load in (mixed_load, w_load, gm_load):
+        load.start()
     everyone = [(lax.rem(g.d + k, 16), g.t) for k in range(1, 16)] + [(g.d, lax.rem(g.t + k, 8)) for k in range(1, 8)]
     greet(everyone)
     take = list(scratch)
@@ -1003,6 +1021,7 @@
     wide.arrive(1)
     wide.settle()
     span = 512
+    mixed_load.wait()
     for n in range(width // span):
         cols = pl.ds(n * span, span)
         dwo[:, cols] = dg(mixed_ref[...], gb[:, cols], TN).astype(BF)
@@ -1023,6 +1042,7 @@
                 for j in range(BLK // small):
                     into[b * (BLK // small) + j, :, cols] = piece[j * small:(j + 1) * small]
 
+    w_load.wait()
     project(away, 1 - c)
     swap = send(away, arrived, csem, 0, core)
     project(summed, c)
@@ -1065,6 +1085,7 @@
         total[at, :] = value
 
     x_load.wait()
+    gm_load.wait()
     tokens.finish(keep)
     scaled, inverse = norm_rows(x_ref[...].astype(F32))
     grad = total[...]
@@ -1133,12 +1154,13 @@
         rear_kernel, "rear", 5,
         (struct(chunks, BF), struct((ddown.shape[0], share), F32), struct((2 * HEAD, share), F32), head_grad, head_grad, head_grad,
          struct(chunks, BF), struct((8, width), F32), struct(lane.shape, F32)),
-        [SM, SM, VM, VM, hbm] + [VM] * 5 + [hbm, VM] + [hbm, VM, VM, hbm] + [VM] * 3,
+        [SM, SM, VM, VM, hbm] + [VM] * 5 + [hbm] * 6 + [VM] * 3,
         [pltpu.VMEM(kv.shape, BF), pltpu.VMEM((rows, 2 * HEAD), BF), pltpu.VMEM((8 * rows, HEAD), BF), pltpu.VMEM(kv.shape, BF), pltpu.VMEM((8, rows), F32),
          pltpu.VMEM((HEAD, rows), F32), pltpu.VMEM((8 * small, width), BF), pltpu.VMEM((rows, wc), BF), pltpu.VMEM((2 * HEAD, width), BF),
          pltpu.VMEM((2, rows, BLK), BF), pltpu.VMEM((8, width // 8, wc), BF), pltpu.VMEM(chunks, BF), pltpu.VMEM(chunks, BF),
          pltpu.VMEM(chunks, BF), pltpu.VMEM((small, width), F32), pltpu.VMEM((width // 8, wc), BF), pltpu.VMEM((share, wc), BF),
-         pltpu.VMEM((8, width), F32), pltpu.VMEM((small, width), BF), DMA((11,)), DMA((2,)), DMA((2,))]
+         pltpu.VMEM((8, width), F32), pltpu.VMEM((small, width), BF), pltpu.VMEM(mixed.shape, BF),
+         pltpu.VMEM(w.shape, BF), pltpu.VMEM(gm.shape, F32), DMA((14,)), DMA((2,)), DMA((2,))]
         + Scatter.scratch(rows, 2 * HEAD) + CoreScatter.scratch(ddown.shape[0], share)
         + CoreScatter.scratch(2 * HEAD, share) + Scatter.scratch(small, width) + Scatter.scratch(width // 8, wc)
         + Gather.scratch() * 3 + RowSums.scratch(width) + Sums.scratch(*lane.shape),
@@ -1155,7 +1177,7 @@
     saves = [pltpu.make_async_copy(high.at[k], tg_out.at[k], tout.at[k]) for k in range(parts)]
     there = [pltpu.make_async_copy(way[0], buffer, insem.at[k]) for k, (way, buffer) in enumerate(zip(ways, buffers))]
     back = [pltpu.make_async_copy(buffer, way[1], outsem.at[k]) for k, (way, buffer) in enumerate(zip(ways, buffers))]
-    for copy in loads + there:
+    for copy in there + loads:
         copy.start()
     for k, ref in ((4, gain1), (5, shift1), (2, ob), (0, gain2), (1, shift2), (3, db)):
         ref[...] = small_ref[k:k + 1, :]
@@ -1163,13 +1185,13 @@
         ub[:, j * 256:(j + 1) * 256] = lane_ref[j:j + 1, :]
     qb[...] = lane_ref[4:5, :]
     vb[...] = lane_ref[5:6, :]
+    for one, two in zip(there, back):
+        one.wait()
+        two.start()
     for k in range(parts):
         loads[k].wait()
         high[k] = low[k].astype(F32)
         saves[k].start()
-    for one, two in zip(there, back):
-        one.wait()
-        two.start()
     for copy in saves + back:
         copy.wait()
 
@@ -1202,7 +1224,7 @@
     meta, edge, lanes = block_order, prefix, block_order.reshape(1, nblk)
     row = lambda v: v.reshape(1, -1)
 
-    w_all, n_all, q, kv, o, lse, mid, mixed, do, gm, sums, low, lane, layer, dw_up, dw_down, up_grad = front_call(
+    w_all, n_all, q, kv, o, lse, mixed, do, gm, sums, low, lane, layer, dw_up, dw_down, up_grad = front_call(
         meta, edge, lanes, tokens, row(first_gain), row(first_shift), query_weight, key_weight, value_weight, row(query_bias), row(value_bias),
         out_weight, up_weight, down_weight, row(out_bias), row(second_gain), row(second_shift), cotangent, row(up_bias), row(down_bias))
     layer, down_grad, out_grad, dwq, dwk, dwv, tg, small, lane = rear_call(

time: 305 us -> 303 us (level)
  no operation moved by 1% of the time
where the time goes in v8:
time: 303 us; the launch traced here: 300 us
  Pallas kernels  298 us (98%)
    pallas_call x2, Pallas kernels, remote_call(): pl.pallas_call(kernel, out_shape=outs, in_specs=ins, out_specs=jax.tree.m...  292 us
    pallas_call x1, Pallas kernels, finish_call(): pl.pallas_call(finish_kernel, out_shape=(struct(layer.shape, BF), struct(...  6.57 us

profile of v8, /device:TPU:1, one launch (start us, length us, event | category | flops | bytes accessed | tf_op | source)
XLA Modules:
  0.0 299.7 jit_solution(4316178949291619439)
XLA Ops:
  1.3 173.2 %front.1 = (bf16[2048,384]{1,0:T(8,128)(2,1)}, bf16[2,512,2048]{2,1,0:T(8,128)(2,1)}, bf16[1024,128]{1,0:T(8,128)(2,1)}, bf16[8,1024,256]{2,1,0:T(8,128)(2,1)}, ...) custom-call(s32[32]{0:T(128)} %meta.3, ...), custom_call_target="tpu_custom_call" | custom-call | tf_op jit(solution)/shard_map/front/pallas_call | solution.py:428
  174.5 118.4 %rear.1 = (bf16[8,64,2048]{2,1,0:T(8,128)(2,1)}, f32[1024,128]{1,0:T(8,128)}, f32[256,128]{1,0:T(8,128)}, f32[128,256]{1,0:T(8,128)}, f32[128,256]{1,0:T(8,128)}...) custom-call(s32[32]{0:T(128)} %meta.3, s32[1]{0:T(128)S(6)} %copy.36.edge_ref, ...), custom_call_target="tpu_custom_call" | custom-call | tf_op jit(solution)/shard_map/rear/pallas_call | solution.py:428
  293.0 6.6 %finish.1 = (bf16[8,64,2048]{2,1,0:T(8,128)(2,1)}, f32[8,64,2048]{2,1,0:T(8,128)}, f32[1,2048]{1,0:T(1,128)}, f32[1,2048]{1,0:T(1,128)}, f32[1,256]{1,0:T(1,128)...) custom-call(bf16[8,64,2048]{2,1,0:T(8,128)(2,1)} %get-tuple-element., ...), custom_call_target="tpu_custom_call" | custom-call | tf_op jit(solution)/shard_map/finish/pallas_call | solution.py:1203

commit v9 on v8

--- a/solution.py
+++ b/solution.py
@@ -1026,6 +1026,7 @@
         cols = pl.ds(n * span, span)
         dwo[:, cols] = dg(mixed_ref[...], gb[:, cols], TN).astype(BF)
     dwos.start()
+    downs.add()
 
     def keep_keys(at, value):
         dqkv[at, HEAD:] = value.astype(BF)
@@ -1046,7 +1047,6 @@
     project(away, 1 - c)
     swap = send(away, arrived, csem, 0, core)
     project(summed, c)
-    downs.add()
     swap.wait_recv()
 
     @pl.loop(0, 8)

time: 303 us -> 300 us (0.990)
  no operation moved by 1% of the time
where the time goes in v9:
time: 300 us; the launch traced here: 299 us
  Pallas kernels  298 us (99%)
    pallas_call x2, Pallas kernels, remote_call(): pl.pallas_call(kernel, out_shape=outs, in_specs=ins, out_specs=jax.tree.m...  291 us
    pallas_call x1, Pallas kernels, finish_call(): pl.pallas_call(finish_kernel, out_shape=(struct(layer.shape, BF), struct(...  6.57 us

profile of v9, /device:TPU:1, one launch (start us, length us, event | category | flops | bytes accessed | tf_op | source)
XLA Modules:
  0.0 299.2 jit_solution(11998663772518939979)
XLA Ops:
  1.3 173.2 %front.1 = (bf16[2048,384]{1,0:T(8,128)(2,1)}, bf16[2,512,2048]{2,1,0:T(8,128)(2,1)}, bf16[1024,128]{1,0:T(8,128)(2,1)}, bf16[8,1024,256]{2,1,0:T(8,128)(2,1)}, ...) custom-call(s32[32]{0:T(128)} %meta.3, ...), custom_call_target="tpu_custom_call" | custom-call | tf_op jit(solution)/shard_map/front/pallas_call | solution.py:428
  174.5 117.9 %rear.1 = (bf16[8,64,2048]{2,1,0:T(8,128)(2,1)}, f32[1024,128]{1,0:T(8,128)}, f32[256,128]{1,0:T(8,128)}, f32[128,256]{1,0:T(8,128)}, f32[128,256]{1,0:T(8,128)}...) custom-call(s32[32]{0:T(128)} %meta.3, s32[1]{0:T(128)S(6)} %copy.36.edge_ref, ...), custom_call_target="tpu_custom_call" | custom-call | tf_op jit(solution)/shard_map/rear/pallas_call | solution.py:428
  292.4 6.6 %finish.1 = (bf16[8,64,2048]{2,1,0:T(8,128)(2,1)}, f32[8,64,2048]{2,1,0:T(8,128)}, f32[1,2048]{1,0:T(1,128)}, f32[1,2048]{1,0:T(1,128)}, f32[1,256]{1,0:T(1,128)...) custom-call(bf16[8,64,2048]{2,1,0:T(8,128)(2,1)} %get-tuple-element., ...), custom_call_target="tpu_custom_call" | custom-call | tf_op jit(solution)/shard_map/finish/pallas_call | solution.py:1203
